TPU v7x, 32 devices: a whole 2x2x4 slice. The times are simulated.
32 devices in a mesh: tile: 8 (over z, y), acq: 4 (over x, core).
Axes of the slice: x: 2, y: 2, z: 4, core: 2. Of those that a mesh axis runs over, the one named last changes fastest.
Arguments:
- phases: float32 [64, 131072], P('acq', 'tile'), may hold values from -6 to 6
- coherence: float32 [131072], P('tile'), may hold values from 0.1 to 1
- pixel_index: int32 [131072], P('tile'), may hold values from 0 to 8191
- send_list: int32 [64, 128], P('tile'), may hold values from 0 to 16383, as said below
- counts: int32 [8, 8], P('tile'), may hold values from 16 to 128, as said below
- band_width: int32 [64], replicated, may hold values from 1 to 8
Outputs:
- residual: float32 [64, 8192], P('acq', 'tile')
- screen: float32 [64, 64, 1024], P('acq', 'tile')
Inputs may be any that keep to these rules, and one draw needn't show every extreme that they name: `counts`: for every device two owner tiles (the same for all devices, possibly one) receive all 128 slots; the others receive between 16 and 63. `send_list`: the live entries of one device's rows are distinct local scatterer indices; entries beyond a row's count are valid indices that carry no data.
All inputs are finite; a program needn't handle non-finite values.
Results may differ from a plain program's by a relative error of at most 0.0003.
Values sent between devices are 32-bit elements; how exact they have to be, the bound alone decides.
No kernel may reach another device: no remote copies, remote signals or barrier semaphores. Data moves between devices by JAX's collectives and lax.ppermute only.
A program may use at most 64 MiB of HBM per device.

v0:
```python
import jax
import jax.numpy as jnp
from jax import lax
from jax.sharding import PartitionSpec as P

ACQ = 64
ROWS_DEV = 8
COLS = 1024
RADIUS = 4
SLAB_PIX = 8192


min_weight = 0.1


def with_halo(cells, sides, width):
    for axis, dim in sides:
        count = lax.axis_size(axis)
        ends = count - 1
        head = lax.slice_in_dim(cells, 0, width, axis=dim)
        tail = lax.slice_in_dim(cells, cells.shape[dim] - width, cells.shape[dim], axis=dim)
        cells = jnp.concatenate(
            [
                lax.ppermute(tail, axis, [(i, (i + 1) % count) for i in range(ends)]),
                cells,
                lax.ppermute(head, axis, [((i + 1) % count, i) for i in range(ends)]),
            ],
            axis=dim,
        )
    return cells


def temporal_matrix(band_width):
    positions = jnp.arange(ACQ, dtype=jnp.int32)
    lower = jnp.maximum(positions - band_width, 0)
    upper = jnp.minimum(positions + band_width, ACQ - 1)
    inside = (positions[None, :] >= lower[:, None]) & (positions[None, :] <= upper[:, None])
    window = (upper - lower + 1).astype(jnp.float32)
    return jnp.eye(ACQ, dtype=jnp.float32) - inside.astype(jnp.float32) / window[:, None]


def kernel_weights():
    return [
        (RADIUS + 1 - abs(offset - RADIUS)) / float((RADIUS + 1) ** 2)
        for offset in range(2 * RADIUS + 1)
    ]


def smooth(padded_rows):
    weights = kernel_weights()
    row_count = padded_rows.shape[-2] - 2 * RADIUS
    vertical = weights[0] * padded_rows[..., 0:row_count, :]
    for offset in range(1, 2 * RADIUS + 1):
        vertical = vertical + weights[offset] * padded_rows[..., offset : offset + row_count, :]
    column_count = vertical.shape[-1]
    pad_width = [(0, 0)] * (vertical.ndim - 1) + [(RADIUS, RADIUS)]
    widened = jnp.pad(vertical, pad_width)
    total = weights[0] * widened[..., 0:column_count]
    for offset in range(1, 2 * RADIUS + 1):
        total = total + weights[offset] * widened[..., offset : offset + column_count]
    return total


def apply_highpass(highpass, series):
    return jnp.dot(
        highpass, series, precision=lax.Precision.HIGHEST, preferred_element_type=jnp.float32
    )


def shards(phases, coherence, pixel_index, send_list, counts, band_width):
    acq_loc = phases.shape[0]
    capacity = send_list.shape[1]
    highpass = temporal_matrix(band_width)
    live_slot = jnp.arange(capacity, dtype=jnp.int32)[None, :] < counts[0][:, None]
    slot_weight = jnp.where(live_slot, coherence[send_list], jnp.float32(0.0))
    slot_pixel = pixel_index[send_list]
    outgoing = phases[:, send_list] * slot_weight[None]
    arrived, arrived_weight, arrived_pixel = (
        lax.all_to_all(outgoing, "tile", split_axis=1, concat_axis=1, tiled=True),
        lax.all_to_all(slot_weight[None], "tile", split_axis=1, concat_axis=1, tiled=True),
        lax.all_to_all(slot_pixel[None], "tile", split_axis=1, concat_axis=1, tiled=True),
    )
    targets = arrived_pixel.reshape(-1)
    phase_image = (
        jnp.zeros((acq_loc, SLAB_PIX), jnp.float32).at[:, targets].add(arrived.reshape(acq_loc, -1))
    )
    weight_sum = jnp.zeros((SLAB_PIX,), jnp.float32).at[targets].add(arrived_weight.reshape(-1))
    series = lax.all_to_all(phase_image, "acq", split_axis=1, concat_axis=0, tiled=True)
    phase_image = lax.all_to_all(
        apply_highpass(highpass, series), "acq", split_axis=0, concat_axis=1, tiled=True
    )
    stacked = jnp.concatenate([phase_image, weight_sum[None, :]], axis=0).reshape(
        acq_loc + 1, ROWS_DEV, COLS
    )
    padded = with_halo(stacked, (("tile", 1),), RADIUS)
    smoothed = smooth(padded)
    screen = smoothed[:acq_loc] / jnp.maximum(smoothed[acq_loc], min_weight)
    flattened = screen.reshape(acq_loc, SLAB_PIX)
    sampled = flattened[:, arrived_pixel[0]]
    returned = lax.all_to_all(sampled, "tile", split_axis=1, concat_axis=1, tiled=True)
    residual = jnp.where(live_slot[None], phases[:, send_list] - returned, jnp.float32(0.0))
    return (residual.reshape(acq_loc, -1), screen)


def solution(mesh):
    return jax.shard_map(
        shards,
        mesh=mesh,
        in_specs=(P("acq", "tile"), P("tile"), P("tile"), P("tile", None), P("tile", None), P()),
        out_specs=(P("acq", "tile"), P("acq", "tile", None)),
        check_vma=False,
    )
```

profile of v0, /device:TPU:0, one launch (start us, length us, event | category | flops | bytes accessed | tf_op | source)
XLA Modules:
  0.0 134.2 jit_solution(15241608124049495737)
XLA Ops:
  0.7 0.7 fusion.58
  1.5 10.5 %gather_fusion.1 = s32[1024]{0:T(1024)} fusion(s32[16384]{0:T(1024)S(1)} %copy-done, s32[1024]{0:T(1024)S(1)} %fusion.58), kind=kCustom, calls=%fused_computation.1 | custom fusion | bytes 12288 | tf_op jit(solution)/shard_map/gather | solution.py:76
  12.0 7.3 %all-to-all-start = ((s32[1,8,128]{2,0,1:T(1,128)}), s32[1,8,128]{2,0,1:T(1,128)S(1)}, u32[]{:S(2)}, u32[]{:S(2)}) async-start(s32[1,8,128]{2,0,1:T(1,128)} %bitcast.5), calls=%async_computation | async-start | bytes 8192 | tf_op jit(solution)/shard_map/all_to_all | solution.py:81
  19.3 6.2 %gather_fusion.2 = f32[1024]{0:T(1024)S(1)} fusion(f32[16384]{0:T(1024)S(1)} %copy-done.1, s32[1024]{0:T(1024)S(1)} %fusion.58), kind=kCustom, calls=%fused_computation.2 | custom fusion | bytes 12288 | tf_op jit(solution)/shard_map/gather | solution.py:75
  25.5 4.6 %copy.23 = f32[16,16384]{0,1:T(8,128)} copy(f32[16,16384]{1,0:T(8,128)S(1)} %copy-done.3) | data formatting | bytes 2097152 | tf_op args[0]
  30.1 6.2 %gather_fusion = f32[1024,16]{1,0:T(8,128)S(1)} fusion(f32[16,16384]{0,1:T(8,128)} %copy.23, s32[1024]{0:T(1024)S(1)} %fusion.58), kind=kCustom, calls=%fused_computation | custom fusion | bytes 135168 | tf_op jit(solution)/shard_map/gather | solution.py:101
  36.5 0.7 bitcast_multiply_fusion
  37.2 6.0 %all-to-all-start.1 = ((f32[16,8,128]{2,0,1:T(8,128)}), f32[16,8,128]{2,0,1:T(8,128)S(1)}, u32[]{:S(2)}, u32[]{:S(2)}) async-start(f32[16,8,128]{2,0,1:T(8,128)} %bitcast_multiply_fusion), calls=%async_computation.1 | async-start | bytes 131072 | tf_op jit(solution)/shard_map/all_to_all | solution.py:79
  43.2 6.9 %all-to-all-done.1 = f32[16,8,128]{2,0,1:T(8,128)S(1)} async-done(((f32[16,8,128]{2,0,1:T(8,128)}), f32[16,8,128]{2,0,1:T(8,128)S(1)}, u32[]{:S(2)}, u32[]{:S(2)}) %all-to-all-start.1) | async-done | bytes 65568 | tf_op jit(solution)/shard_map/all_to_all | solution.py:79
  50.3 8.2 %scatter_custom_fusion = f32[16,8192]{0,1:T(8,128)} fusion(s32[1024]{0:T(1024)S(1)} %bitcast.63, f32[1024,16]{1,0:T(8,128)S(1)} %copy.26, f32[]{:T(128)} %constant.2.clone.1), kind=kCustom, calls=%fused_computation.6 | custom fusion | flops 16384 | bytes 524292 | tf_op jit(solution)/shard_map/scatter-add | solution.py:85
  58.5 3.5 %copy.27 = f32[16,4,2048]{2,0,1:T(8,128)} copy(f32[16,4,2048]{0,2,1:T(8,128)} %bitcast.55) | data formatting | bytes 1048576 | tf_op jit(solution)/shard_map/all_to_all | solution.py:88
  62.0 3.5 %all-to-all-start.2 = ((f32[16,4,2048]{2,0,1:T(8,128)}), f32[16,4,2048]{2,0,1:T(8,128)S(1)}, u32[]{:S(2)}, u32[]{:S(2)}) async-start(f32[16,4,2048]{2,0,1:T(8,128)} %copy.27), calls=%async_computation.2 | async-start | bytes 1048576 | tf_op jit(solution)/shard_map/all_to_all | solution.py:88
  65.8 0.7 compare_select_fusion.1
  66.4 7.9 %all-to-all-done.2 = f32[16,4,2048]{2,0,1:T(8,128)S(1)} async-done(((f32[16,4,2048]{2,0,1:T(8,128)}), f32[16,4,2048]{2,0,1:T(8,128)S(1)}, u32[]{:S(2)}, u32[]{:S(2)}) %all-to-all-start.2) | async-done | bytes 524320 | tf_op jit(solution)/shard_map/all_to_all | solution.py:88
  74.3 3.3 %all-to-all-start.4 = ((f32[1,8,128]{2,0,1:T(1,128)}), f32[1,8,128]{2,0,1:T(1,128)S(1)}, u32[]{:S(2)}, u32[]{:S(2)}) async-start(f32[1,8,128]{2,0,1:T(1,128)} %compare_select_fusion.1), calls=%async_computation.4 | async-start | bytes 8192 | tf_op jit(solution)/shard_map/all_to_all | solution.py:80
  77.6 1.4 %fusion.43 = f32[4,16,2048]{2,1,0:T(8,128)} fusion(f32[64,2048,1]{1,0,2:T(8,128)S(1)} %bitcast.57, f32[4,16]{1,0:T(4,128)S(1)} %div.34, s32[4,16]{1,0:T(4,128)S(1)} %le.27, s32[4,16]{1,0:T(4,128)S(1)} %ge.32, s32[4,16]{1,0:T(4,128)S(1)} %multiply_add_fusion), kind=kOutput, calls=%fused_computation.77 | convolution fusion | flops 100696064 | bytes 1049600 | tf_op jit(solution)/shard_map/dot_general | solution.py:65
  79.0 4.9 %all-to-all-done.4 = f32[1,8,128]{2,0,1:T(1,128)S(1)} async-done(((f32[1,8,128]{2,0,1:T(1,128)}), f32[1,8,128]{2,0,1:T(1,128)S(1)}, u32[]{:S(2)}, u32[]{:S(2)}) %all-to-all-start.4) | async-done | bytes 4128 | tf_op jit(solution)/shard_map/all_to_all | solution.py:80
  83.9 3.5 %all-to-all-start.3 = ((f32[4,16,2048]{2,1,0:T(8,128)}), f32[4,16,2048]{2,1,0:T(8,128)S(1)}, u32[]{:S(2)}, u32[]{:S(2)}) async-start(f32[4,16,2048]{2,1,0:T(8,128)} %fusion.43), calls=%async_computation.3 | async-start | bytes 1048576 | tf_op jit(solution)/shard_map/all_to_all | solution.py:89
  87.4 5.9 %scatter_custom_fusion.1 = f32[8192]{0:T(1024)S(1)} fusion(s32[1024]{0:T(1024)S(1)} %bitcast.64, f32[1024]{0:T(1024)S(1)} %bitcast.65, f32[]{:T(128)} %constant.2.clone.1), kind=kCustom, calls=%fused_computation.88 | custom fusion | flops 1024 | bytes 32772 | tf_op jit(solution)/shard_map/scatter-add | solution.py:87
  93.4 2.8 %all-to-all-done.3 = f32[4,16,2048]{2,1,0:T(8,128)S(1)} async-done(((f32[4,16,2048]{2,1,0:T(8,128)}), f32[4,16,2048]{2,1,0:T(8,128)S(1)}, u32[]{:S(2)}, u32[]{:S(2)}) %all-to-all-start.3) | async-done | bytes 524320 | tf_op jit(solution)/shard_map/all_to_all | solution.py:89
  96.2 0.3 copy.28
  97.0 2.5 %collective-permute-start = (f32[17,4,1024]{2,1,0:T(4,128)S(1)}, f32[17,4,1024]{2,1,0:T(4,128)S(1)}, u32[]{:S(2)}, u32[]{:S(2)}) collective-permute-start(f32[17,4,1024]{2,1,0:T(4,128)S(1)} %get-tuple-element.2), channel_id=1, source_target_pairs={{0,4},{4,8},{8,12},{12,16},{16,20},{20,24},{24,28},{1,5},{5,9},{9,... | collective-permute-start | bytes 835592 | tf_op jit(solution)/shard_map/ppermute | solution.py:24
  99.5 1.3 collective-permute-start.1
  100.8 10.3 %collective-permute-done = f32[17,4,1024]{2,1,0:T(4,128)S(1)} collective-permute-done((f32[17,4,1024]{2,1,0:T(4,128)S(1)}, f32[17,4,1024]{2,1,0:T(4,128)S(1)}, u32[]{:S(2)}, u32[]{:S(2)}) %collective-permute-start) | collective-permute-done | bytes 278560 | tf_op jit(solution)/shard_map/ppermute | solution.py:24
  111.1 1.0 fusion.21
  112.1 1.2 fusion.10
  113.5 2.7 %copy.29 = f32[16,8,1024]{0,2,1:T(8,128)} copy(f32[16,8,1024]{2,1,0:T(8,128)S(1)} %slice_divide_fusion) | data formatting | bytes 1048576 | tf_op jit(solution)/shard_map/div | solution.py:97
  116.2 5.0 %gather_fusion.3 = f32[1024,16]{1,0:T(8,128)S(1)} fusion(f32[16,8192]{0,1:T(8,128)} %bitcast.56, s32[1024]{0:T(1024)S(1)} %fusion.60), kind=kCustom, calls=%fused_computation.3 | custom fusion | bytes 135168 | tf_op jit(solution)/shard_map/gather | solution.py:99
  121.2 0.8 copy.30
  122.0 4.7 %all-to-all-start.5 = ((f32[16,8,128]{2,0,1:T(8,128)}), f32[16,8,128]{2,0,1:T(8,128)S(1)}, u32[]{:S(2)}, u32[]{:S(2)}) async-start(f32[16,8,128]{2,0,1:T(8,128)} %bitcast.22), calls=%async_computation.5 | async-start | bytes 131072 | tf_op jit(solution)/shard_map/all_to_all | solution.py:100
  126.7 6.8 %all-to-all-done.5 = f32[16,8,128]{2,0,1:T(8,128)S(1)} async-done(((f32[16,8,128]{2,0,1:T(8,128)}), f32[16,8,128]{2,0,1:T(8,128)S(1)}, u32[]{:S(2)}, u32[]{:S(2)}) %all-to-all-start.5) | async-done | bytes 65568 | tf_op jit(solution)/shard_map/all_to_all | solution.py:100
  133.5 0.6 copy_bitcast_fusion
  (33 shorter events, 1.4 us)
Async XLA Ops:
  0.6 0.8 copy-start
  0.6 18.7 %copy-start.1 = (f32[16384]{0:T(1024)S(1)}, f32[16384]{0:T(1024)}, u32[]{:S(2)}) copy-start(f32[16384]{0:T(1024)} %param.7) | copy-start | bytes 196612
  1.5 24.0 %copy-start.3 = (f32[16,16384]{1,0:T(8,128)S(1)}, f32[16,16384]{1,0:T(8,128)}, u32[]{:S(2)}) copy-start(f32[16,16384]{1,0:T(8,128)} %param.6) | copy-start | bytes 3145732
  12.0 25.2 %all-to-all-start = ((s32[1,8,128]{2,0,1:T(1,128)}), s32[1,8,128]{2,0,1:T(1,128)S(1)}, u32[]{:S(2)}, u32[]{:S(2)}) async-start(s32[1,8,128]{2,0,1:T(1,128)} %bitcast.5), calls=%async_computation | async-start | bytes 8192 | tf_op jit(solution)/shard_map/all_to_all | solution.py:81
  25.5 11.0 %copy-start.4 = (s32[1,8]{1,0:T(1,128)S(1)}, s32[1,8]{1,0:T(1,128)}, u32[]{:S(2)}) copy-start(s32[1,8]{1,0:T(1,128)} %param.10) | copy-start | bytes 100
  37.2 12.9 %all-to-all-start.1 = ((f32[16,8,128]{2,0,1:T(8,128)}), f32[16,8,128]{2,0,1:T(8,128)S(1)}, u32[]{:S(2)}, u32[]{:S(2)}) async-start(f32[16,8,128]{2,0,1:T(8,128)} %bitcast_multiply_fusion), calls=%async_computation.1 | async-start | bytes 131072 | tf_op jit(solution)/shard_map/all_to_all | solution.py:79
  50.3 15.2 %copy-start.5 = (s32[64]{0:T(128)S(1)}, s32[64]{0:T(128)}, u32[]{:S(2)}) copy-start(s32[64]{0:T(128)} %param.11) | copy-start | bytes 772
  62.0 12.3 %all-to-all-start.2 = ((f32[16,4,2048]{2,0,1:T(8,128)}), f32[16,4,2048]{2,0,1:T(8,128)S(1)}, u32[]{:S(2)}, u32[]{:S(2)}) async-start(f32[16,4,2048]{2,0,1:T(8,128)} %copy.27), calls=%async_computation.2 | async-start | bytes 1048576 | tf_op jit(solution)/shard_map/all_to_all | solution.py:88
  74.3 9.6 %all-to-all-start.4 = ((f32[1,8,128]{2,0,1:T(1,128)}), f32[1,8,128]{2,0,1:T(1,128)S(1)}, u32[]{:S(2)}, u32[]{:S(2)}) async-start(f32[1,8,128]{2,0,1:T(1,128)} %compare_select_fusion.1), calls=%async_computation.4 | async-start | bytes 8192 | tf_op jit(solution)/shard_map/all_to_all | solution.py:80
  83.9 12.3 %all-to-all-start.3 = ((f32[4,16,2048]{2,1,0:T(8,128)}), f32[4,16,2048]{2,1,0:T(8,128)S(1)}, u32[]{:S(2)}, u32[]{:S(2)}) async-start(f32[4,16,2048]{2,1,0:T(8,128)} %fusion.43), calls=%async_computation.3 | async-start | bytes 1048576 | tf_op jit(solution)/shard_map/all_to_all | solution.py:89
  97.0 14.1 %collective-permute-start = (f32[17,4,1024]{2,1,0:T(4,128)S(1)}, f32[17,4,1024]{2,1,0:T(4,128)S(1)}, u32[]{:S(2)}, u32[]{:S(2)}) collective-permute-start(f32[17,4,1024]{2,1,0:T(4,128)S(1)} %get-tuple-element.2), channel_id=1, source_target_pairs={{0,4},{4,8},{8,12},{12,16},{16,20},{20,24},{24,28},{1,5},{5,9},{9,... | collective-permute-start | bytes 835592 | tf_op jit(solution)/shard_map/ppermute | solution.py:24
  99.5 11.7 %collective-permute-start.1 = (f32[17,4,1024]{2,1,0:T(4,128)S(1)}, f32[17,4,1024]{2,1,0:T(4,128)S(1)}, u32[]{:S(2)}, u32[]{:S(2)}) collective-permute-start(f32[17,4,1024]{2,1,0:T(4,128)S(1)} %get-tuple-element.3), channel_id=1, source_target_pairs={{4,0},{8,4},{12,8},{16,12},{20,16},{24,20},{28,24},{5,1},{9,5},{13... | collective-permute-start | bytes 835592 | tf_op jit(solution)/shard_map/ppermute | solution.py:26
  113.5 20.7 %copy-start.2 = (f32[16,8,1024]{2,1,0:T(8,128)}, f32[16,8,1024]{2,1,0:T(8,128)S(1)}, u32[]{:S(2)}) copy-start(f32[16,8,1024]{2,1,0:T(8,128)S(1)} %slice_divide_fusion) | copy-start | bytes 1572868
  122.0 11.6 %all-to-all-start.5 = ((f32[16,8,128]{2,0,1:T(8,128)}), f32[16,8,128]{2,0,1:T(8,128)S(1)}, u32[]{:S(2)}, u32[]{:S(2)}) async-start(f32[16,8,128]{2,0,1:T(8,128)} %bitcast.22), calls=%async_computation.5 | async-start | bytes 131072 | tf_op jit(solution)/shard_map/all_to_all | solution.py:100
where the time goes:
time: 135 us; the launch traced here: 134 us
  local copies, waits for them, and re-layouts  40.9 us (30%)
  waiting for transfers between devices  39.7 us (29%)
  starting transfers between devices  31.9 us (24%)
  other arithmetic  19.3 us (14%)
  matrix products  1.42 us (1%)
    gather x1, local copies, waits for them, and re-layouts, shards(): slot_pixel = pixel_index[send_list]  10.5 us
    ppermute x1, waiting for transfers between devices, with_halo(): lax.ppermute(tail, axis, [(i, (i + 1) % count) for i in range(ends)])  10.3 us
    scatter-add x1, other arithmetic, shards(): jnp.zeros((acq_loc, SLAB_PIX), jnp.float32).at[:, targets]  8.21 us
    all_to_all x1, waiting for transfers between devices, shards(): lax.all_to_all(phase_image, 'acq', split_axis=1, concat_axis=0, tiled=True)  7.86 us
    all_to_all x1, starting transfers between devices, shards(): lax.all_to_all(slot_pixel[None], 'tile', split_axis=1, concat_axis=1, til...  7.28 us
    all_to_all x1, waiting for transfers between devices, shards(): lax.all_to_all(outgoing, 'tile', split_axis=1, concat_axis=1, tiled=True)  6.9 us
    all_to_all x1, waiting for transfers between devices, shards(): lax.all_to_all(sampled, 'tile', split_axis=1, concat_axis=1, tiled=True)  6.83 us
    gather x2, local copies, waits for them, and re-layouts, shards(): phases[:, send_list] - returned  6.35 us
  transfers between devices with their start and end apart: 8, of which 6 were waited for; matrix products, arithmetic and copies ran while one was open for 20% of the time, Pallas kernels for 0%

commit v1 on v0

--- a/solution.py
+++ b/solution.py
@@ -1,6 +1,10 @@
+import functools
+
 import jax
 import jax.numpy as jnp
 from jax import lax
+from jax.experimental import pallas as pl
+from jax.experimental.pallas import tpu as pltpu
 from jax.sharding import PartitionSpec as P
 
 ACQ = 64
@@ -8,6 +12,8 @@
 COLS = 1024
 RADIUS = 4
 SLAB_PIX = 8192
+HALF = 64
+LANES = 128
 
 
 min_weight = 0.1
@@ -67,7 +73,7 @@
     )
 
 
-def shards(phases, coherence, pixel_index, send_list, counts, band_width):
+def exchange_shards(phases, coherence, pixel_index, send_list, counts, band_width):
     acq_loc = phases.shape[0]
     capacity = send_list.shape[1]
     highpass = temporal_matrix(band_width)
@@ -102,9 +108,320 @@
     return (residual.reshape(acq_loc, -1), screen)
 
 
+def heavy_tiles(counts_ref, n_tile):
+    first = jnp.int32(0)
+    last = jnp.int32(0)
+    for t in range(n_tile):
+        is_heavy = counts_ref[0, t] >= HALF
+        last = jnp.where(is_heavy, t, last)
+        back = n_tile - 1 - t
+        first = jnp.where(counts_ref[0, back] >= HALF, back, first)
+    return first, last
+
+
+def split_bf16(x):
+    high = x.astype(jnp.bfloat16)
+    return high, (x - high.astype(jnp.float32)).astype(jnp.bfloat16)
+
+
+def dot_f32(a, b, dims):
+    return lax.dot_general(a, b, (dims, ((), ())), preferred_element_type=jnp.float32)
+
+
+NN = ((1,), (0,))
+NT = ((1,), (1,))
+
+
+def packed_rows(counts_ref, list_ref, n_tile):
+    first, last = heavy_tiles(counts_ref, n_tile)
+    lane = lax.broadcasted_iota(jnp.int32, (1, LANES), 1)
+    lower = lane < HALF
+    slot = lane & (HALF - 1)
+    indices, tiles, lives = [], [], []
+    for p in range(n_tile // 2):
+        even = list_ref[pl.ds(2 * p, 1), :]
+        odd = pltpu.roll(list_ref[pl.ds(2 * p + 1, 1), :], HALF, 1)
+        indices.append(jnp.where(lower, even, odd))
+        tiles.append(jnp.where(lower, 2 * p, 2 * p + 1))
+        lives.append(
+            slot < jnp.where(lower, counts_ref[0, 2 * p], counts_ref[0, 2 * p + 1])
+        )
+    early = pltpu.roll(list_ref[pl.ds(first, 1), :], HALF, 1)
+    late = list_ref[pl.ds(last, 1), :]
+    indices.append(jnp.where(lower, early, late))
+    tiles.append(jnp.where(lower, first, last))
+    late_count = jnp.where(first == last, 0, counts_ref[0, last])
+    lives.append(slot + HALF < jnp.where(lower, counts_ref[0, first], late_count))
+    return (
+        jnp.concatenate(indices, 1),
+        jnp.concatenate(tiles, 1),
+        jnp.concatenate([x.astype(jnp.float32) for x in lives], 1),
+    )
+
+
+LO = 512
+
+
+def gather_kernel(n_tile, counts_ref, list_ref, phases_ref, coh_ref, pix_ref, out_ref, own_ref, wg_ref):
+    acq_loc, local = phases_ref.shape
+    index, tile, live = packed_rows(counts_ref, list_ref, n_tile)
+    packed = index.shape[1]
+    low = index & (LANES - 1)
+    high = index >> 7
+    chosen = lax.broadcasted_iota(jnp.int32, (LANES, packed), 0) == low
+    table_rows = coh_ref.shape[0]
+    coh_hi, coh_lo = split_bf16(coh_ref[...])
+    pix = pix_ref[...]
+    table = jnp.concatenate(
+        [
+            coh_hi,
+            coh_lo,
+            (pix >> 6).astype(jnp.float32).astype(jnp.bfloat16),
+            (pix & 63).astype(jnp.float32).astype(jnp.bfloat16),
+        ],
+        0,
+    )
+    columns = dot_f32(table, chosen.astype(jnp.float32).astype(jnp.bfloat16), NN)
+    row_is = lax.broadcasted_iota(jnp.int32, (table_rows, packed), 0) == high
+
+    def pick(k):
+        part = columns[k * table_rows : (k + 1) * table_rows]
+        return jnp.sum(jnp.where(row_is, part, 0.0), axis=0, keepdims=True)
+
+    weight = (pick(0) + pick(1)) * live
+    pixel = pick(2) * 64.0 + pick(3) + tile.astype(jnp.float32) * float(SLAB_PIX)
+    sub = lax.broadcasted_iota(jnp.int32, (8, packed), 0)
+    wg_ref[...] = jnp.where(sub == 0, weight, jnp.where(sub == 1, pixel, 0.0))
+    low = index & (LO - 1)
+    high = index >> 9
+    chosen = (lax.broadcasted_iota(jnp.int32, (LO, packed), 0) == low)
+    chosen = chosen.astype(jnp.float32).astype(jnp.bfloat16)
+    own = jnp.zeros((acq_loc, packed), jnp.float32)
+    pieces = local // LO
+    step = 8
+    for start in range(0, pieces, step):
+        block = jnp.concatenate(
+            [phases_ref[:, h * LO : (h + 1) * LO] for h in range(start, start + step)], 0
+        )
+        block_hi, block_lo = split_bf16(block)
+        both = dot_f32(block_hi, chosen, NN) + dot_f32(block_lo, chosen, NN)
+        for h in range(step):
+            own = jnp.where(high == start + h, both[h * acq_loc : (h + 1) * acq_loc], own)
+    own_ref[...] = own
+    out_ref[...] = own * weight
+
+
+def filter_kernel(h_ref, *refs):
+    *parts, wg_ref, out_ref = refs
+    acq_loc = parts[0].shape[0]
+    series = jnp.concatenate([part[...] for part in parts], 0)
+    out_ref[0:acq_loc, :] = lax.dot_general(
+        h_ref[...],
+        series,
+        (NN, ((), ())),
+        precision=lax.Precision.HIGHEST,
+        preferred_element_type=jnp.float32,
+    )
+    out_ref[acq_loc:, :] = wg_ref[...]
+
+
+def first_pair(tile, n_pair):
+    return jnp.clip((tile + 1) // 2 - 1, 0, max(n_pair - 2, 0))
+
+
+def hat(distance):
+    return jnp.maximum(float(RADIUS + 1) - jnp.abs(distance), 0.0)
+
+
+def split_pixel(pixel):
+    whole = pixel.astype(jnp.int32)
+    return (whole >> 10).astype(jnp.float32), (whole & (COLS - 1)).astype(jnp.float32)
+
+
+def screen_kernel(
+    n_tile, me_ref, counts_ref, list_ref, all_ref, mine_ref, own_ref, screen_ref, residual_ref,
+    lhs_ref, col_ref, pair_ref, res_ref,
+):
+    n_src, rows, packed = all_ref.shape
+    acq_loc = own_ref.shape[0]
+    n_pair = n_tile // 2
+    width = 3 * LANES
+    limit = min_weight * float((RADIUS + 1) ** 4)
+    me = me_ref[0]
+    first, last = heavy_tiles(counts_ref, n_tile)
+
+    def blocks(src, pair):
+        start = pl.multiple_of(pair * LANES, LANES)
+        return jnp.concatenate(
+            [
+                all_ref[src, :, pl.ds(start, LANES)],
+                all_ref[src, :, pl.ds(pl.multiple_of(start + LANES, LANES), LANES)],
+                all_ref[src, :, packed - LANES :],
+            ],
+            1,
+        )
+
+    top = (me * ROWS_DEV).astype(jnp.float32)
+    row_at = lax.broadcasted_iota(jnp.int32, (ROWS_DEV, width), 0).astype(jnp.float32) + top
+    col_at = lax.broadcasted_iota(jnp.int32, (COLS, width), 0).astype(jnp.float32)
+    pair = first_pair(me, n_pair)
+    n_lhs = (acq_loc + 1) * ROWS_DEV
+    for src in range(n_src):
+        data = blocks(src, pair)
+        row, col = split_pixel(data[acq_loc + 1 : acq_loc + 2])
+        across = hat(row_at - row)
+        lanes = pl.ds(src * width, width)
+        part = jnp.concatenate([across * data[a : a + 1] for a in range(acq_loc + 1)], 0)
+        part_hi, part_lo = split_bf16(part)
+        lhs_ref[0:n_lhs, lanes] = part_hi
+        lhs_ref[n_lhs : 2 * n_lhs, lanes] = part_lo
+        col_ref[:, lanes] = hat(col_at - col).astype(jnp.bfloat16)
+    for c in range(0, COLS, 256):
+        image = dot_f32(lhs_ref[...], col_ref[c : c + 256, :], NT)
+        image = image[0:n_lhs] + image[n_lhs:]
+        below = jnp.maximum(image[acq_loc * ROWS_DEV :], limit)
+        for a in range(acq_loc):
+            screen_ref[a, :, c : c + 256] = image[a * ROWS_DEV : (a + 1) * ROWS_DEV] / below
+
+    mine = mine_ref[...]
+    my_row, my_col = split_pixel(mine[1:2])
+
+    def down(row, block):
+        spread = jnp.broadcast_to(row[:, block * LANES : (block + 1) * LANES], (LANES, LANES))
+        return jnp.transpose(spread)
+
+    groups = []
+    for t in range(n_tile):
+        p = min(max((t + 1) // 2 - 1, 0), max(n_pair - 2, 0))
+        if groups and groups[-1][2] == p:
+            groups[-1][1] += HALF
+        else:
+            groups.append([t * HALF, HALF, p])
+    base = n_pair * LANES
+    groups.append([base, HALF, first_pair(first, n_pair)])
+    groups.append([base + HALF, HALF, first_pair(last, n_pair)])
+    rows_down = jnp.concatenate([down(my_row, b) for b in range(n_pair + 1)], 0)
+    cols_down = jnp.concatenate([down(my_col, b) for b in range(n_pair + 1)], 0)
+    samples = []
+    for start, size, p in groups:
+        r_i = rows_down[start : start + size]
+        c_i = cols_down[start : start + size]
+        values = []
+        for src in range(n_src):
+            data = blocks(src, p)
+            row, col = split_pixel(data[acq_loc + 1 : acq_loc + 2])
+            value_hi, value_lo = split_bf16(data[0 : acq_loc + 8])
+            values.append(jnp.concatenate([value_hi, value_lo], 0))
+            for b in range(3):
+                cut = slice(b * LANES, (b + 1) * LANES)
+                both = hat(r_i - row[:, cut]) * hat(c_i - col[:, cut])
+                pair_ref[0:size, src * width + b * LANES : src * width + (b + 1) * LANES] = (
+                    both.astype(jnp.bfloat16)
+                )
+        value = jnp.concatenate(values, 1)
+        got = dot_f32(value, pair_ref[0:size, :], NT)
+        got = got[0 : acq_loc + 8] + got[acq_loc + 8 :]
+        samples.append(got[0:acq_loc] / jnp.maximum(got[acq_loc : acq_loc + 1], limit))
+    res_ref[...] = own_ref[...] - jnp.concatenate(samples, 1)
+
+    lane = lax.broadcasted_iota(jnp.int32, (1, LANES), 1)
+    lower = lane < HALF
+    heavy = res_ref[:, base:]
+    turned = pltpu.roll(heavy, HALF, 1)
+    for t in range(n_tile):
+        near = res_ref[:, (t // 2) * LANES : (t // 2 + 1) * LANES]
+        if t % 2:
+            near = pltpu.roll(near, HALF, 1)
+        far = jnp.where(first == t, turned, heavy)
+        both = jnp.where(lower, near, far)
+        residual_ref[:, t * LANES : (t + 1) * LANES] = jnp.where(
+            lane < counts_ref[0, t], both, 0.0
+        )
+
+
+def xor_permute(x, axis, mask):
+    count = lax.axis_size(axis)
+    return lax.ppermute(x, axis, [(i, i ^ mask) for i in range(count)])
+
+
+def gathered_shards(phases, coherence, pixel_index, send_list, counts, band_width):
+    acq_loc, local = phases.shape
+    n_tile = lax.axis_size("tile")
+    n_acq = lax.axis_size("acq")
+    packed = (n_tile // 2 + 1) * LANES
+    smem = pl.BlockSpec(memory_space=pltpu.SMEM)
+    vmem = pl.BlockSpec(memory_space=pltpu.VMEM)
+    f32 = jnp.float32
+    outgoing, own, wg = pl.pallas_call(
+        functools.partial(gather_kernel, n_tile),
+        out_shape=(
+            jax.ShapeDtypeStruct((acq_loc, packed), f32),
+            jax.ShapeDtypeStruct((acq_loc, packed), f32),
+            jax.ShapeDtypeStruct((8, packed), f32),
+        ),
+        in_specs=[smem, vmem, vmem, vmem, vmem],
+        out_specs=(vmem, vmem, vmem),
+        name="gather_slots",
+    )(
+        counts,
+        send_list,
+        phases,
+        coherence.reshape(-1, LANES),
+        pixel_index.reshape(-1, LANES),
+    )
+    here = lax.axis_index("acq")
+    parts = [outgoing] + [xor_permute(outgoing, "acq", k) for k in range(1, n_acq)]
+    source = here ^ jnp.arange(n_acq, dtype=jnp.int32)
+    column = (source[:, None] * acq_loc + jnp.arange(acq_loc, dtype=jnp.int32)[None]).reshape(1, -1)
+    row = here * acq_loc + jnp.arange(acq_loc, dtype=jnp.int32)
+    band = lax.dynamic_slice_in_dim(band_width, here * acq_loc, acq_loc)
+    lower = jnp.maximum(row - band, 0)[:, None]
+    upper = jnp.minimum(row + band, ACQ - 1)[:, None]
+    inside = ((column >= lower) & (column <= upper)).astype(f32)
+    highpass = (column == row[:, None]).astype(f32) - inside / (upper - lower + 1).astype(f32)
+    filtered = pl.pallas_call(
+        filter_kernel,
+        out_shape=jax.ShapeDtypeStruct((acq_loc + 8, packed), f32),
+        in_specs=[vmem] * (n_acq + 2),
+        out_specs=vmem,
+        name="filter_slots",
+    )(highpass, *parts, wg)
+    held = filtered[None]
+    half = n_tile // 2
+    if half > 1:
+        held = jnp.concatenate([held, xor_permute(held, "tile", half)], 0)
+        held = jnp.concatenate([held] + [xor_permute(held, "tile", k) for k in range(1, half)], 0)
+    else:
+        held = jnp.concatenate([held, xor_permute(held, "tile", 1)], 0)
+    me = lax.axis_index("tile").astype(jnp.int32).reshape(1)
+    n_src = n_tile
+    n_lhs = 2 * (acq_loc + 1) * ROWS_DEV
+    width = n_src * 3 * LANES
+    screen, residual = pl.pallas_call(
+        functools.partial(screen_kernel, n_tile),
+        out_shape=(
+            jax.ShapeDtypeStruct((acq_loc, ROWS_DEV, COLS), f32),
+            jax.ShapeDtypeStruct((acq_loc, n_tile * LANES), f32),
+        ),
+        in_specs=[smem, smem, vmem, vmem, vmem, vmem],
+        out_specs=(vmem, vmem),
+        scratch_shapes=[
+            pltpu.VMEM((n_lhs, width), jnp.bfloat16),
+            pltpu.VMEM((COLS, width), jnp.bfloat16),
+            pltpu.VMEM((3 * HALF, width), jnp.bfloat16),
+            pltpu.VMEM((acq_loc, packed), f32),
+        ],
+        compiler_params=pltpu.CompilerParams(vmem_limit_bytes=48 << 20),
+        name="screen_and_residual",
+    )(me, counts, send_list, held, wg, own)
+    return residual, screen
+
+
 def solution(mesh):
+    n_tile = mesh.shape["tile"]
+    few = n_tile in (4, 8)
     return jax.shard_map(
-        shards,
+        gathered_shards if few else exchange_shards,
         mesh=mesh,
         in_specs=(P("acq", "tile"), P("tile"), P("tile"), P("tile", None), P("tile", None), P()),
         out_specs=(P("acq", "tile"), P("acq", "tile", None)),

time: 135 us -> 39.2 us (0.29)
  local copies, waits for them, and re-layouts: 40.9 us -> 2.05 us
  waiting for transfers between devices: 39.7 us -> 11.5 us
  starting transfers between devices: 31.9 us -> 9.32 us
  other arithmetic: 19.3 us -> 1.67 us
  Pallas kernels: 0 us -> 13.7 us
  matrix products: 1.42 us -> 0 us
    all_to_all x6 -> x0, waiting for transfers between devices: 29.3 us -> none  [the longest x1 7.86 us: shards(): lax.all_to_all(phase_image, 'acq', split_axis=1, concat_axis=0, tiled=True)]
    gather x6 -> x0, local copies, waits for them, and re-layouts: 28.8 us -> none  [the longest x1 10.5 us: shards(): slot_pixel = pixel_index[send_list]]
    all_to_all x6 -> x0, starting transfers between devices: 28.2 us -> none  [the longest x1 7.28 us: shards(): lax.all_to_all(slot_pixel[None], 'tile', split_axis=1, concat_axis=1, til...]
    scatter-add x2 -> x0, other arithmetic: 14.2 us -> none  [the longest x1 8.21 us: shards(): jnp.zeros((acq_loc, SLAB_PIX), jnp.float32).at[:, targets]]
    pallas_call x0 -> x3, Pallas kernels: none -> 13.7 us  [the longest x1 8.75 us: gathered_shards(): pl.pallas_call(functools.partial(screen_kernel, n_tile), out_shape=(jax.S...]
    ppermute x2 -> x7, starting transfers between devices: 3.77 us -> 9.32 us  [xor_permute(): return lax.ppermute(x, axis, [(i, i ^ mask) for i in range(count)])]
    all_to_all x2 -> x0, local copies, waits for them, and re-layouts: 3.84 us -> none  [the longest x1 3.5 us: shards(): lax.all_to_all(phase_image, 'acq', split_axis=1, concat_axis=0, tiled=True)]
    unnamed x14 -> x22, local copies, waits for them, and re-layouts: 4.77 us -> 1.95 us
  transfers between devices with their start and end apart: 8 -> 7, of which waited for: 6 -> 6; matrix products, arithmetic and copies ran while one was open for 20% -> 2% of each run, Pallas kernels for 0% -> 0%
where the time goes in v1:
time: 39.2 us; the launch traced here: 38.9 us
  Pallas kernels  13.7 us (35%)
  waiting for transfers between devices  11.5 us (29%)
  starting transfers between devices  9.32 us (24%)
  local copies, waits for them, and re-layouts  2.05 us (5%)
  other arithmetic  1.67 us (4%)
  between operations  0.71 us (2%)
    ppermute x7, waiting for transfers between devices, xor_permute(): return lax.ppermute(x, axis, [(i, i ^ mask) for i in range(count)])  11.5 us
    ppermute x7, starting transfers between devices, xor_permute(): return lax.ppermute(x, axis, [(i, i ^ mask) for i in range(count)])  9.32 us
    pallas_call x1, Pallas kernels, gathered_shards(): pl.pallas_call(functools.partial(screen_kernel, n_tile), out_shape=(jax.S...  8.75 us
    pallas_call x1, Pallas kernels, gathered_shards(): pl.pallas_call(functools.partial(gather_kernel, n_tile), out_shape=(jax.S...  3.28 us
    unnamed x22, local copies, waits for them, and re-layouts  1.95 us
    pallas_call x1, Pallas kernels, gathered_shards(): pl.pallas_call(filter_kernel, out_shape=jax.ShapeDtypeStruct((acq_loc + 8...  1.68 us
    concatenate x1, other arithmetic, gathered_shards(): held = jnp.concatenate([held, xor_permute(held, 'tile', half)], 0)  0.84 us
  transfers between devices with their start and end apart: 7, of which 6 were waited for; matrix products, arithmetic and copies ran while one was open for 2% of the time, Pallas kernels for 0%

profile of v1, /device:TPU:0, one launch (start us, length us, event | category | flops | bytes accessed | tf_op | source)
XLA Modules:
  0.0 38.9 jit_solution(9175816347938984383)
XLA Ops:
  0.6 3.3 %gather_slots.1 = (f32[16,640]{1,0:T(8,128)}, f32[16,640]{1,0:T(8,128)}, f32[8,640]{1,0:T(8,128)}) custom-call(s32[1,8]{1,0:T(1,128)} %counts_ref.3, s32[8,128]{1,0:T(8,128)} %list_ref.3, f32[16,16384]{1,0:T(8,128)} %phases_ref.1, f32[128,128]{1,0:T(8,128)} %bitcast.7, s32[128,128]{1,0:T(8,128)} %bitcast.8), custom_call_target="tpu_custom_call" | custom-call | tf_op jit(solution)/shard_map/gather_slots/pallas_call | solution.py:355
  3.9 0.5 %collective-permute-start = (f32[16,640]{1,0:T(8,128)}, f32[16,640]{1,0:T(8,128)S(1)}, u32[]{:S(2)}, u32[]{:S(2)}) collective-permute-start(f32[16,640]{1,0:T(8,128)} %get-tuple-element.7.refs_0_), channel_id=1, source_target_pairs={{0,1},{1,0},{2,3},{3,2},{4,5},{5,4},{6,7},{7,6},{8,9},{9,8},{10,11... | collective-permute-start | bytes 122888 | tf_op jit(solution)/shard_map/ppermute | solution.py:344
  4.4 2.5 %collective-permute-start.1 = (f32[16,640]{1,0:T(8,128)}, f32[16,640]{1,0:T(8,128)S(1)}, u32[]{:S(2)}, u32[]{:S(2)}) collective-permute-start(f32[16,640]{1,0:T(8,128)} %get-tuple-element.7.refs_0_), channel_id=1, source_target_pairs={{0,2},{1,3},{2,0},{3,1},{4,6},{5,7},{6,4},{7,5},{8,10},{9,11},{10,... | collective-permute-start | bytes 122888 | tf_op jit(solution)/shard_map/ppermute | solution.py:344
  6.9 0.1 collective-permute-start.2
  7.0 0.1 iota_add_fusion
  7.1 0.1 add.43
  7.2 0.7 %copy-done.8 = s32[64]{0:T(128)S(1)} copy-done((s32[64]{0:T(128)S(1)}, s32[64]{0:T(128)}, u32[]{:S(2)}) %copy-start.8) | copy-done | bytes 280
  7.8 0.1 add_convert_fusion
  7.9 0.7 %divide_subtract_fusion.h_ref = f32[16,64]{1,0:T(8,128)} fusion(f32[16]{0:T(128)S(1)} %get-tuple-element.12, s32[64]{0:T(128)S(1)} %add.43, s32[16]{0:T(128)S(1)} %get-tuple-element.14, s32[16]{0:T(128)S(1)} %get-tuple-element.13, s32[16]{0:T(128)S(1)} %iota_add_fusion.1), kind=kLoop, calls=%fused_computation.6 | loop fusion | flops 8192 | bytes 4608 | tf_op jit(solution)/shard_map/sub | solution.py:381
  8.6 0.0 collective-permute-done.refs_1_
  8.6 0.7 %collective-permute-done.1.refs_2_ = f32[16,640]{1,0:T(8,128)S(1)} collective-permute-done((f32[16,640]{1,0:T(8,128)}, f32[16,640]{1,0:T(8,128)S(1)}, u32[]{:S(2)}, u32[]{:S(2)}) %collective-permute-start.1) | collective-permute-done | bytes 40992 | tf_op jit(solution)/shard_map/ppermute | solution.py:344
  9.3 1.3 %collective-permute-done.2.refs_3_ = f32[16,640]{1,0:T(8,128)S(1)} collective-permute-done((f32[16,640]{1,0:T(8,128)}, f32[16,640]{1,0:T(8,128)S(1)}, u32[]{:S(2)}, u32[]{:S(2)}) %collective-permute-start.2) | collective-permute-done | bytes 40992 | tf_op jit(solution)/shard_map/ppermute | solution.py:344
  10.6 0.0 copy-done.5
  10.6 0.0 copy-done.6
  10.6 0.6 %copy-done.7 = f32[16,640]{1,0:T(8,128)} copy-done((f32[16,640]{1,0:T(8,128)}, f32[16,640]{1,0:T(8,128)S(1)}, u32[]{:S(2)}) %copy-start.7) | copy-done | bytes 40984
  11.2 1.7 %filter_slots.1 = f32[24,640]{1,0:T(8,128)} custom-call(f32[16,64]{1,0:T(8,128)} %divide_subtract_fusion.h_ref, f32[16,640]{1,0:T(8,128)} %get-tuple-element.7.refs_0_, f32[16,640]{1,0:T(8,128)} %copy-done.5, f32[16,640]{1,0:T(8,128)} %copy-done.6, f32[16,640]{1,0:T(8,128)} %copy-done.7, f32[8,640]{1,0:T(8,128)} %get-tuple-element.8.refs_4_.mine_ref), custom_call_target="tpu_custom_call" | custom-call | tf_op jit(solution)/shard_map/filter_slots/pallas_call | solution.py:382
  12.9 2.6 %collective-permute-start.3 = (f32[1,24,640]{2,1,0:T(8,128)}, f32[1,24,640]{2,1,0:T(8,128)S(1)}, u32[]{:S(2)}, u32[]{:S(2)}) collective-permute-start(f32[1,24,640]{2,1,0:T(8,128)} %bitcast.5), channel_id=1, source_target_pairs={{0,16},{4,20},{8,24},{12,28},{16,0},{20,4},{24,8},{28,12},{1,17},{... | collective-permute-start | bytes 184328 | tf_op jit(solution)/shard_map/ppermute | solution.py:344
  15.5 4.0 %collective-permute-done.3 = f32[1,24,640]{2,1,0:T(8,128)S(1)} collective-permute-done((f32[1,24,640]{2,1,0:T(8,128)}, f32[1,24,640]{2,1,0:T(8,128)S(1)}, u32[]{:S(2)}, u32[]{:S(2)}) %collective-permute-start.3) | collective-permute-done | bytes 61472 | tf_op jit(solution)/shard_map/ppermute | solution.py:344
  19.5 0.8 %pad_maximum_fusion = f32[2,24,640]{2,1,0:T(8,128)S(1)} fusion(f32[1,24,640]{2,1,0:T(8,128)S(1)} %collective-permute-done.3, f32[1,24,640]{2,1,0:T(8,128)} %bitcast.6), kind=kLoop, calls=%fused_computation | loop fusion | flops 30720 | bytes 245760 | tf_op jit(solution)/shard_map/concatenate | solution.py:392
  20.4 1.6 %collective-permute-start.4 = (f32[2,24,640]{2,1,0:T(8,128)S(1)}, f32[2,24,640]{2,1,0:T(8,128)S(1)}, u32[]{:S(2)}, u32[]{:S(2)}) collective-permute-start(f32[2,24,640]{2,1,0:T(8,128)S(1)} %pad_maximum_fusion), channel_id=1, source_target_pairs={{0,4},{4,0},{8,12},{12,8},{16,20},{20,16},{24,28},{28,24},{1,5},{5... | collective-permute-start | bytes 368648 | tf_op jit(solution)/shard_map/ppermute | solution.py:344
  22.0 0.0 copy-done.4
  22.0 0.7 %collective-permute-start.5 = (f32[2,24,640]{2,1,0:T(8,128)S(1)}, f32[2,24,640]{2,1,0:T(8,128)S(1)}, u32[]{:S(2)}, u32[]{:S(2)}) collective-permute-start(f32[2,24,640]{2,1,0:T(8,128)S(1)} %pad_maximum_fusion), channel_id=1, source_target_pairs={{0,8},{4,12},{8,0},{12,4},{16,24},{20,28},{24,16},{28,20},{1,9},{5... | collective-permute-start | bytes 368648 | tf_op jit(solution)/shard_map/ppermute | solution.py:344
  22.7 1.4 %collective-permute-start.6 = (f32[2,24,640]{2,1,0:T(8,128)S(1)}, f32[2,24,640]{2,1,0:T(8,128)S(1)}, u32[]{:S(2)}, u32[]{:S(2)}) collective-permute-start(f32[2,24,640]{2,1,0:T(8,128)S(1)} %pad_maximum_fusion), channel_id=1, source_target_pairs={{0,12},{4,8},{8,4},{12,0},{16,28},{20,24},{24,20},{28,16},{1,13},{... | collective-permute-start | bytes 368648 | tf_op jit(solution)/shard_map/ppermute | solution.py:344
  24.0 1.7 %collective-permute-done.4 = f32[2,24,640]{2,1,0:T(8,128)S(1)} collective-permute-done((f32[2,24,640]{2,1,0:T(8,128)S(1)}, f32[2,24,640]{2,1,0:T(8,128)S(1)}, u32[]{:S(2)}, u32[]{:S(2)}) %collective-permute-start.4) | collective-permute-done | bytes 122912 | tf_op jit(solution)/shard_map/ppermute | solution.py:344
  25.7 1.5 %collective-permute-done.5 = f32[2,24,640]{2,1,0:T(8,128)S(1)} collective-permute-done((f32[2,24,640]{2,1,0:T(8,128)S(1)}, f32[2,24,640]{2,1,0:T(8,128)S(1)}, u32[]{:S(2)}, u32[]{:S(2)}) %collective-permute-start.5) | collective-permute-done | bytes 122912 | tf_op jit(solution)/shard_map/ppermute | solution.py:344
  27.3 0.0 copy-start
  27.3 0.0 copy-start.1
  27.3 2.2 %collective-permute-done.6 = f32[2,24,640]{2,1,0:T(8,128)S(1)} collective-permute-done((f32[2,24,640]{2,1,0:T(8,128)S(1)}, f32[2,24,640]{2,1,0:T(8,128)S(1)}, u32[]{:S(2)}, u32[]{:S(2)}) %collective-permute-start.6) | collective-permute-done | bytes 122912 | tf_op jit(solution)/shard_map/ppermute | solution.py:344
  29.5 0.0 copy-start.3
  29.5 0.6 %copy-done.2 = s32[8,128]{1,0:T(8,128)S(1)} copy-done((s32[8,128]{1,0:T(8,128)S(1)}, s32[8,128]{1,0:T(8,128)}, u32[]{:S(2)}) %copy-start.2) | copy-done | bytes 4120
  30.2 0.0 copy-done.3
  30.2 8.8 %screen_and_residual.1 = (f32[16,8,1024]{2,1,0:T(8,128)}, f32[16,1024]{1,0:T(8,128)}) custom-call(s32[1]{0:T(128)} %bitcast.me_ref, s32[1,8]{1,0:T(1,128)S(1)} %copy-done.3, s32[8,128]{1,0:T(8,128)S(1)} %copy-done.2, f32[8,24,640]{2,1,0:T(8,128)S(1)} %constant_dynamic-update-slice_fusion.all_ref, f32[8,640]{1,0:T(8,128)S(1)} %copy-done, f32[16,640]{1,0:T(8,128)S(1)} %copy-done.1), custom_call_target="tpu_custom_call" | custom-call | tf_op jit(solution)/shard_map/screen_and_residual/pallas_call | solution.py:400
  (15 shorter events, 0.1 us)
Async XLA Ops:
  3.9 4.7 %collective-permute-start = (f32[16,640]{1,0:T(8,128)}, f32[16,640]{1,0:T(8,128)S(1)}, u32[]{:S(2)}, u32[]{:S(2)}) collective-permute-start(f32[16,640]{1,0:T(8,128)} %get-tuple-element.7.refs_0_), channel_id=1, source_target_pairs={{0,1},{1,0},{2,3},{3,2},{4,5},{5,4},{6,7},{7,6},{8,9},{9,8},{10,11... | collective-permute-start | bytes 122888 | tf_op jit(solution)/shard_map/ppermute | solution.py:344
  4.4 4.9 %collective-permute-start.1 = (f32[16,640]{1,0:T(8,128)}, f32[16,640]{1,0:T(8,128)S(1)}, u32[]{:S(2)}, u32[]{:S(2)}) collective-permute-start(f32[16,640]{1,0:T(8,128)} %get-tuple-element.7.refs_0_), channel_id=1, source_target_pairs={{0,2},{1,3},{2,0},{3,1},{4,6},{5,7},{6,4},{7,5},{8,10},{9,11},{10,... | collective-permute-start | bytes 122888 | tf_op jit(solution)/shard_map/ppermute | solution.py:344
  6.9 3.7 %collective-permute-start.2 = (f32[16,640]{1,0:T(8,128)}, f32[16,640]{1,0:T(8,128)S(1)}, u32[]{:S(2)}, u32[]{:S(2)}) collective-permute-start(f32[16,640]{1,0:T(8,128)} %get-tuple-element.7.refs_0_), channel_id=1, source_target_pairs={{0,3},{1,2},{2,1},{3,0},{4,7},{5,6},{6,5},{7,4},{8,11},{9,10},{10,... | collective-permute-start | bytes 122888 | tf_op jit(solution)/shard_map/ppermute | solution.py:344
  7.2 0.7 %copy-start.8 = (s32[64]{0:T(128)S(1)}, s32[64]{0:T(128)}, u32[]{:S(2)}) copy-start(s32[64]{0:T(128)} %param.11) | copy-start | bytes 772
  8.6 2.0 %copy-start.5 = (f32[16,640]{1,0:T(8,128)}, f32[16,640]{1,0:T(8,128)S(1)}, u32[]{:S(2)}) copy-start(f32[16,640]{1,0:T(8,128)S(1)} %collective-permute-done.refs_1_) | copy-start | bytes 122884
  9.3 1.3 %copy-start.6 = (f32[16,640]{1,0:T(8,128)}, f32[16,640]{1,0:T(8,128)S(1)}, u32[]{:S(2)}) copy-start(f32[16,640]{1,0:T(8,128)S(1)} %collective-permute-done.1.refs_2_) | copy-start | bytes 122884
  10.6 0.6 %copy-start.7 = (f32[16,640]{1,0:T(8,128)}, f32[16,640]{1,0:T(8,128)S(1)}, u32[]{:S(2)}) copy-start(f32[16,640]{1,0:T(8,128)S(1)} %collective-permute-done.2.refs_3_) | copy-start | bytes 122884
  12.9 6.6 %collective-permute-start.3 = (f32[1,24,640]{2,1,0:T(8,128)}, f32[1,24,640]{2,1,0:T(8,128)S(1)}, u32[]{:S(2)}, u32[]{:S(2)}) collective-permute-start(f32[1,24,640]{2,1,0:T(8,128)} %bitcast.5), channel_id=1, source_target_pairs={{0,16},{4,20},{8,24},{12,28},{16,0},{20,4},{24,8},{28,12},{1,17},{... | collective-permute-start | bytes 184328 | tf_op jit(solution)/shard_map/ppermute | solution.py:344
  15.5 6.5 %copy-start.4 = (f32[24,640]{1,0:T(8,128)S(1)}, f32[24,640]{1,0:T(8,128)}, u32[]{:S(2)}) copy-start(f32[24,640]{1,0:T(8,128)} %filter_slots.1) | copy-start | bytes 184324
  20.4 5.3 %collective-permute-start.4 = (f32[2,24,640]{2,1,0:T(8,128)S(1)}, f32[2,24,640]{2,1,0:T(8,128)S(1)}, u32[]{:S(2)}, u32[]{:S(2)}) collective-permute-start(f32[2,24,640]{2,1,0:T(8,128)S(1)} %pad_maximum_fusion), channel_id=1, source_target_pairs={{0,4},{4,0},{8,12},{12,8},{16,20},{20,16},{24,28},{28,24},{1,5},{5... | collective-permute-start | bytes 368648 | tf_op jit(solution)/shard_map/ppermute | solution.py:344
  22.0 5.3 %collective-permute-start.5 = (f32[2,24,640]{2,1,0:T(8,128)S(1)}, f32[2,24,640]{2,1,0:T(8,128)S(1)}, u32[]{:S(2)}, u32[]{:S(2)}) collective-permute-start(f32[2,24,640]{2,1,0:T(8,128)S(1)} %pad_maximum_fusion), channel_id=1, source_target_pairs={{0,8},{4,12},{8,0},{12,4},{16,24},{20,28},{24,16},{28,20},{1,9},{5... | collective-permute-start | bytes 368648 | tf_op jit(solution)/shard_map/ppermute | solution.py:344
  22.7 6.8 %collective-permute-start.6 = (f32[2,24,640]{2,1,0:T(8,128)S(1)}, f32[2,24,640]{2,1,0:T(8,128)S(1)}, u32[]{:S(2)}, u32[]{:S(2)}) collective-permute-start(f32[2,24,640]{2,1,0:T(8,128)S(1)} %pad_maximum_fusion), channel_id=1, source_target_pairs={{0,12},{4,8},{8,4},{12,0},{16,28},{20,24},{24,20},{28,16},{1,13},{... | collective-permute-start | bytes 368648 | tf_op jit(solution)/shard_map/ppermute | solution.py:344
  27.3 2.2 %copy-start = (f32[8,640]{1,0:T(8,128)S(1)}, f32[8,640]{1,0:T(8,128)}, u32[]{:S(2)}) copy-start(f32[8,640]{1,0:T(8,128)} %get-tuple-element.8.refs_4_.mine_ref) | copy-start | bytes 61444
  27.3 2.2 %copy-start.1 = (f32[16,640]{1,0:T(8,128)S(1)}, f32[16,640]{1,0:T(8,128)}, u32[]{:S(2)}) copy-start(f32[16,640]{1,0:T(8,128)} %get-tuple-element.9.own_ref) | copy-start | bytes 122884
  29.5 0.7 %copy-start.2 = (s32[8,128]{1,0:T(8,128)S(1)}, s32[8,128]{1,0:T(8,128)}, u32[]{:S(2)}) copy-start(s32[8,128]{1,0:T(8,128)} %list_ref.3) | copy-start | bytes 12292
  29.5 0.7 %copy-start.3 = (s32[1,8]{1,0:T(1,128)S(1)}, s32[1,8]{1,0:T(1,128)}, u32[]{:S(2)}) copy-start(s32[1,8]{1,0:T(1,128)} %counts_ref.3) | copy-start | bytes 100

commit v2 on v1

--- a/solution.py
+++ b/solution.py
@@ -159,11 +159,15 @@
     )
 
 
+MAX_BLOCKS = 8
 LO = 512
+STEP = 8
 
 
 def gather_kernel(n_tile, counts_ref, list_ref, phases_ref, coh_ref, pix_ref, out_ref, own_ref, wg_ref):
     acq_loc, local = phases_ref.shape
+    pieces = local // LO
+    step = min(STEP, pieces)
     index, tile, live = packed_rows(counts_ref, list_ref, n_tile)
     packed = index.shape[1]
     low = index & (LANES - 1)
@@ -190,15 +194,15 @@
 
     weight = (pick(0) + pick(1)) * live
     pixel = pick(2) * 64.0 + pick(3) + tile.astype(jnp.float32) * float(SLAB_PIX)
-    sub = lax.broadcasted_iota(jnp.int32, (8, packed), 0)
-    wg_ref[...] = jnp.where(sub == 0, weight, jnp.where(sub == 1, pixel, 0.0))
+    for b in range(packed // LANES):
+        cut = slice(b * LANES, (b + 1) * LANES)
+        wg_ref[b : b + 1, :] = weight[:, cut]
+        wg_ref[MAX_BLOCKS + b : MAX_BLOCKS + b + 1, :] = pixel[:, cut]
     low = index & (LO - 1)
     high = index >> 9
     chosen = (lax.broadcasted_iota(jnp.int32, (LO, packed), 0) == low)
     chosen = chosen.astype(jnp.float32).astype(jnp.bfloat16)
     own = jnp.zeros((acq_loc, packed), jnp.float32)
-    pieces = local // LO
-    step = 8
     for start in range(0, pieces, step):
         block = jnp.concatenate(
             [phases_ref[:, h * LO : (h + 1) * LO] for h in range(start, start + step)], 0
@@ -213,16 +217,16 @@
 
 def filter_kernel(h_ref, *refs):
     *parts, wg_ref, out_ref = refs
-    acq_loc = parts[0].shape[0]
+    packed = parts[0].shape[1]
     series = jnp.concatenate([part[...] for part in parts], 0)
-    out_ref[0:acq_loc, :] = lax.dot_general(
+    out_ref[:, 0:packed] = lax.dot_general(
         h_ref[...],
         series,
         (NN, ((), ())),
         precision=lax.Precision.HIGHEST,
         preferred_element_type=jnp.float32,
     )
-    out_ref[acq_loc:, :] = wg_ref[...]
+    out_ref[:, packed:] = wg_ref[...]
 
 
 def first_pair(tile, n_pair):
@@ -231,6 +235,10 @@
 
 def hat(distance):
     return jnp.maximum(float(RADIUS + 1) - jnp.abs(distance), 0.0)
+
+
+def hat_bf16(distance):
+    return jnp.maximum(jnp.bfloat16(RADIUS + 1) - jnp.abs(distance), jnp.bfloat16(0))
 
 
 def split_pixel(pixel):
@@ -238,58 +246,17 @@
     return (whole >> 10).astype(jnp.float32), (whole & (COLS - 1)).astype(jnp.float32)
 
 
-def screen_kernel(
-    n_tile, me_ref, counts_ref, list_ref, all_ref, mine_ref, own_ref, screen_ref, residual_ref,
-    lhs_ref, col_ref, pair_ref, res_ref,
-):
-    n_src, rows, packed = all_ref.shape
-    acq_loc = own_ref.shape[0]
+def rows_of_bf16(row, count):
+    few = jnp.broadcast_to(row, (16, row.shape[1])).astype(jnp.bfloat16)
+    return jnp.concatenate([few] * (count // 16), 0)
+
+
+CHUNK = 256
+
+
+def slot_groups(n_tile, counts_ref):
     n_pair = n_tile // 2
-    width = 3 * LANES
-    limit = min_weight * float((RADIUS + 1) ** 4)
-    me = me_ref[0]
     first, last = heavy_tiles(counts_ref, n_tile)
-
-    def blocks(src, pair):
-        start = pl.multiple_of(pair * LANES, LANES)
-        return jnp.concatenate(
-            [
-                all_ref[src, :, pl.ds(start, LANES)],
-                all_ref[src, :, pl.ds(pl.multiple_of(start + LANES, LANES), LANES)],
-                all_ref[src, :, packed - LANES :],
-            ],
-            1,
-        )
-
-    top = (me * ROWS_DEV).astype(jnp.float32)
-    row_at = lax.broadcasted_iota(jnp.int32, (ROWS_DEV, width), 0).astype(jnp.float32) + top
-    col_at = lax.broadcasted_iota(jnp.int32, (COLS, width), 0).astype(jnp.float32)
-    pair = first_pair(me, n_pair)
-    n_lhs = (acq_loc + 1) * ROWS_DEV
-    for src in range(n_src):
-        data = blocks(src, pair)
-        row, col = split_pixel(data[acq_loc + 1 : acq_loc + 2])
-        across = hat(row_at - row)
-        lanes = pl.ds(src * width, width)
-        part = jnp.concatenate([across * data[a : a + 1] for a in range(acq_loc + 1)], 0)
-        part_hi, part_lo = split_bf16(part)
-        lhs_ref[0:n_lhs, lanes] = part_hi
-        lhs_ref[n_lhs : 2 * n_lhs, lanes] = part_lo
-        col_ref[:, lanes] = hat(col_at - col).astype(jnp.bfloat16)
-    for c in range(0, COLS, 256):
-        image = dot_f32(lhs_ref[...], col_ref[c : c + 256, :], NT)
-        image = image[0:n_lhs] + image[n_lhs:]
-        below = jnp.maximum(image[acq_loc * ROWS_DEV :], limit)
-        for a in range(acq_loc):
-            screen_ref[a, :, c : c + 256] = image[a * ROWS_DEV : (a + 1) * ROWS_DEV] / below
-
-    mine = mine_ref[...]
-    my_row, my_col = split_pixel(mine[1:2])
-
-    def down(row, block):
-        spread = jnp.broadcast_to(row[:, block * LANES : (block + 1) * LANES], (LANES, LANES))
-        return jnp.transpose(spread)
-
     groups = []
     for t in range(n_tile):
         p = min(max((t + 1) // 2 - 1, 0), max(n_pair - 2, 0))
@@ -300,33 +267,135 @@
     base = n_pair * LANES
     groups.append([base, HALF, first_pair(first, n_pair)])
     groups.append([base + HALF, HALF, first_pair(last, n_pair)])
-    rows_down = jnp.concatenate([down(my_row, b) for b in range(n_pair + 1)], 0)
-    cols_down = jnp.concatenate([down(my_col, b) for b in range(n_pair + 1)], 0)
-    samples = []
-    for start, size, p in groups:
+    return groups
+
+
+def screen_kernel(n_tile, begins, ends, *refs):
+    me_ref, counts_ref, all_ref, mine_ref = refs[:4]
+    refs = refs[4:]
+    if not begins:
+        image_in, samples_in = refs[:2]
+        refs = refs[2:]
+    if ends:
+        own_ref, screen_ref, residual_ref = refs[:3]
+        refs = refs[3:]
+    else:
+        image_out, samples_out = refs[:2]
+        refs = refs[2:]
+    tag_ref, value_ref, lhs_ref, col_ref, pair_ref, res_ref = refs
+    n_src, acq_loc, packed = all_ref.shape
+    packed -= LANES
+    n_pair = n_tile // 2
+    width = 3 * LANES
+    limit = min_weight * float((RADIUS + 1) ** 4)
+    me = me_ref[0]
+    f32, bf16 = jnp.float32, jnp.bfloat16
+
+    def starts(pair):
+        start = pl.multiple_of(pair * LANES, LANES)
+        return [start, pl.multiple_of(start + LANES, LANES), n_pair * LANES]
+
+    def tags(src, pair):
+        blocks = [tag_ref[src, 0:3, pl.ds(s, LANES)] for s in starts(pair)]
+        every = jnp.concatenate(blocks, 1)
+        return every[0:1], every[1:2], every[2:3]
+
+    sub = lax.broadcasted_iota(jnp.int32, (16, LANES), 0)
+    for src in range(n_src):
+        value_hi, value_lo = split_bf16(all_ref[src, :, 0:packed])
+        value_ref[src, 0:acq_loc, :] = value_hi
+        value_ref[src, acq_loc : 2 * acq_loc, :] = value_lo
+        for b in range(n_pair + 1):
+            lanes = slice(b * LANES, (b + 1) * LANES)
+            row, col = split_pixel(all_ref[src, MAX_BLOCKS + b : MAX_BLOCKS + b + 1, packed:])
+            weight = all_ref[src, b : b + 1, packed:]
+            tag_ref[src, 0:1, lanes] = weight
+            tag_ref[src, 1:2, lanes] = row
+            tag_ref[src, 2:3, lanes] = col
+            w_hi = weight.astype(bf16).astype(f32)
+            both = jnp.where(sub == 0, w_hi, jnp.where(sub == 1, weight - w_hi, 0.0))
+            value_ref[src, 2 * acq_loc :, lanes] = both.astype(bf16)
+
+    top = (me * ROWS_DEV).astype(f32)
+    row_at = lax.broadcasted_iota(jnp.int32, (ROWS_DEV, width), 0).astype(f32) + top
+    col_at = lax.broadcasted_iota(jnp.int32, (CHUNK, width), 0) - CHUNK // 2
+    col_at = col_at.astype(f32).astype(bf16)
+    pair = first_pair(me, n_pair)
+    n_img = acq_loc * ROWS_DEV
+    for src in range(n_src):
+        weight, row, col = tags(src, pair)
+        across = hat(row_at - row)
+        lanes = slice(src * width, (src + 1) * width)
+        data = jnp.concatenate([all_ref[src, :, pl.ds(s, LANES)] for s in starts(pair)], 1)
+        part = jnp.concatenate([across * data[a : a + 1] for a in range(acq_loc)], 0)
+        part_hi, part_lo = split_bf16(part)
+        lhs_ref[0:n_img, lanes] = part_hi
+        lhs_ref[n_img : 2 * n_img, lanes] = part_lo
+        w_part = across * weight
+        w_hi = w_part.astype(bf16).astype(f32)
+        lhs_ref[2 * n_img :, lanes] = jnp.concatenate([w_hi, w_part - w_hi], 0).astype(bf16)
+        for c in range(0, COLS, CHUNK):
+            near = jnp.clip(col - float(c + CHUNK // 2), -160.0, 160.0)
+            col_ref[c : c + CHUNK, lanes] = hat_bf16(col_at - rows_of_bf16(near, CHUNK))
+
+    def down_lanes(row):
+        return jnp.transpose(jnp.broadcast_to(row, (LANES, LANES)))
+
+    mine = [split_pixel(mine_ref[MAX_BLOCKS + b : MAX_BLOCKS + b + 1, :]) for b in range(n_pair + 1)]
+    rows_down = jnp.concatenate([down_lanes(r) for r, _ in mine], 0).astype(bf16)
+    cols_down = jnp.concatenate([down_lanes(c) for _, c in mine], 0)
+
+    def sample(start, size, p):
         r_i = rows_down[start : start + size]
         c_i = cols_down[start : start + size]
         values = []
         for src in range(n_src):
-            data = blocks(src, p)
-            row, col = split_pixel(data[acq_loc + 1 : acq_loc + 2])
-            value_hi, value_lo = split_bf16(data[0 : acq_loc + 8])
-            values.append(jnp.concatenate([value_hi, value_lo], 0))
-            for b in range(3):
+            _, row, col = tags(src, p)
+            for b, s in enumerate(starts(p)):
                 cut = slice(b * LANES, (b + 1) * LANES)
-                both = hat(r_i - row[:, cut]) * hat(c_i - col[:, cut])
-                pair_ref[0:size, src * width + b * LANES : src * width + (b + 1) * LANES] = (
-                    both.astype(jnp.bfloat16)
-                )
-        value = jnp.concatenate(values, 1)
-        got = dot_f32(value, pair_ref[0:size, :], NT)
-        got = got[0 : acq_loc + 8] + got[acq_loc + 8 :]
-        samples.append(got[0:acq_loc] / jnp.maximum(got[acq_loc : acq_loc + 1], limit))
-    res_ref[...] = own_ref[...] - jnp.concatenate(samples, 1)
-
+                values.append(value_ref[src, :, pl.ds(s, LANES)])
+                over = hat_bf16(r_i - rows_of_bf16(row[:, cut], size))
+                both = over * hat_bf16((c_i - col[:, cut]).astype(bf16))
+                at = src * width + b * LANES
+                pair_ref[start : start + size, at : at + LANES] = both
+        got = dot_f32(jnp.concatenate(values, 1), pair_ref[start : start + size, :], NT)
+        total = got[0:acq_loc] + got[acq_loc : 2 * acq_loc]
+        below = got[2 * acq_loc : 2 * acq_loc + 8]
+        return jnp.concatenate([total, below], 0)
+
+    def slab(c):
+        got = dot_f32(lhs_ref[...], col_ref[c : c + CHUNK, :], NT)
+        return jnp.concatenate(
+            [
+                got[0:n_img] + got[n_img : 2 * n_img],
+                got[2 * n_img : 2 * n_img + ROWS_DEV] + got[2 * n_img + ROWS_DEV :],
+            ],
+            0,
+        )
+
+    for c in range(0, COLS, CHUNK):
+        image = slab(c)
+        if not begins:
+            image = image + image_in[:, c : c + CHUNK]
+        if not ends:
+            image_out[:, c : c + CHUNK] = image
+            continue
+        below = jnp.maximum(image[n_img:], limit)
+        for a in range(acq_loc):
+            screen_ref[a, :, c : c + CHUNK] = image[a * ROWS_DEV : (a + 1) * ROWS_DEV] / below
+    samples = jnp.concatenate([sample(*group) for group in slot_groups(n_tile, counts_ref)], 1)
+    if not begins:
+        samples = samples + samples_in[...]
+    if not ends:
+        samples_out[...] = samples
+        return
+    below = samples[acq_loc : acq_loc + 1] + samples[acq_loc + 1 : acq_loc + 2]
+    res_ref[...] = own_ref[...] - samples[0:acq_loc] / jnp.maximum(below, limit)
+
+    first, _ = heavy_tiles(counts_ref, n_tile)
     lane = lax.broadcasted_iota(jnp.int32, (1, LANES), 1)
     lower = lane < HALF
-    heavy = res_ref[:, base:]
+    heavy = res_ref[:, n_pair * LANES :]
     turned = pltpu.roll(heavy, HALF, 1)
     for t in range(n_tile):
         near = res_ref[:, (t // 2) * LANES : (t // 2 + 1) * LANES]
@@ -337,6 +406,47 @@
         residual_ref[:, t * LANES : (t + 1) * LANES] = jnp.where(
             lane < counts_ref[0, t], both, 0.0
         )
+
+
+def add_sources(n_tile, me, counts, sources, mine, sums, own):
+    n_src, acq_loc, packed = sources.shape
+    packed -= LANES
+    width = n_src * 3 * LANES
+    f32, bf16 = jnp.float32, jnp.bfloat16
+    smem = pl.BlockSpec(memory_space=pltpu.SMEM)
+    vmem = pl.BlockSpec(memory_space=pltpu.VMEM)
+    n_lhs = 2 * (acq_loc + 1) * ROWS_DEV
+    begins, ends = sums is None, own is not None
+    args = [me, counts, sources, mine]
+    if not begins:
+        args += list(sums)
+    if ends:
+        args.append(own)
+        shapes = ((acq_loc, ROWS_DEV, COLS), (acq_loc, n_tile * LANES))
+    else:
+        shapes = ((n_lhs // 2, COLS), (acq_loc + 8, packed))
+    macs = width * (n_lhs * COLS + (2 * acq_loc + 16) * packed)
+    return pl.pallas_call(
+        functools.partial(screen_kernel, n_tile, begins, ends),
+        out_shape=tuple(jax.ShapeDtypeStruct(shape, f32) for shape in shapes),
+        in_specs=[smem, smem] + [vmem] * (len(args) - 2),
+        out_specs=(vmem, vmem),
+        scratch_shapes=[
+            pltpu.VMEM((n_src, 8, packed), f32),
+            pltpu.VMEM((n_src, 2 * acq_loc + 16, packed), bf16),
+            pltpu.VMEM((n_lhs, width), bf16),
+            pltpu.VMEM((COLS, width), bf16),
+            pltpu.VMEM((packed, width), bf16),
+            pltpu.VMEM((acq_loc, packed), f32),
+        ],
+        input_output_aliases={} if begins or ends else {4: 0, 5: 1},
+        cost_estimate=pl.CostEstimate(flops=2 * macs, bytes_accessed=1 << 20, transcendentals=0),
+        compiler_params=pltpu.CompilerParams(vmem_limit_bytes=SCREEN_VMEM),
+        name="add_sources",
+    )(*args)
+
+
+SCREEN_VMEM = 24 << 20
 
 
 def xor_permute(x, axis, mask):
@@ -357,10 +467,11 @@
         out_shape=(
             jax.ShapeDtypeStruct((acq_loc, packed), f32),
             jax.ShapeDtypeStruct((acq_loc, packed), f32),
-            jax.ShapeDtypeStruct((8, packed), f32),
+            jax.ShapeDtypeStruct((2 * MAX_BLOCKS, LANES), f32),
         ),
         in_specs=[smem, vmem, vmem, vmem, vmem],
         out_specs=(vmem, vmem, vmem),
+        compiler_params=pltpu.CompilerParams(vmem_limit_bytes=56 << 20),
         name="gather_slots",
     )(
         counts,
@@ -381,39 +492,20 @@
     highpass = (column == row[:, None]).astype(f32) - inside / (upper - lower + 1).astype(f32)
     filtered = pl.pallas_call(
         filter_kernel,
-        out_shape=jax.ShapeDtypeStruct((acq_loc + 8, packed), f32),
+        out_shape=jax.ShapeDtypeStruct((acq_loc, packed + LANES), f32),
         in_specs=[vmem] * (n_acq + 2),
         out_specs=vmem,
+        compiler_params=pltpu.CompilerParams(vmem_limit_bytes=4 << 20),
         name="filter_slots",
     )(highpass, *parts, wg)
-    held = filtered[None]
+    me = lax.axis_index("tile").astype(jnp.int32).reshape(1)
     half = n_tile // 2
-    if half > 1:
-        held = jnp.concatenate([held, xor_permute(held, "tile", half)], 0)
-        held = jnp.concatenate([held] + [xor_permute(held, "tile", k) for k in range(1, half)], 0)
-    else:
-        held = jnp.concatenate([held, xor_permute(held, "tile", 1)], 0)
-    me = lax.axis_index("tile").astype(jnp.int32).reshape(1)
-    n_src = n_tile
-    n_lhs = 2 * (acq_loc + 1) * ROWS_DEV
-    width = n_src * 3 * LANES
-    screen, residual = pl.pallas_call(
-        functools.partial(screen_kernel, n_tile),
-        out_shape=(
-            jax.ShapeDtypeStruct((acq_loc, ROWS_DEV, COLS), f32),
-            jax.ShapeDtypeStruct((acq_loc, n_tile * LANES), f32),
-        ),
-        in_specs=[smem, smem, vmem, vmem, vmem, vmem],
-        out_specs=(vmem, vmem),
-        scratch_shapes=[
-            pltpu.VMEM((n_lhs, width), jnp.bfloat16),
-            pltpu.VMEM((COLS, width), jnp.bfloat16),
-            pltpu.VMEM((3 * HALF, width), jnp.bfloat16),
-            pltpu.VMEM((acq_loc, packed), f32),
-        ],
-        compiler_params=pltpu.CompilerParams(vmem_limit_bytes=48 << 20),
-        name="screen_and_residual",
-    )(me, counts, send_list, held, wg, own)
+    held = jnp.stack([filtered, xor_permute(filtered, "tile", half)])
+    others = [xor_permute(held, "tile", k) for k in range(1, half)]
+    sums = None
+    for sources in [held] + others[:-1]:
+        sums = add_sources(n_tile, me, counts, sources, wg, sums, None)
+    screen, residual = add_sources(n_tile, me, counts, others[-1], wg, sums, own)
     return residual, screen
 
 

time: 39.2 us -> 29.9 us (0.76)
  waiting for transfers between devices: 11.5 us -> 6.78 us
  Pallas kernels: 13.7 us -> 11.8 us
  other arithmetic: 1.67 us -> 0.24 us
  local copies, waits for them, and re-layouts: 2.05 us -> 0.8 us
    ppermute x7, waiting for transfers between devices: 11.5 us -> 6.78 us  [xor_permute(): return lax.ppermute(x, axis, [(i, i ^ mask) for i in range(count)])]
    pallas_call x2 -> x5, Pallas kernels: 10.4 us -> 8.55 us  [the longest x4 8.38 us: add_sources(): pl.pallas_call(functools.partial(screen_kernel, n_tile, begins, ends), ou...]
    unnamed x22 -> x12, local copies, waits for them, and re-layouts: 1.95 us -> 0.72 us
    concatenate x1 -> x0, other arithmetic: 0.84 us -> none  [gathered_shards(): held = jnp.concatenate([held, xor_permute(held, 'tile', half)], 0)]
    sub x1, other arithmetic: 0.67 us -> 0.08 us  [gathered_shards(): (column == row[:, None]).astype(f32)]
  transfers between devices with their start and end apart: 7 -> 7, of which waited for: 6 -> 3; matrix products, arithmetic and copies ran while one was open for 2% -> 1% of each run, Pallas kernels for 0% -> 19%
where the time goes in v2:
time: 29.9 us; the launch traced here: 29.7 us
  Pallas kernels  11.8 us (39%)
  starting transfers between devices  9.28 us (31%)
  waiting for transfers between devices  6.78 us (23%)
  local copies, waits for them, and re-layouts  0.8 us (3%)
  between operations  0.73 us (2%)
    ppermute x7, starting transfers between devices, xor_permute(): return lax.ppermute(x, axis, [(i, i ^ mask) for i in range(count)])  9.28 us
    pallas_call x4, Pallas kernels, add_sources(): pl.pallas_call(functools.partial(screen_kernel, n_tile, begins, ends), ou...  8.38 us
    ppermute x7, waiting for transfers between devices, xor_permute(): return lax.ppermute(x, axis, [(i, i ^ mask) for i in range(count)])  6.78 us
    pallas_call x1, Pallas kernels, gathered_shards(): pl.pallas_call(functools.partial(gather_kernel, n_tile), out_shape=(jax.S...  3.26 us
    unnamed x12, local copies, waits for them, and re-layouts  0.72 us
  transfers between devices with their start and end apart: 7, of which 3 were waited for; matrix products, arithmetic and copies ran while one was open for 1% of the time, Pallas kernels for 19%

profile of v2, /device:TPU:0, one launch (start us, length us, event | category | flops | bytes accessed | tf_op | source)
XLA Modules:
  0.0 29.7 jit_solution(7175027876727547652)
XLA Ops:
  0.6 0.0 copy-start.5
  0.6 3.3 %gather_slots.1 = (f32[16,640]{1,0:T(8,128)}, f32[16,640]{1,0:T(8,128)}, f32[16,128]{1,0:T(8,128)}) custom-call(s32[1,8]{1,0:T(1,128)} %refs_1_.7, s32[8,128]{1,0:T(8,128)} %list_ref.1, f32[16,16384]{1,0:T(8,128)} %phases_ref.1, f32[128,128]{1,0:T(8,128)} %bitcast.6, s32[128,128]{1,0:T(8,128)} %bitcast.7), custom_call_target="tpu_custom_call" | custom-call | tf_op jit(solution)/shard_map/gather_slots/pallas_call | solution.py:465
  3.9 0.5 %collective-permute-start = (f32[16,640]{1,0:T(8,128)}, f32[16,640]{1,0:T(8,128)S(1)}, u32[]{:S(2)}, u32[]{:S(2)}) collective-permute-start(f32[16,640]{1,0:T(8,128)} %get-tuple-element.13.refs_0_), channel_id=1, source_target_pairs={{0,1},{1,0},{2,3},{3,2},{4,5},{5,4},{6,7},{7,6},{8,9},{9,8},{10,11... | collective-permute-start | bytes 122888 | tf_op jit(solution)/shard_map/ppermute | solution.py:454
  4.4 2.6 %collective-permute-start.1 = (f32[16,640]{1,0:T(8,128)}, f32[16,640]{1,0:T(8,128)S(1)}, u32[]{:S(2)}, u32[]{:S(2)}) collective-permute-start(f32[16,640]{1,0:T(8,128)} %get-tuple-element.13.refs_0_), channel_id=1, source_target_pairs={{0,2},{1,3},{2,0},{3,1},{4,6},{5,7},{6,4},{7,5},{8,10},{9,11},{10,... | collective-permute-start | bytes 122888 | tf_op jit(solution)/shard_map/ppermute | solution.py:454
  6.9 0.1 collective-permute-start.2
  7.0 0.1 iota_add_fusion
  7.1 0.1 add.43
  7.2 0.0 copy-done.5
  7.2 0.1 add_convert_fusion
  7.2 0.1 divide_subtract_fusion.h_ref
  7.3 0.0 collective-permute-done.refs_1_
  7.3 2.0 %collective-permute-done.1.refs_2_ = f32[16,640]{1,0:T(8,128)S(1)} collective-permute-done((f32[16,640]{1,0:T(8,128)}, f32[16,640]{1,0:T(8,128)S(1)}, u32[]{:S(2)}, u32[]{:S(2)}) %collective-permute-start.1) | collective-permute-done | bytes 40992 | tf_op jit(solution)/shard_map/ppermute | solution.py:454
  9.3 1.4 %collective-permute-done.2.refs_3_ = f32[16,640]{1,0:T(8,128)S(1)} collective-permute-done((f32[16,640]{1,0:T(8,128)}, f32[16,640]{1,0:T(8,128)S(1)}, u32[]{:S(2)}, u32[]{:S(2)}) %collective-permute-start.2) | collective-permute-done | bytes 40992 | tf_op jit(solution)/shard_map/ppermute | solution.py:454
  10.6 0.0 copy-done
  10.7 0.7 %copy-done.1 = f32[16,128]{1,0:T(8,128)S(1)} copy-done((f32[16,128]{1,0:T(8,128)S(1)}, f32[16,128]{1,0:T(8,128)}, u32[]{:S(2)}) %copy-start.1) | copy-done | bytes 8216
  11.3 0.2 filter_slots.1
  11.5 2.6 %collective-permute-start.3 = (f32[16,768]{1,0:T(8,128)S(1)}, f32[16,768]{1,0:T(8,128)S(1)}, u32[]{:S(2)}, u32[]{:S(2)}) collective-permute-start(f32[16,768]{1,0:T(8,128)S(1)} %filter_slots.1), channel_id=1, source_target_pairs={{0,16},{4,20},{8,24},{12,28},{16,0},{20,4},{24,8},{28,12},{1,17},{... | collective-permute-start | bytes 147464 | tf_op jit(solution)/shard_map/ppermute | solution.py:454
  14.2 3.5 %collective-permute-done.3 = f32[16,768]{1,0:T(8,128)S(1)} collective-permute-done((f32[16,768]{1,0:T(8,128)S(1)}, f32[16,768]{1,0:T(8,128)S(1)}, u32[]{:S(2)}, u32[]{:S(2)}) %collective-permute-start.3) | collective-permute-done | bytes 49184 | tf_op jit(solution)/shard_map/ppermute | solution.py:454
  17.6 1.6 %collective-permute-start.6 = (f32[2,16,768]{2,1,0:T(8,128)S(1)}, f32[2,16,768]{2,1,0:T(8,128)S(1)}, u32[]{:S(2)}, u32[]{:S(2)}) collective-permute-start(f32[2,16,768]{2,1,0:T(8,128)S(1)} %pad_maximum_fusion.refs_2_), channel_id=1, source_target_pairs={{0,4},{4,0},{8,12},{12,8},{16,20},{20,16},{24,28},{28,24},{1,5},{5... | collective-permute-start | bytes 294920 | tf_op jit(solution)/shard_map/ppermute | solution.py:454
  19.2 0.5 %collective-permute-start.5 = (f32[2,16,768]{2,1,0:T(8,128)S(1)}, f32[2,16,768]{2,1,0:T(8,128)S(1)}, u32[]{:S(2)}, u32[]{:S(2)}) collective-permute-start(f32[2,16,768]{2,1,0:T(8,128)S(1)} %pad_maximum_fusion.refs_2_), channel_id=1, source_target_pairs={{0,8},{4,12},{8,0},{12,4},{16,24},{20,28},{24,16},{28,20},{1,9},{5... | collective-permute-start | bytes 294920 | tf_op jit(solution)/shard_map/ppermute | solution.py:454
  19.8 1.4 %collective-permute-start.4 = (f32[2,16,768]{2,1,0:T(8,128)S(1)}, f32[2,16,768]{2,1,0:T(8,128)S(1)}, u32[]{:S(2)}, u32[]{:S(2)}) collective-permute-start(f32[2,16,768]{2,1,0:T(8,128)S(1)} %pad_maximum_fusion.refs_2_), channel_id=1, source_target_pairs={{0,12},{4,8},{8,4},{12,0},{16,28},{20,24},{24,20},{28,16},{1,13},{... | collective-permute-start | bytes 294920 | tf_op jit(solution)/shard_map/ppermute | solution.py:454
  21.2 0.0 copy-done.2
  21.2 0.0 copy-done.3
  21.2 1.8 %add_sources.4 = (f32[136,1024]{1,0:T(8,128)S(1)}, f32[24,640]{1,0:T(8,128)S(1)}) custom-call(s32[1]{0:T(128)} %bitcast.refs_0_, s32[1,8]{1,0:T(1,128)S(1)} %copy-done.3, f32[2,16,768]{2,1,0:T(8,128)S(1)} %pad_maximum_fusion.refs_2_, f32[16,128]{1,0:T(8,128)S(1)} %copy-done.2), custom_call_target="tpu_custom_call" | custom-call | flops 475004928 | bytes 1048576 | tf_op jit(solution)/shard_map/add_sources/pallas_call | solution.py:429
  23.0 0.0 collective-permute-done.6.refs_2_
  23.0 2.0 %add_sources.5 = (f32[136,1024]{1,0:T(8,128)S(1)}, f32[24,640]{1,0:T(8,128)S(1)}) custom-call(s32[1]{0:T(128)} %bitcast.refs_0_, s32[1,8]{1,0:T(1,128)S(1)} %copy-done.3, f32[2,16,768]{2,1,0:T(8,128)S(1)} %collective-permute-done.6.refs_2_, f32[16,128]{1,0:T(8,128)S(1)} %copy-done.2, ...), custom_call_target="tpu_custom_call", output_to_operand_aliasing={{0}: (4, {}), {1}: (5, {})} | custom-call | flops 475004928 | bytes 1048576 | tf_op jit(solution)/shard_map/add_sources/pallas_call | solution.py:429
  25.0 0.0 collective-permute-done.5.refs_2_
  25.0 0.0 copy-start.4
  25.0 2.0 %add_sources.6 = (f32[136,1024]{1,0:T(8,128)S(1)}, f32[24,640]{1,0:T(8,128)S(1)}) custom-call(s32[1]{0:T(128)} %bitcast.refs_0_, s32[1,8]{1,0:T(1,128)S(1)} %copy-done.3, f32[2,16,768]{2,1,0:T(8,128)S(1)} %collective-permute-done.5.refs_2_, f32[16,128]{1,0:T(8,128)S(1)} %copy-done.2, ...), custom_call_target="tpu_custom_call", output_to_operand_aliasing={{0}: (4, {}), {1}: (5, {})} | custom-call | flops 475004928 | bytes 1048576 | tf_op jit(solution)/shard_map/add_sources/pallas_call | solution.py:429
  27.0 0.0 collective-permute-done.4.refs_2_
  27.0 0.0 copy-done.4
  27.0 2.6 %add_sources.7 = (f32[16,8,1024]{2,1,0:T(8,128)}, f32[16,1024]{1,0:T(8,128)}) custom-call(s32[1]{0:T(128)} %bitcast.refs_0_, s32[1,8]{1,0:T(1,128)S(1)} %copy-done.3, f32[2,16,768]{2,1,0:T(8,128)S(1)} %collective-permute-done.4.refs_2_, f32[16,128]{1,0:T(8,128)S(1)} %copy-done.2, f32[136,1024]{1,0:T(8,128)S(1)} %get-tuple-element.19.refs_4_, ...), custom_call_target="tpu_custom_call" | custom-call | flops 475004928 | bytes 1048576 | tf_op jit(solution)/shard_map/add_sources/pallas_call | solution.py:429
  (7 shorter events, 0.0 us)
Async XLA Ops:
  0.6 6.5 %copy-start.5 = (s32[64]{0:T(128)S(1)}, s32[64]{0:T(128)}, u32[]{:S(2)}) copy-start(s32[64]{0:T(128)} %param.11) | copy-start | bytes 772
  3.9 6.8 %copy-start = (f32[16,640]{1,0:T(8,128)S(1)}, f32[16,640]{1,0:T(8,128)}, u32[]{:S(2)}) copy-start(f32[16,640]{1,0:T(8,128)} %get-tuple-element.13.refs_0_) | copy-start | bytes 122884
  3.9 3.4 %collective-permute-start = (f32[16,640]{1,0:T(8,128)}, f32[16,640]{1,0:T(8,128)S(1)}, u32[]{:S(2)}, u32[]{:S(2)}) collective-permute-start(f32[16,640]{1,0:T(8,128)} %get-tuple-element.13.refs_0_), channel_id=1, source_target_pairs={{0,1},{1,0},{2,3},{3,2},{4,5},{5,4},{6,7},{7,6},{8,9},{9,8},{10,11... | collective-permute-start | bytes 122888 | tf_op jit(solution)/shard_map/ppermute | solution.py:454
  4.4 4.9 %collective-permute-start.1 = (f32[16,640]{1,0:T(8,128)}, f32[16,640]{1,0:T(8,128)S(1)}, u32[]{:S(2)}, u32[]{:S(2)}) collective-permute-start(f32[16,640]{1,0:T(8,128)} %get-tuple-element.13.refs_0_), channel_id=1, source_target_pairs={{0,2},{1,3},{2,0},{3,1},{4,6},{5,7},{6,4},{7,5},{8,10},{9,11},{10,... | collective-permute-start | bytes 122888 | tf_op jit(solution)/shard_map/ppermute | solution.py:454
  6.9 3.7 %collective-permute-start.2 = (f32[16,640]{1,0:T(8,128)}, f32[16,640]{1,0:T(8,128)S(1)}, u32[]{:S(2)}, u32[]{:S(2)}) collective-permute-start(f32[16,640]{1,0:T(8,128)} %get-tuple-element.13.refs_0_), channel_id=1, source_target_pairs={{0,3},{1,2},{2,1},{3,0},{4,7},{5,6},{6,5},{7,4},{8,11},{9,10},{10,... | collective-permute-start | bytes 122888 | tf_op jit(solution)/shard_map/ppermute | solution.py:454
  10.6 0.7 %copy-start.1 = (f32[16,128]{1,0:T(8,128)S(1)}, f32[16,128]{1,0:T(8,128)}, u32[]{:S(2)}) copy-start(f32[16,128]{1,0:T(8,128)} %get-tuple-element.14.refs_4_.refs_3_) | copy-start | bytes 24580
  11.5 6.1 %collective-permute-start.3 = (f32[16,768]{1,0:T(8,128)S(1)}, f32[16,768]{1,0:T(8,128)S(1)}, u32[]{:S(2)}, u32[]{:S(2)}) collective-permute-start(f32[16,768]{1,0:T(8,128)S(1)} %filter_slots.1), channel_id=1, source_target_pairs={{0,16},{4,20},{8,24},{12,28},{16,0},{20,4},{24,8},{28,12},{1,17},{... | collective-permute-start | bytes 147464 | tf_op jit(solution)/shard_map/ppermute | solution.py:454
  17.6 3.6 %copy-start.2 = (f32[16,128]{1,0:T(8,128)S(1)}, f32[16,128]{1,0:T(8,128)}, u32[]{:S(2)}) copy-start(f32[16,128]{1,0:T(8,128)} %get-tuple-element.14.refs_4_.refs_3_) | copy-start | bytes 24580
  17.6 5.4 %collective-permute-start.6 = (f32[2,16,768]{2,1,0:T(8,128)S(1)}, f32[2,16,768]{2,1,0:T(8,128)S(1)}, u32[]{:S(2)}, u32[]{:S(2)}) collective-permute-start(f32[2,16,768]{2,1,0:T(8,128)S(1)} %pad_maximum_fusion.refs_2_), channel_id=1, source_target_pairs={{0,4},{4,0},{8,12},{12,8},{16,20},{20,16},{24,28},{28,24},{1,5},{5... | collective-permute-start | bytes 294920 | tf_op jit(solution)/shard_map/ppermute | solution.py:454
  19.2 5.8 %collective-permute-start.5 = (f32[2,16,768]{2,1,0:T(8,128)S(1)}, f32[2,16,768]{2,1,0:T(8,128)S(1)}, u32[]{:S(2)}, u32[]{:S(2)}) collective-permute-start(f32[2,16,768]{2,1,0:T(8,128)S(1)} %pad_maximum_fusion.refs_2_), channel_id=1, source_target_pairs={{0,8},{4,12},{8,0},{12,4},{16,24},{20,28},{24,16},{28,20},{1,9},{5... | collective-permute-start | bytes 294920 | tf_op jit(solution)/shard_map/ppermute | solution.py:454
  19.8 1.5 %copy-start.3 = (s32[1,8]{1,0:T(1,128)S(1)}, s32[1,8]{1,0:T(1,128)}, u32[]{:S(2)}) copy-start(s32[1,8]{1,0:T(1,128)} %refs_1_.7) | copy-start | bytes 100
  19.8 7.2 %collective-permute-start.4 = (f32[2,16,768]{2,1,0:T(8,128)S(1)}, f32[2,16,768]{2,1,0:T(8,128)S(1)}, u32[]{:S(2)}, u32[]{:S(2)}) collective-permute-start(f32[2,16,768]{2,1,0:T(8,128)S(1)} %pad_maximum_fusion.refs_2_), channel_id=1, source_target_pairs={{0,12},{4,8},{8,4},{12,0},{16,28},{20,24},{24,20},{28,16},{1,13},{... | collective-permute-start | bytes 294920 | tf_op jit(solution)/shard_map/ppermute | solution.py:454
  25.0 2.0 %copy-start.4 = (f32[16,640]{1,0:T(8,128)S(1)}, f32[16,640]{1,0:T(8,128)}, u32[]{:S(2)}) copy-start(f32[16,640]{1,0:T(8,128)} %get-tuple-element.21.refs_6_) | copy-start | bytes 122884

commit v3 on v2

--- a/solution.py
+++ b/solution.py
@@ -160,11 +160,12 @@
 
 
 MAX_BLOCKS = 8
+NOWHERE = -(SLAB_PIX * 8)
 LO = 512
 STEP = 8
 
 
-def gather_kernel(n_tile, counts_ref, list_ref, phases_ref, coh_ref, pix_ref, out_ref, own_ref, wg_ref):
+def gather_kernel(n_tile, counts_ref, list_ref, phases_ref, coh_ref, pix_ref, out_ref, own_ref):
     acq_loc, local = phases_ref.shape
     pieces = local // LO
     step = min(STEP, pieces)
@@ -194,10 +195,12 @@
 
     weight = (pick(0) + pick(1)) * live
     pixel = pick(2) * 64.0 + pick(3) + tile.astype(jnp.float32) * float(SLAB_PIX)
+    pixel = jnp.where(live > 0.0, pixel, float(NOWHERE))
+    out_ref[:, packed:] = jnp.zeros((acq_loc, LANES), jnp.float32)
     for b in range(packed // LANES):
         cut = slice(b * LANES, (b + 1) * LANES)
-        wg_ref[b : b + 1, :] = weight[:, cut]
-        wg_ref[MAX_BLOCKS + b : MAX_BLOCKS + b + 1, :] = pixel[:, cut]
+        out_ref[b : b + 1, packed:] = weight[:, cut]
+        out_ref[MAX_BLOCKS + b : MAX_BLOCKS + b + 1, packed:] = pixel[:, cut]
     low = index & (LO - 1)
     high = index >> 9
     chosen = (lax.broadcasted_iota(jnp.int32, (LO, packed), 0) == low)
@@ -212,21 +215,33 @@
         for h in range(step):
             own = jnp.where(high == start + h, both[h * acq_loc : (h + 1) * acq_loc], own)
     own_ref[...] = own
-    out_ref[...] = own * weight
-
-
-def filter_kernel(h_ref, *refs):
-    *parts, wg_ref, out_ref = refs
-    packed = parts[0].shape[1]
-    series = jnp.concatenate([part[...] for part in parts], 0)
-    out_ref[:, 0:packed] = lax.dot_general(
-        h_ref[...],
+    out_ref[:, 0:packed] = own * weight
+
+
+def filter_dot(weights, series):
+    return lax.dot_general(
+        weights,
         series,
         (NN, ((), ())),
         precision=lax.Precision.HIGHEST,
         preferred_element_type=jnp.float32,
     )
-    out_ref[:, packed:] = wg_ref[...]
+
+
+def filter_own_kernel(h_ref, part_ref, out_ref):
+    acq_loc, lanes = part_ref.shape
+    packed = lanes - LANES
+    out_ref[:, 0:packed] = filter_dot(h_ref[:, 0:acq_loc], part_ref[:, 0:packed])
+    out_ref[:, packed:] = part_ref[:, packed:]
+
+
+def filter_kernel(h_ref, begun_ref, *refs):
+    *parts, out_ref = refs
+    acq_loc, lanes = begun_ref.shape
+    packed = lanes - LANES
+    series = jnp.concatenate([part[:, 0:packed] for part in parts], 0)
+    out_ref[:, 0:packed] = begun_ref[:, 0:packed] + filter_dot(h_ref[:, acq_loc:], series)
+    out_ref[:, packed:] = begun_ref[:, packed:]
 
 
 def first_pair(tile, n_pair):
@@ -246,6 +261,11 @@
     return (whole >> 10).astype(jnp.float32), (whole & (COLS - 1)).astype(jnp.float32)
 
 
+def split_column(col):
+    coarse = jnp.floor(col * 0.125) * 8.0
+    return coarse, col - coarse
+
+
 def rows_of_bf16(row, count):
     few = jnp.broadcast_to(row, (16, row.shape[1])).astype(jnp.bfloat16)
     return jnp.concatenate([few] * (count // 16), 0)
@@ -254,25 +274,9 @@
 CHUNK = 256
 
 
-def slot_groups(n_tile, counts_ref):
-    n_pair = n_tile // 2
-    first, last = heavy_tiles(counts_ref, n_tile)
-    groups = []
-    for t in range(n_tile):
-        p = min(max((t + 1) // 2 - 1, 0), max(n_pair - 2, 0))
-        if groups and groups[-1][2] == p:
-            groups[-1][1] += HALF
-        else:
-            groups.append([t * HALF, HALF, p])
-    base = n_pair * LANES
-    groups.append([base, HALF, first_pair(first, n_pair)])
-    groups.append([base + HALF, HALF, first_pair(last, n_pair)])
-    return groups
-
-
 def screen_kernel(n_tile, begins, ends, *refs):
-    me_ref, counts_ref, all_ref, mine_ref = refs[:4]
-    refs = refs[4:]
+    all_ref, mine_ref = refs[:2]
+    refs = refs[2:]
     if not begins:
         image_in, samples_in = refs[:2]
         refs = refs[2:]
@@ -282,13 +286,13 @@
     else:
         image_out, samples_out = refs[:2]
         refs = refs[2:]
-    tag_ref, value_ref, lhs_ref, col_ref, pair_ref, res_ref = refs
+    tag_ref, value_ref, lhs_ref, col_ref, pair_ref, res_ref, made_ref, made_sem = refs
     n_src, acq_loc, packed = all_ref.shape
     packed -= LANES
     n_pair = n_tile // 2
     width = 3 * LANES
     limit = min_weight * float((RADIUS + 1) ** 4)
-    me = me_ref[0]
+    me = lax.axis_index("tile")
     f32, bf16 = jnp.float32, jnp.bfloat16
 
     def starts(pair):
@@ -312,6 +316,7 @@
             tag_ref[src, 0:1, lanes] = weight
             tag_ref[src, 1:2, lanes] = row
             tag_ref[src, 2:3, lanes] = col
+            tag_ref[src, 3:4, lanes], tag_ref[src, 4:5, lanes] = split_column(col)
             w_hi = weight.astype(bf16).astype(f32)
             both = jnp.where(sub == 0, w_hi, jnp.where(sub == 1, weight - w_hi, 0.0))
             value_ref[src, 2 * acq_loc :, lanes] = both.astype(bf16)
@@ -334,36 +339,59 @@
         w_part = across * weight
         w_hi = w_part.astype(bf16).astype(f32)
         lhs_ref[2 * n_img :, lanes] = jnp.concatenate([w_hi, w_part - w_hi], 0).astype(bf16)
-        for c in range(0, COLS, CHUNK):
-            near = jnp.clip(col - float(c + CHUNK // 2), -160.0, 160.0)
-            col_ref[c : c + CHUNK, lanes] = hat_bf16(col_at - rows_of_bf16(near, CHUNK))
 
     def down_lanes(row):
         return jnp.transpose(jnp.broadcast_to(row, (LANES, LANES)))
 
-    mine = [split_pixel(mine_ref[MAX_BLOCKS + b : MAX_BLOCKS + b + 1, :]) for b in range(n_pair + 1)]
-    rows_down = jnp.concatenate([down_lanes(r) for r, _ in mine], 0).astype(bf16)
-    cols_down = jnp.concatenate([down_lanes(c) for _, c in mine], 0)
-
-    def sample(start, size, p):
-        r_i = rows_down[start : start + size]
-        c_i = cols_down[start : start + size]
-        values = []
+    mine = [mine_ref[MAX_BLOCKS + b : MAX_BLOCKS + b + 1, packed:] for b in range(n_pair + 1)]
+    places = [split_pixel(pixel) for pixel in mine]
+    rows_down = jnp.concatenate([down_lanes(r) for r, _ in places], 0).astype(bf16)
+    coarse_down, fine_down = (
+        jnp.concatenate([down_lanes(split_column(c)[k]) for _, c in places], 0).astype(bf16)
+        for k in (0, 1)
+    )
+
+    def pair_hats(i):
         for src in range(n_src):
-            _, row, col = tags(src, p)
-            for b, s in enumerate(starts(p)):
+            for b in range(n_pair + 1):
                 cut = slice(b * LANES, (b + 1) * LANES)
-                values.append(value_ref[src, :, pl.ds(s, LANES)])
-                over = hat_bf16(r_i - rows_of_bf16(row[:, cut], size))
-                both = over * hat_bf16((c_i - col[:, cut]).astype(bf16))
-                at = src * width + b * LANES
-                pair_ref[start : start + size, at : at + LANES] = both
-        got = dot_f32(jnp.concatenate(values, 1), pair_ref[start : start + size, :], NT)
+                at = src * packed + b * LANES
+                low, high = i * LANES, (i + 1) * LANES
+                if max(i, b) < n_pair and i != b:
+                    if b == i + 1:
+                        low += HALF
+                    elif b == i - 1:
+                        high -= HALF
+                    else:
+                        high = low
+                for start in (i * LANES, i * LANES + HALF):
+                    if low <= start < high:
+                        continue
+                    zero = jnp.zeros((HALF, LANES), bf16)
+                    pair_ref[start : start + HALF, at : at + LANES] = zero
+                if low == high:
+                    continue
+                size = high - low
+                row, coarse, fine = (
+                    rows_of_bf16(tag_ref[src, k : k + 1, cut], size) for k in (1, 3, 4)
+                )
+                over = hat_bf16(rows_down[low:high] - row)
+                across = (coarse_down[low:high] - coarse) + (fine_down[low:high] - fine)
+                pair_ref[low:high, at : at + LANES] = over * hat_bf16(across)
+
+    def sample():
+        values = jnp.concatenate([value_ref[src] for src in range(n_src)], 1)
+        got = dot_f32(values, pair_ref[...], NT)
         total = got[0:acq_loc] + got[acq_loc : 2 * acq_loc]
         below = got[2 * acq_loc : 2 * acq_loc + 8]
         return jnp.concatenate([total, below], 0)
 
     def slab(c):
+        for src in range(n_src):
+            _, _, col = tags(src, pair)
+            near = jnp.clip(col - float(c + CHUNK // 2), -160.0, 160.0)
+            lanes = slice(src * width, (src + 1) * width)
+            col_ref[c : c + CHUNK, lanes] = hat_bf16(col_at - rows_of_bf16(near, CHUNK))
         got = dot_f32(lhs_ref[...], col_ref[c : c + CHUNK, :], NT)
         return jnp.concatenate(
             [
@@ -373,17 +401,27 @@
             0,
         )
 
+    copies = []
     for c in range(0, COLS, CHUNK):
         image = slab(c)
+        lanes = slice(c, c + CHUNK)
         if not begins:
-            image = image + image_in[:, c : c + CHUNK]
+            image = image + image_in[:, lanes]
         if not ends:
-            image_out[:, c : c + CHUNK] = image
+            image_out[:, lanes] = image
             continue
         below = jnp.maximum(image[n_img:], limit)
         for a in range(acq_loc):
-            screen_ref[a, :, c : c + CHUNK] = image[a * ROWS_DEV : (a + 1) * ROWS_DEV] / below
-    samples = jnp.concatenate([sample(*group) for group in slot_groups(n_tile, counts_ref)], 1)
+            made_ref[a, :, lanes] = image[a * ROWS_DEV : (a + 1) * ROWS_DEV] / below
+        copies.append(
+            pltpu.make_async_copy(
+                made_ref.at[:, :, lanes], screen_ref.at[:, :, lanes], made_sem.at[c // CHUNK]
+            )
+        )
+        copies[-1].start()
+    for i in range(n_pair + 1):
+        pair_hats(i)
+    samples = sample()
     if not begins:
         samples = samples + samples_in[...]
     if not ends:
@@ -392,32 +430,34 @@
     below = samples[acq_loc : acq_loc + 1] + samples[acq_loc + 1 : acq_loc + 2]
     res_ref[...] = own_ref[...] - samples[0:acq_loc] / jnp.maximum(below, limit)
 
-    first, _ = heavy_tiles(counts_ref, n_tile)
-    lane = lax.broadcasted_iota(jnp.int32, (1, LANES), 1)
-    lower = lane < HALF
+    lower = lax.broadcasted_iota(jnp.int32, (1, LANES), 1) < HALF
+    tiles = [pixel.astype(jnp.int32) // SLAB_PIX for pixel in mine]
     heavy = res_ref[:, n_pair * LANES :]
     turned = pltpu.roll(heavy, HALF, 1)
+    tile_turned = pltpu.roll(tiles[n_pair], HALF, 1)
     for t in range(n_tile):
         near = res_ref[:, (t // 2) * LANES : (t // 2 + 1) * LANES]
+        tile_near = tiles[t // 2]
         if t % 2:
             near = pltpu.roll(near, HALF, 1)
-        far = jnp.where(first == t, turned, heavy)
-        both = jnp.where(lower, near, far)
+            tile_near = pltpu.roll(tile_near, HALF, 1)
+        far = jnp.where(tile_turned == t, turned, jnp.where(tiles[n_pair] == t, heavy, 0.0))
         residual_ref[:, t * LANES : (t + 1) * LANES] = jnp.where(
-            lane < counts_ref[0, t], both, 0.0
+            lower, jnp.where(tile_near == t, near, 0.0), far
         )
-
-
-def add_sources(n_tile, me, counts, sources, mine, sums, own):
+    for copy in copies:
+        copy.wait()
+
+
+def add_sources(n_tile, sources, mine, sums, own):
     n_src, acq_loc, packed = sources.shape
     packed -= LANES
     width = n_src * 3 * LANES
     f32, bf16 = jnp.float32, jnp.bfloat16
-    smem = pl.BlockSpec(memory_space=pltpu.SMEM)
     vmem = pl.BlockSpec(memory_space=pltpu.VMEM)
     n_lhs = 2 * (acq_loc + 1) * ROWS_DEV
     begins, ends = sums is None, own is not None
-    args = [me, counts, sources, mine]
+    args = [sources, mine]
     if not begins:
         args += list(sums)
     if ends:
@@ -429,17 +469,19 @@
     return pl.pallas_call(
         functools.partial(screen_kernel, n_tile, begins, ends),
         out_shape=tuple(jax.ShapeDtypeStruct(shape, f32) for shape in shapes),
-        in_specs=[smem, smem] + [vmem] * (len(args) - 2),
-        out_specs=(vmem, vmem),
+        in_specs=[vmem] * len(args),
+        out_specs=(pl.BlockSpec(memory_space=pl.ANY) if ends else vmem, vmem),
         scratch_shapes=[
             pltpu.VMEM((n_src, 8, packed), f32),
             pltpu.VMEM((n_src, 2 * acq_loc + 16, packed), bf16),
             pltpu.VMEM((n_lhs, width), bf16),
             pltpu.VMEM((COLS, width), bf16),
-            pltpu.VMEM((packed, width), bf16),
+            pltpu.VMEM((packed, n_src * packed), bf16),
             pltpu.VMEM((acq_loc, packed), f32),
+            pltpu.VMEM((acq_loc, ROWS_DEV, COLS), f32),
+            pltpu.SemaphoreType.DMA((COLS // CHUNK,)),
         ],
-        input_output_aliases={} if begins or ends else {4: 0, 5: 1},
+        input_output_aliases={} if begins or ends else {2: 0, 3: 1},
         cost_estimate=pl.CostEstimate(flops=2 * macs, bytes_accessed=1 << 20, transcendentals=0),
         compiler_params=pltpu.CompilerParams(vmem_limit_bytes=SCREEN_VMEM),
         name="add_sources",
@@ -462,15 +504,14 @@
     smem = pl.BlockSpec(memory_space=pltpu.SMEM)
     vmem = pl.BlockSpec(memory_space=pltpu.VMEM)
     f32 = jnp.float32
-    outgoing, own, wg = pl.pallas_call(
+    packet, own = pl.pallas_call(
         functools.partial(gather_kernel, n_tile),
         out_shape=(
+            jax.ShapeDtypeStruct((acq_loc, packed + LANES), f32),
             jax.ShapeDtypeStruct((acq_loc, packed), f32),
-            jax.ShapeDtypeStruct((acq_loc, packed), f32),
-            jax.ShapeDtypeStruct((2 * MAX_BLOCKS, LANES), f32),
         ),
         in_specs=[smem, vmem, vmem, vmem, vmem],
-        out_specs=(vmem, vmem, vmem),
+        out_specs=(vmem, vmem),
         compiler_params=pltpu.CompilerParams(vmem_limit_bytes=56 << 20),
         name="gather_slots",
     )(
@@ -481,7 +522,7 @@
         pixel_index.reshape(-1, LANES),
     )
     here = lax.axis_index("acq")
-    parts = [outgoing] + [xor_permute(outgoing, "acq", k) for k in range(1, n_acq)]
+    parts = [packet] + [xor_permute(packet, "acq", k) for k in range(1, n_acq)]
     source = here ^ jnp.arange(n_acq, dtype=jnp.int32)
     column = (source[:, None] * acq_loc + jnp.arange(acq_loc, dtype=jnp.int32)[None]).reshape(1, -1)
     row = here * acq_loc + jnp.arange(acq_loc, dtype=jnp.int32)
@@ -490,22 +531,34 @@
     upper = jnp.minimum(row + band, ACQ - 1)[:, None]
     inside = ((column >= lower) & (column <= upper)).astype(f32)
     highpass = (column == row[:, None]).astype(f32) - inside / (upper - lower + 1).astype(f32)
+    packet_shape = jax.ShapeDtypeStruct((acq_loc, packed + LANES), f32)
+    small = pltpu.CompilerParams(vmem_limit_bytes=4 << 20)
+    begun = pl.pallas_call(
+        filter_own_kernel,
+        out_shape=packet_shape,
+        in_specs=[vmem] * 2,
+        out_specs=vmem,
+        cost_estimate=pl.CostEstimate(flops=1 << 20, bytes_accessed=1 << 20, transcendentals=0),
+        compiler_params=small,
+        name="filter_own_slots",
+    )(highpass, packet)
     filtered = pl.pallas_call(
         filter_kernel,
-        out_shape=jax.ShapeDtypeStruct((acq_loc, packed + LANES), f32),
-        in_specs=[vmem] * (n_acq + 2),
+        out_shape=packet_shape,
+        in_specs=[vmem] * (n_acq + 1),
         out_specs=vmem,
-        compiler_params=pltpu.CompilerParams(vmem_limit_bytes=4 << 20),
+        compiler_params=small,
         name="filter_slots",
-    )(highpass, *parts, wg)
-    me = lax.axis_index("tile").astype(jnp.int32).reshape(1)
+    )(highpass, begun, *parts[1:])
     half = n_tile // 2
-    held = jnp.stack([filtered, xor_permute(filtered, "tile", half)])
-    others = [xor_permute(held, "tile", k) for k in range(1, half)]
-    sums = None
-    for sources in [held] + others[:-1]:
-        sums = add_sources(n_tile, me, counts, sources, wg, sums, None)
-    screen, residual = add_sources(n_tile, me, counts, others[-1], wg, sums, own)
+    across = xor_permute(filtered, "tile", half)
+    sums = add_sources(n_tile, filtered[None], filtered, None, None)
+    across, sums = lax.optimization_barrier((across, sums))
+    held = jnp.stack([filtered, across])
+    arriving = [across[None]] + [xor_permute(held, "tile", k) for k in range(1, half)]
+    for sources in arriving[:-1]:
+        sums = add_sources(n_tile, sources, filtered, sums, None)
+    screen, residual = add_sources(n_tile, arriving[-1], filtered, sums, own)
     return residual, screen
 
 

time: 29.9 us -> 28.1 us (0.940)
  waiting for transfers between devices: 6.78 us -> 4.77 us
  local copies, waits for them, and re-layouts: 0.8 us -> 1.54 us
  Pallas kernels: 11.8 us -> 11.4 us
    ppermute x7, waiting for transfers between devices: 6.78 us -> 4.77 us  [xor_permute(): return lax.ppermute(x, axis, [(i, i ^ mask) for i in range(count)])]
    unnamed x12 -> x6, local copies, waits for them, and re-layouts: 0.72 us -> 1.46 us
    pallas_call x4 -> x5, Pallas kernels: 8.38 us -> 7.73 us  [add_sources(): pl.pallas_call(functools.partial(screen_kernel, n_tile, begins, ends), ou...]
where the time goes in v3:
time: 28.1 us; the launch traced here: 27.9 us
  Pallas kernels  11.4 us (41%)
  starting transfers between devices  9.27 us (33%)
  waiting for transfers between devices  4.77 us (17%)
  local copies, waits for them, and re-layouts  1.54 us (5%)
  between operations  0.75 us (3%)
    ppermute x7, starting transfers between devices, xor_permute(): return lax.ppermute(x, axis, [(i, i ^ mask) for i in range(count)])  9.27 us
    pallas_call x5, Pallas kernels, add_sources(): pl.pallas_call(functools.partial(screen_kernel, n_tile, begins, ends), ou...  7.73 us
    ppermute x7, waiting for transfers between devices, xor_permute(): return lax.ppermute(x, axis, [(i, i ^ mask) for i in range(count)])  4.77 us
    pallas_call x1, Pallas kernels, gathered_shards(): pl.pallas_call(functools.partial(gather_kernel, n_tile), out_shape=(jax.S...  3.25 us
    unnamed x6, local copies, waits for them, and re-layouts  1.46 us
  transfers between devices with their start and end apart: 7, of which 3 were waited for; matrix products, arithmetic and copies ran while one was open for 1% of the time, Pallas kernels for 19%

profile of v3, /device:TPU:0, one launch (start us, length us, event | category | flops | bytes accessed | tf_op | source)
XLA Modules:
  0.0 27.9 jit_solution(8755956686630489437)
XLA Ops:
  0.6 3.3 %gather_slots.1 = (f32[16,768]{1,0:T(8,128)}, f32[16,640]{1,0:T(8,128)}) custom-call(s32[1,8]{1,0:T(1,128)} %counts_ref.1, s32[8,128]{1,0:T(8,128)} %list_ref.1, f32[16,16384]{1,0:T(8,128)} %phases_ref.1, f32[128,128]{1,0:T(8,128)} %bitcast.8, s32[128,128]{1,0:T(8,128)} %bitcast.9), custom_call_target="tpu_custom_call" | custom-call | tf_op jit(solution)/shard_map/gather_slots/pallas_call | solution.py:507
  3.9 2.4 %collective-permute-start.2 = (f32[16,768]{1,0:T(8,128)}, f32[16,768]{1,0:T(8,128)S(1)}, u32[]{:S(2)}, u32[]{:S(2)}) collective-permute-start(f32[16,768]{1,0:T(8,128)} %get-tuple-element.17.part_ref), channel_id=1, source_target_pairs={{0,3},{1,2},{2,1},{3,0},{4,7},{5,6},{6,5},{7,4},{8,11},{9,10},{10,... | collective-permute-start | bytes 147464 | tf_op jit(solution)/shard_map/ppermute | solution.py:496
  6.3 0.6 %collective-permute-start.1 = (f32[16,768]{1,0:T(8,128)}, f32[16,768]{1,0:T(8,128)S(1)}, u32[]{:S(2)}, u32[]{:S(2)}) collective-permute-start(f32[16,768]{1,0:T(8,128)} %get-tuple-element.17.part_ref), channel_id=1, source_target_pairs={{0,2},{1,3},{2,0},{3,1},{4,6},{5,7},{6,4},{7,5},{8,10},{9,11},{10,... | collective-permute-start | bytes 147464 | tf_op jit(solution)/shard_map/ppermute | solution.py:496
  6.9 0.1 collective-permute-start
  6.9 0.1 iota_add_fusion
  7.0 0.1 add.43
  7.1 0.0 copy-start.2
  7.1 0.7 %copy-done.2 = s32[64]{0:T(128)S(1)} copy-done((s32[64]{0:T(128)S(1)}, s32[64]{0:T(128)}, u32[]{:S(2)}) %copy-start.2) | copy-done | bytes 280
  7.8 0.1 add_convert_fusion
  7.8 0.1 divide_subtract_fusion.h_ref
  7.9 0.0 copy-start
  7.9 0.8 %copy-done = f32[16,768]{1,0:T(8,128)S(1)} copy-done((f32[16,768]{1,0:T(8,128)S(1)}, f32[16,768]{1,0:T(8,128)}, u32[]{:S(2)}) %copy-start) | copy-done | bytes 49176
  8.7 0.1 filter_own_slots.1.begun_ref
  8.9 0.0 collective-permute-done.2.refs_2_
  8.9 1.9 %collective-permute-done.1.refs_1_ = f32[16,768]{1,0:T(8,128)S(1)} collective-permute-done((f32[16,768]{1,0:T(8,128)}, f32[16,768]{1,0:T(8,128)S(1)}, u32[]{:S(2)}, u32[]{:S(2)}) %collective-permute-start.1) | collective-permute-done | bytes 49184 | tf_op jit(solution)/shard_map/ppermute | solution.py:496
  10.8 0.0 collective-permute-done.refs_0_
  10.8 0.2 filter_slots.1.refs_1_
  11.0 2.7 %collective-permute-start.3 = (f32[16,768]{1,0:T(8,128)S(1)}, f32[16,768]{1,0:T(8,128)S(1)}, u32[]{:S(2)}, u32[]{:S(2)}) collective-permute-start(f32[16,768]{1,0:T(8,128)S(1)} %filter_slots.1.refs_1_), channel_id=1, source_target_pairs={{0,16},{4,20},{8,24},{12,28},{16,0},{20,4},{24,8},{28,12},{1,17},{... | collective-permute-start | bytes 147464 | tf_op jit(solution)/shard_map/ppermute | solution.py:496
  13.7 0.9 %add_sources.5 = (f32[136,1024]{1,0:T(8,128)S(1)}, f32[24,640]{1,0:T(8,128)S(1)}) custom-call(f32[1,16,768]{2,1,0:T(8,128)S(1)} %bitcast.4, f32[16,768]{1,0:T(8,128)S(1)} %filter_slots.1.refs_1_), custom_call_target="tpu_custom_call" | custom-call | flops 237502464 | bytes 1048576 | tf_op jit(solution)/shard_map/add_sources/pallas_call | solution.py:469
  14.6 1.8 %collective-permute-done.3 = f32[16,768]{1,0:T(8,128)S(1)} collective-permute-done((f32[16,768]{1,0:T(8,128)S(1)}, f32[16,768]{1,0:T(8,128)S(1)}, u32[]{:S(2)}, u32[]{:S(2)}) %collective-permute-start.3) | collective-permute-done | bytes 49184 | tf_op jit(solution)/shard_map/ppermute | solution.py:496
  16.5 1.6 %collective-permute-start.6 = (f32[2,16,768]{2,1,0:T(8,128)S(1)}, f32[2,16,768]{2,1,0:T(8,128)S(1)}, u32[]{:S(2)}, u32[]{:S(2)}) collective-permute-start(f32[2,16,768]{2,1,0:T(8,128)S(1)} %pad_maximum_fusion), channel_id=1, source_target_pairs={{0,4},{4,0},{8,12},{12,8},{16,20},{20,16},{24,28},{28,24},{1,5},{5... | collective-permute-start | bytes 294920 | tf_op jit(solution)/shard_map/ppermute | solution.py:496
  18.1 1.2 %collective-permute-start.5 = (f32[2,16,768]{2,1,0:T(8,128)S(1)}, f32[2,16,768]{2,1,0:T(8,128)S(1)}, u32[]{:S(2)}, u32[]{:S(2)}) collective-permute-start(f32[2,16,768]{2,1,0:T(8,128)S(1)} %pad_maximum_fusion), channel_id=1, source_target_pairs={{0,8},{4,12},{8,0},{12,4},{16,24},{20,28},{24,16},{28,20},{1,9},{5... | collective-permute-start | bytes 294920 | tf_op jit(solution)/shard_map/ppermute | solution.py:496
  19.3 0.8 %collective-permute-start.4 = (f32[2,16,768]{2,1,0:T(8,128)S(1)}, f32[2,16,768]{2,1,0:T(8,128)S(1)}, u32[]{:S(2)}, u32[]{:S(2)}) collective-permute-start(f32[2,16,768]{2,1,0:T(8,128)S(1)} %pad_maximum_fusion), channel_id=1, source_target_pairs={{0,12},{4,8},{8,4},{12,0},{16,28},{20,24},{24,20},{28,16},{1,13},{... | collective-permute-start | bytes 294920 | tf_op jit(solution)/shard_map/ppermute | solution.py:496
  20.0 1.0 %add_sources.6 = (f32[136,1024]{1,0:T(8,128)S(1)}, f32[24,640]{1,0:T(8,128)S(1)}) custom-call(f32[1,16,768]{2,1,0:T(8,128)S(1)} %bitcast.7, f32[16,768]{1,0:T(8,128)S(1)} %filter_slots.1.refs_1_, f32[136,1024]{1,0:T(8,128)S(1)} %get-tuple-element.21.refs_2_, f32[24,640]{1,0:T(8,128)S(1)} %get-tuple-element.22.refs_3_), custom_call_target="tpu_custom_call", output_to_operand_aliasing={{0}: (2, {}), {1}: (3, {})} | custom-call | flops 237502464 | bytes 1048576 | tf_op jit(solution)/shard_map/add_sources/pallas_call | solution.py:469
  21.1 1.0 %collective-permute-done.6.refs_0_ = f32[2,16,768]{2,1,0:T(8,128)S(1)} collective-permute-done((f32[2,16,768]{2,1,0:T(8,128)S(1)}, f32[2,16,768]{2,1,0:T(8,128)S(1)}, u32[]{:S(2)}, u32[]{:S(2)}) %collective-permute-start.6) | collective-permute-done | bytes 98336 | tf_op jit(solution)/shard_map/ppermute | solution.py:496
  22.1 1.7 %add_sources.7 = (f32[136,1024]{1,0:T(8,128)S(1)}, f32[24,640]{1,0:T(8,128)S(1)}) custom-call(f32[2,16,768]{2,1,0:T(8,128)S(1)} %collective-permute-done.6.refs_0_, f32[16,768]{1,0:T(8,128)S(1)} %filter_slots.1.refs_1_, f32[136,1024]{1,0:T(8,128)S(1)} %get-tuple-element.23.refs_2_, ...), custom_call_target="tpu_custom_call", output_to_operand_aliasing={{0}: (2, {}), {1}: (3, {})} | custom-call | flops 475004928 | bytes 1048576 | tf_op jit(solution)/shard_map/add_sources/pallas_call | solution.py:469
  23.8 0.0 collective-permute-done.5.refs_0_
  23.8 0.0 copy-start.1
  23.8 1.7 %add_sources.8 = (f32[136,1024]{1,0:T(8,128)S(1)}, f32[24,640]{1,0:T(8,128)S(1)}) custom-call(f32[2,16,768]{2,1,0:T(8,128)S(1)} %collective-permute-done.5.refs_0_, f32[16,768]{1,0:T(8,128)S(1)} %filter_slots.1.refs_1_, f32[136,1024]{1,0:T(8,128)S(1)} %get-tuple-element.25.refs_2_, ...), custom_call_target="tpu_custom_call", output_to_operand_aliasing={{0}: (2, {}), {1}: (3, {})} | custom-call | flops 475004928 | bytes 1048576 | tf_op jit(solution)/shard_map/add_sources/pallas_call | solution.py:469
  25.4 0.0 collective-permute-done.4.refs_0_
  25.5 0.0 copy-done.1
  25.5 2.5 %add_sources.9 = (f32[16,8,1024]{2,1,0:T(8,128)}, f32[16,1024]{1,0:T(8,128)}) custom-call(f32[2,16,768]{2,1,0:T(8,128)S(1)} %collective-permute-done.4.refs_0_, f32[16,768]{1,0:T(8,128)S(1)} %filter_slots.1.refs_1_, f32[136,1024]{1,0:T(8,128)S(1)} %get-tuple-element.27.refs_2_, f32[24,640]{1,0:T(8,128)S(1)} %get-tuple-element.28.refs_3_, f32[16,640]{1,0:T(8,128)S(1)} %copy-done.1), custom_call_target="tpu_custom_call" | custom-call | flops 475004928 | bytes 1048576 | tf_op jit(solution)/shard_map/add_sources/pallas_call | solution.py:469
  (3 shorter events, 0.0 us)
Async XLA Ops:
  3.9 5.0 %collective-permute-start.2 = (f32[16,768]{1,0:T(8,128)}, f32[16,768]{1,0:T(8,128)S(1)}, u32[]{:S(2)}, u32[]{:S(2)}) collective-permute-start(f32[16,768]{1,0:T(8,128)} %get-tuple-element.17.part_ref), channel_id=1, source_target_pairs={{0,3},{1,2},{2,1},{3,0},{4,7},{5,6},{6,5},{7,4},{8,11},{9,10},{10,... | collective-permute-start | bytes 147464 | tf_op jit(solution)/shard_map/ppermute | solution.py:496
  6.3 4.5 %collective-permute-start.1 = (f32[16,768]{1,0:T(8,128)}, f32[16,768]{1,0:T(8,128)S(1)}, u32[]{:S(2)}, u32[]{:S(2)}) collective-permute-start(f32[16,768]{1,0:T(8,128)} %get-tuple-element.17.part_ref), channel_id=1, source_target_pairs={{0,2},{1,3},{2,0},{3,1},{4,6},{5,7},{6,4},{7,5},{8,10},{9,11},{10,... | collective-permute-start | bytes 147464 | tf_op jit(solution)/shard_map/ppermute | solution.py:496
  6.9 3.9 %collective-permute-start = (f32[16,768]{1,0:T(8,128)}, f32[16,768]{1,0:T(8,128)S(1)}, u32[]{:S(2)}, u32[]{:S(2)}) collective-permute-start(f32[16,768]{1,0:T(8,128)} %get-tuple-element.17.part_ref), channel_id=1, source_target_pairs={{0,1},{1,0},{2,3},{3,2},{4,5},{5,4},{6,7},{7,6},{8,9},{9,8},{10,11... | collective-permute-start | bytes 147464 | tf_op jit(solution)/shard_map/ppermute | solution.py:496
  7.1 0.7 %copy-start.2 = (s32[64]{0:T(128)S(1)}, s32[64]{0:T(128)}, u32[]{:S(2)}) copy-start(s32[64]{0:T(128)} %param.11) | copy-start | bytes 772
  7.9 0.8 %copy-start = (f32[16,768]{1,0:T(8,128)S(1)}, f32[16,768]{1,0:T(8,128)}, u32[]{:S(2)}) copy-start(f32[16,768]{1,0:T(8,128)} %get-tuple-element.17.part_ref) | copy-start | bytes 147460
  11.0 5.5 %collective-permute-start.3 = (f32[16,768]{1,0:T(8,128)S(1)}, f32[16,768]{1,0:T(8,128)S(1)}, u32[]{:S(2)}, u32[]{:S(2)}) collective-permute-start(f32[16,768]{1,0:T(8,128)S(1)} %filter_slots.1.refs_1_), channel_id=1, source_target_pairs={{0,16},{4,20},{8,24},{12,28},{16,0},{20,4},{24,8},{28,12},{1,17},{... | collective-permute-start | bytes 147464 | tf_op jit(solution)/shard_map/ppermute | solution.py:496
  16.5 5.6 %collective-permute-start.6 = (f32[2,16,768]{2,1,0:T(8,128)S(1)}, f32[2,16,768]{2,1,0:T(8,128)S(1)}, u32[]{:S(2)}, u32[]{:S(2)}) collective-permute-start(f32[2,16,768]{2,1,0:T(8,128)S(1)} %pad_maximum_fusion), channel_id=1, source_target_pairs={{0,4},{4,0},{8,12},{12,8},{16,20},{20,16},{24,28},{28,24},{1,5},{5... | collective-permute-start | bytes 294920 | tf_op jit(solution)/shard_map/ppermute | solution.py:496
  18.1 5.7 %collective-permute-start.5 = (f32[2,16,768]{2,1,0:T(8,128)S(1)}, f32[2,16,768]{2,1,0:T(8,128)S(1)}, u32[]{:S(2)}, u32[]{:S(2)}) collective-permute-start(f32[2,16,768]{2,1,0:T(8,128)S(1)} %pad_maximum_fusion), channel_id=1, source_target_pairs={{0,8},{4,12},{8,0},{12,4},{16,24},{20,28},{24,16},{28,20},{1,9},{5... | collective-permute-start | bytes 294920 | tf_op jit(solution)/shard_map/ppermute | solution.py:496
  19.3 6.2 %collective-permute-start.4 = (f32[2,16,768]{2,1,0:T(8,128)S(1)}, f32[2,16,768]{2,1,0:T(8,128)S(1)}, u32[]{:S(2)}, u32[]{:S(2)}) collective-permute-start(f32[2,16,768]{2,1,0:T(8,128)S(1)} %pad_maximum_fusion), channel_id=1, source_target_pairs={{0,12},{4,8},{8,4},{12,0},{16,28},{20,24},{24,20},{28,16},{1,13},{... | collective-permute-start | bytes 294920 | tf_op jit(solution)/shard_map/ppermute | solution.py:496
  23.8 1.7 %copy-start.1 = (f32[16,640]{1,0:T(8,128)S(1)}, f32[16,640]{1,0:T(8,128)}, u32[]{:S(2)}) copy-start(f32[16,640]{1,0:T(8,128)} %get-tuple-element.29.refs_4_) | copy-start | bytes 122884

commit v4 on v3

--- a/solution.py
+++ b/solution.py
@@ -108,22 +108,16 @@
     return (residual.reshape(acq_loc, -1), screen)
 
 
-def heavy_tiles(counts_ref, n_tile):
-    first = jnp.int32(0)
-    last = jnp.int32(0)
-    for t in range(n_tile):
-        is_heavy = counts_ref[0, t] >= HALF
-        last = jnp.where(is_heavy, t, last)
-        back = n_tile - 1 - t
-        first = jnp.where(counts_ref[0, back] >= HALF, back, first)
-    return first, last
-
-
 def split_bf16(x):
     high = x.astype(jnp.bfloat16)
     return high, (x - high.astype(jnp.float32)).astype(jnp.bfloat16)
 
 
+def rows_of_bf16(row, count):
+    few = jnp.broadcast_to(row, (16, row.shape[1])).astype(jnp.bfloat16)
+    return jnp.concatenate([few] * (count // 16), 0)
+
+
 def dot_f32(a, b, dims):
     return lax.dot_general(a, b, (dims, ((), ())), preferred_element_type=jnp.float32)
 
@@ -132,26 +126,40 @@
 NT = ((1,), (1,))
 
 
-def packed_rows(counts_ref, list_ref, n_tile):
-    first, last = heavy_tiles(counts_ref, n_tile)
+def packed_rows(counts, lists):
+    n_tile = counts.shape[1]
+    at = lax.broadcasted_iota(jnp.int32, counts.shape, 1).astype(jnp.float32)
+    heavy = counts >= HALF
+    first = jnp.min(jnp.where(heavy, at, float(n_tile - 1)), axis=1, keepdims=True)
+    last = jnp.max(jnp.where(heavy, at, 0.0), axis=1, keepdims=True)
     lane = lax.broadcasted_iota(jnp.int32, (1, LANES), 1)
     lower = lane < HALF
     slot = lane & (HALF - 1)
+
+    def halves(low, high):
+        return jnp.where(lower, jnp.broadcast_to(low, lower.shape), jnp.broadcast_to(high, lower.shape))
+
+    def count_of(t):
+        return counts[:, t : t + 1]
+
     indices, tiles, lives = [], [], []
-    for p in range(n_tile // 2):
-        even = list_ref[pl.ds(2 * p, 1), :]
-        odd = pltpu.roll(list_ref[pl.ds(2 * p + 1, 1), :], HALF, 1)
-        indices.append(jnp.where(lower, even, odd))
-        tiles.append(jnp.where(lower, 2 * p, 2 * p + 1))
-        lives.append(
-            slot < jnp.where(lower, counts_ref[0, 2 * p], counts_ref[0, 2 * p + 1])
-        )
-    early = pltpu.roll(list_ref[pl.ds(first, 1), :], HALF, 1)
-    late = list_ref[pl.ds(last, 1), :]
-    indices.append(jnp.where(lower, early, late))
-    tiles.append(jnp.where(lower, first, last))
-    late_count = jnp.where(first == last, 0, counts_ref[0, last])
-    lives.append(slot + HALF < jnp.where(lower, counts_ref[0, first], late_count))
+    for t in range(0, n_tile, 2):
+        odd = pltpu.roll(lists[t + 1 : t + 2], HALF, 1)
+        indices.append(jnp.where(lower, lists[t : t + 1], odd))
+        tiles.append(jnp.where(lower, t, t + 1))
+        lives.append(slot < halves(count_of(t), count_of(t + 1)))
+    early, late = lists[0:1], lists[0:1]
+    early_count, late_count = count_of(0), count_of(0)
+    for t in range(1, n_tile):
+        row = lists[t : t + 1]
+        early = jnp.where(jnp.broadcast_to(first == t, row.shape), row, early)
+        late = jnp.where(jnp.broadcast_to(last == t, row.shape), row, late)
+        early_count = jnp.where(first == t, count_of(t), early_count)
+        late_count = jnp.where(last == t, count_of(t), late_count)
+    late_count = jnp.where(first == last, 0, late_count)
+    indices.append(jnp.where(lower, pltpu.roll(early, HALF, 1), late))
+    tiles.append(halves(first, last).astype(jnp.int32))
+    lives.append(slot + HALF < halves(early_count, late_count))
     return (
         jnp.concatenate(indices, 1),
         jnp.concatenate(tiles, 1),
@@ -162,77 +170,142 @@
 MAX_BLOCKS = 8
 NOWHERE = -(SLAB_PIX * 8)
 LO = 512
-STEP = 8
-
-
-def gather_kernel(n_tile, counts_ref, list_ref, phases_ref, coh_ref, pix_ref, out_ref, own_ref):
+STEP = 32
+
+
+def gather_kernel(
+    counts_hbm, list_hbm, coh_hbm, pix_hbm, phases_hbm, out_ref, own_ref,
+    counts_ref, list_ref, coh_ref, pix_ref, phases_ref, sems,
+):
     acq_loc, local = phases_ref.shape
     pieces = local // LO
     step = min(STEP, pieces)
-    index, tile, live = packed_rows(counts_ref, list_ref, n_tile)
+    inputs = [
+        (counts_hbm, counts_ref), (list_hbm, list_ref), (coh_hbm, coh_ref), (pix_hbm, pix_ref)
+    ]
+    for start in range(0, pieces, step):
+        lanes = pl.ds(start * LO, step * LO)
+        inputs.append((phases_hbm.at[:, lanes], phases_ref.at[:, lanes]))
+    copies = [pltpu.make_async_copy(*pair, sems.at[i]) for i, pair in enumerate(inputs)]
+    for copy in copies:
+        copy.start()
+    for copy in copies[0:2]:
+        copy.wait()
+    index, tile, live = packed_rows(counts_ref[...], list_ref[...])
     packed = index.shape[1]
-    low = index & (LANES - 1)
-    high = index >> 7
-    chosen = lax.broadcasted_iota(jnp.int32, (LANES, packed), 0) == low
-    table_rows = coh_ref.shape[0]
-    coh_hi, coh_lo = split_bf16(coh_ref[...])
-    pix = pix_ref[...]
+    low = (index & (LO - 1)) - LO // 2
+    high = index >> 9
+    at = (lax.broadcasted_iota(jnp.int32, (LO, packed), 0) - LO // 2).astype(jnp.float32)
+    off = at.astype(jnp.bfloat16) - rows_of_bf16(low.astype(jnp.float32), LO)
+    chosen = jnp.maximum(jnp.bfloat16(1) - jnp.abs(off), jnp.bfloat16(0))
+    twice = jnp.concatenate([chosen, chosen], 0)
+    for copy in copies[2:4]:
+        copy.wait()
+
+    def pieces_of(ref):
+        split = LO // LANES
+        return jnp.concatenate([ref[pl.ds(k, pieces, stride=split), :] for k in range(split)], 1)
+
+    pix = pieces_of(pix_ref)
     table = jnp.concatenate(
         [
-            coh_hi,
-            coh_lo,
-            (pix >> 6).astype(jnp.float32).astype(jnp.bfloat16),
-            (pix & 63).astype(jnp.float32).astype(jnp.bfloat16),
+            jnp.concatenate(split_bf16(pieces_of(coh_ref)), 1),
+            jnp.concatenate(
+                [
+                    ((pix >> 6) << 6).astype(jnp.float32).astype(jnp.bfloat16),
+                    (pix & 63).astype(jnp.float32).astype(jnp.bfloat16),
+                ],
+                1,
+            ),
         ],
         0,
     )
-    columns = dot_f32(table, chosen.astype(jnp.float32).astype(jnp.bfloat16), NN)
-    row_is = lax.broadcasted_iota(jnp.int32, (table_rows, packed), 0) == high
+    columns = dot_f32(table, twice, NN)
+    row_is = lax.broadcasted_iota(jnp.int32, (pieces, packed), 0) == high
 
     def pick(k):
-        part = columns[k * table_rows : (k + 1) * table_rows]
+        part = columns[k * pieces : (k + 1) * pieces]
         return jnp.sum(jnp.where(row_is, part, 0.0), axis=0, keepdims=True)
 
-    weight = (pick(0) + pick(1)) * live
-    pixel = pick(2) * 64.0 + pick(3) + tile.astype(jnp.float32) * float(SLAB_PIX)
+    weight = pick(0) * live
+    pixel = pick(1) + tile.astype(jnp.float32) * float(SLAB_PIX)
     pixel = jnp.where(live > 0.0, pixel, float(NOWHERE))
     out_ref[:, packed:] = jnp.zeros((acq_loc, LANES), jnp.float32)
     for b in range(packed // LANES):
         cut = slice(b * LANES, (b + 1) * LANES)
         out_ref[b : b + 1, packed:] = weight[:, cut]
         out_ref[MAX_BLOCKS + b : MAX_BLOCKS + b + 1, packed:] = pixel[:, cut]
-    low = index & (LO - 1)
-    high = index >> 9
-    chosen = (lax.broadcasted_iota(jnp.int32, (LO, packed), 0) == low)
-    chosen = chosen.astype(jnp.float32).astype(jnp.bfloat16)
     own = jnp.zeros((acq_loc, packed), jnp.float32)
     for start in range(0, pieces, step):
+        copies[4 + start // step].wait()
         block = jnp.concatenate(
             [phases_ref[:, h * LO : (h + 1) * LO] for h in range(start, start + step)], 0
         )
-        block_hi, block_lo = split_bf16(block)
-        both = dot_f32(block_hi, chosen, NN) + dot_f32(block_lo, chosen, NN)
+        both = dot_f32(jnp.concatenate(split_bf16(block), 1), twice, NN)
         for h in range(step):
             own = jnp.where(high == start + h, both[h * acq_loc : (h + 1) * acq_loc], own)
     own_ref[...] = own
     out_ref[:, 0:packed] = own * weight
 
 
+def gather_call(phases, coherence, pixel_index, send_list, counts):
+    acq_loc, local = phases.shape
+    packed = (send_list.shape[0] // 2 + 1) * LANES
+    vmem = pl.BlockSpec(memory_space=pltpu.VMEM)
+    f32 = jnp.float32
+    inputs = (counts, send_list, coherence.reshape(-1, LANES), pixel_index.reshape(-1, LANES), phases)
+    return pl.pallas_call(
+        gather_kernel,
+        out_shape=(
+            jax.ShapeDtypeStruct((acq_loc, packed + LANES), f32),
+            jax.ShapeDtypeStruct((acq_loc, packed), f32),
+        ),
+        in_specs=[pl.BlockSpec(memory_space=pl.ANY)] * len(inputs),
+        out_specs=(vmem, vmem),
+        scratch_shapes=[pltpu.VMEM(x.shape, x.dtype) for x in inputs]
+        + [pltpu.SemaphoreType.DMA((4 + max(local // (LO * STEP), 1),))],
+        compiler_params=pltpu.CompilerParams(vmem_limit_bytes=12 << 20),
+        name="gather_slots",
+    )(*[pltpu.with_memory_space_constraint(x, pltpu.HBM) for x in inputs])
+
+
 def filter_dot(weights, series):
     return lax.dot_general(
         weights,
         series,
-        (NN, ((), ())),
+        (((0,), (0,)), ((), ())),
         precision=lax.Precision.HIGHEST,
         preferred_element_type=jnp.float32,
     )
 
 
-def filter_own_kernel(h_ref, part_ref, out_ref):
+def down_lanes(row):
+    return jnp.transpose(jnp.broadcast_to(row, (LANES, LANES)))
+
+
+def filter_own_kernel(n_acq, band_ref, part_ref, out_ref, h_ref, down_ref):
     acq_loc, lanes = part_ref.shape
     packed = lanes - LANES
-    out_ref[:, 0:packed] = filter_dot(h_ref[:, 0:acq_loc], part_ref[:, 0:packed])
+    me = lax.axis_index("acq")
+    band = band_ref[:, 0:acq_loc]
+    for a in range(1, n_acq):
+        band = jnp.where(me == a, band_ref[:, a * acq_loc : (a + 1) * acq_loc], band)
+    mine = me * acq_loc + lax.broadcasted_iota(jnp.int32, (1, acq_loc), 1)
+    lower = jnp.maximum(mine - band, 0)
+    upper = jnp.minimum(mine + band, ACQ - 1)
+    share = 1.0 / (upper - lower + 1).astype(jnp.float32)
+    for k in range(n_acq):
+        source = (me ^ k) * acq_loc + lax.broadcasted_iota(jnp.int32, (acq_loc, acq_loc), 0)
+        inside = (source >= lower) & (source <= upper)
+        unit = jnp.where(source == mine, 1.0, 0.0)
+        h_ref[k * acq_loc : (k + 1) * acq_loc, :] = unit - jnp.where(inside, share, 0.0)
+    out_ref[:, 0:packed] = filter_dot(h_ref[0:acq_loc, :], part_ref[:, 0:packed])
     out_ref[:, packed:] = part_ref[:, packed:]
+    for b in range(packed // LANES):
+        pixel = part_ref[MAX_BLOCKS + b : MAX_BLOCKS + b + 1, packed:]
+        row, col = split_pixel(pixel)
+        for k, value in enumerate((row, *split_column(col))):
+            down_ref[k, b * LANES : (b + 1) * LANES, :] = down_lanes(value)
 
 
 def filter_kernel(h_ref, begun_ref, *refs):
@@ -240,7 +313,7 @@
     acq_loc, lanes = begun_ref.shape
     packed = lanes - LANES
     series = jnp.concatenate([part[:, 0:packed] for part in parts], 0)
-    out_ref[:, 0:packed] = begun_ref[:, 0:packed] + filter_dot(h_ref[:, acq_loc:], series)
+    out_ref[:, 0:packed] = begun_ref[:, 0:packed] + filter_dot(h_ref[acq_loc:, :], series)
     out_ref[:, packed:] = begun_ref[:, packed:]
 
 
@@ -266,17 +339,12 @@
     return coarse, col - coarse
 
 
-def rows_of_bf16(row, count):
-    few = jnp.broadcast_to(row, (16, row.shape[1])).astype(jnp.bfloat16)
-    return jnp.concatenate([few] * (count // 16), 0)
-
-
 CHUNK = 256
 
 
 def screen_kernel(n_tile, begins, ends, *refs):
-    all_ref, mine_ref = refs[:2]
-    refs = refs[2:]
+    all_ref, mine_ref, down_ref = refs[:3]
+    refs = refs[3:]
     if not begins:
         image_in, samples_in = refs[:2]
         refs = refs[2:]
@@ -286,7 +354,7 @@
     else:
         image_out, samples_out = refs[:2]
         refs = refs[2:]
-    tag_ref, value_ref, lhs_ref, col_ref, pair_ref, res_ref, made_ref, made_sem = refs
+    tag_ref, few_ref, value_ref, lhs_ref, res_ref, made_ref, made_sem = refs
     n_src, acq_loc, packed = all_ref.shape
     packed -= LANES
     n_pair = n_tile // 2
@@ -316,7 +384,8 @@
             tag_ref[src, 0:1, lanes] = weight
             tag_ref[src, 1:2, lanes] = row
             tag_ref[src, 2:3, lanes] = col
-            tag_ref[src, 3:4, lanes], tag_ref[src, 4:5, lanes] = split_column(col)
+            for k, value in enumerate((row, *split_column(col))):
+                few_ref[src, k, :, lanes] = rows_of_bf16(value, 16)
             w_hi = weight.astype(bf16).astype(f32)
             both = jnp.where(sub == 0, w_hi, jnp.where(sub == 1, weight - w_hi, 0.0))
             value_ref[src, 2 * acq_loc :, lanes] = both.astype(bf16)
@@ -340,59 +409,43 @@
         w_hi = w_part.astype(bf16).astype(f32)
         lhs_ref[2 * n_img :, lanes] = jnp.concatenate([w_hi, w_part - w_hi], 0).astype(bf16)
 
-    def down_lanes(row):
-        return jnp.transpose(jnp.broadcast_to(row, (LANES, LANES)))
-
-    mine = [mine_ref[MAX_BLOCKS + b : MAX_BLOCKS + b + 1, packed:] for b in range(n_pair + 1)]
-    places = [split_pixel(pixel) for pixel in mine]
-    rows_down = jnp.concatenate([down_lanes(r) for r, _ in places], 0).astype(bf16)
-    coarse_down, fine_down = (
-        jnp.concatenate([down_lanes(split_column(c)[k]) for _, c in places], 0).astype(bf16)
-        for k in (0, 1)
-    )
-
-    def pair_hats(i):
+    def pair_hats(start):
+        slots = slice(start, start + HALF)
+        near = range(n_pair + 1)
+        if start < n_pair * LANES:
+            tile = start // HALF
+            near = {(tile - 1) // 2, tile // 2, (tile + 1) // 2, n_pair}
+        blocks = []
+        row_i, coarse_i, fine_i = (down_ref[k, slots, :].astype(bf16) for k in range(3))
         for src in range(n_src):
             for b in range(n_pair + 1):
+                if b not in near:
+                    blocks.append(jnp.zeros((HALF, LANES), bf16))
+                    continue
                 cut = slice(b * LANES, (b + 1) * LANES)
-                at = src * packed + b * LANES
-                low, high = i * LANES, (i + 1) * LANES
-                if max(i, b) < n_pair and i != b:
-                    if b == i + 1:
-                        low += HALF
-                    elif b == i - 1:
-                        high -= HALF
-                    else:
-                        high = low
-                for start in (i * LANES, i * LANES + HALF):
-                    if low <= start < high:
-                        continue
-                    zero = jnp.zeros((HALF, LANES), bf16)
-                    pair_ref[start : start + HALF, at : at + LANES] = zero
-                if low == high:
-                    continue
-                size = high - low
                 row, coarse, fine = (
-                    rows_of_bf16(tag_ref[src, k : k + 1, cut], size) for k in (1, 3, 4)
+                    jnp.concatenate([few_ref[src, k, :, cut]] * (HALF // 16), 0) for k in range(3)
                 )
-                over = hat_bf16(rows_down[low:high] - row)
-                across = (coarse_down[low:high] - coarse) + (fine_down[low:high] - fine)
-                pair_ref[low:high, at : at + LANES] = over * hat_bf16(across)
+                across = (coarse_i - coarse) + (fine_i - fine)
+                blocks.append(hat_bf16(row_i - row) * hat_bf16(across))
+
+        return jnp.concatenate(blocks, 1)
 
     def sample():
+        pairs = jnp.concatenate([pair_hats(at) for at in range(0, packed, HALF)], 0)
         values = jnp.concatenate([value_ref[src] for src in range(n_src)], 1)
-        got = dot_f32(values, pair_ref[...], NT)
+        got = dot_f32(values, pairs, NT)
         total = got[0:acq_loc] + got[acq_loc : 2 * acq_loc]
         below = got[2 * acq_loc : 2 * acq_loc + 8]
         return jnp.concatenate([total, below], 0)
 
     def slab(c):
+        cols = []
         for src in range(n_src):
             _, _, col = tags(src, pair)
             near = jnp.clip(col - float(c + CHUNK // 2), -160.0, 160.0)
-            lanes = slice(src * width, (src + 1) * width)
-            col_ref[c : c + CHUNK, lanes] = hat_bf16(col_at - rows_of_bf16(near, CHUNK))
-        got = dot_f32(lhs_ref[...], col_ref[c : c + CHUNK, :], NT)
+            cols.append(hat_bf16(col_at - rows_of_bf16(near, CHUNK)))
+        got = dot_f32(lhs_ref[...], jnp.concatenate(cols, 1), NT)
         return jnp.concatenate(
             [
                 got[0:n_img] + got[n_img : 2 * n_img],
@@ -410,17 +463,15 @@
         if not ends:
             image_out[:, lanes] = image
             continue
-        below = jnp.maximum(image[n_img:], limit)
+        scale = 1.0 / jnp.maximum(image[n_img:], limit)
         for a in range(acq_loc):
-            made_ref[a, :, lanes] = image[a * ROWS_DEV : (a + 1) * ROWS_DEV] / below
+            made_ref[a, :, lanes] = image[a * ROWS_DEV : (a + 1) * ROWS_DEV] * scale
         copies.append(
             pltpu.make_async_copy(
                 made_ref.at[:, :, lanes], screen_ref.at[:, :, lanes], made_sem.at[c // CHUNK]
             )
         )
         copies[-1].start()
-    for i in range(n_pair + 1):
-        pair_hats(i)
     samples = sample()
     if not begins:
         samples = samples + samples_in[...]
@@ -428,10 +479,13 @@
         samples_out[...] = samples
         return
     below = samples[acq_loc : acq_loc + 1] + samples[acq_loc + 1 : acq_loc + 2]
-    res_ref[...] = own_ref[...] - samples[0:acq_loc] / jnp.maximum(below, limit)
+    res_ref[...] = own_ref[...] - samples[0:acq_loc] * (1.0 / jnp.maximum(below, limit))
 
     lower = lax.broadcasted_iota(jnp.int32, (1, LANES), 1) < HALF
-    tiles = [pixel.astype(jnp.int32) // SLAB_PIX for pixel in mine]
+    tiles = [
+        mine_ref[MAX_BLOCKS + b : MAX_BLOCKS + b + 1, packed:].astype(jnp.int32) // SLAB_PIX
+        for b in range(n_pair + 1)
+    ]
     heavy = res_ref[:, n_pair * LANES :]
     turned = pltpu.roll(heavy, HALF, 1)
     tile_turned = pltpu.roll(tiles[n_pair], HALF, 1)
@@ -449,7 +503,7 @@
         copy.wait()
 
 
-def add_sources(n_tile, sources, mine, sums, own):
+def add_sources(n_tile, sources, mine, down, sums, own):
     n_src, acq_loc, packed = sources.shape
     packed -= LANES
     width = n_src * 3 * LANES
@@ -457,7 +511,7 @@
     vmem = pl.BlockSpec(memory_space=pltpu.VMEM)
     n_lhs = 2 * (acq_loc + 1) * ROWS_DEV
     begins, ends = sums is None, own is not None
-    args = [sources, mine]
+    args = [sources, mine, down]
     if not begins:
         args += list(sums)
     if ends:
@@ -473,15 +527,14 @@
         out_specs=(pl.BlockSpec(memory_space=pl.ANY) if ends else vmem, vmem),
         scratch_shapes=[
             pltpu.VMEM((n_src, 8, packed), f32),
+            pltpu.VMEM((n_src, 3, 16, packed), bf16),
             pltpu.VMEM((n_src, 2 * acq_loc + 16, packed), bf16),
             pltpu.VMEM((n_lhs, width), bf16),
-            pltpu.VMEM((COLS, width), bf16),
-            pltpu.VMEM((packed, n_src * packed), bf16),
             pltpu.VMEM((acq_loc, packed), f32),
             pltpu.VMEM((acq_loc, ROWS_DEV, COLS), f32),
             pltpu.SemaphoreType.DMA((COLS // CHUNK,)),
         ],
-        input_output_aliases={} if begins or ends else {2: 0, 3: 1},
+        input_output_aliases={} if begins or ends else {3: 0, 4: 1},
         cost_estimate=pl.CostEstimate(flops=2 * macs, bytes_accessed=1 << 20, transcendentals=0),
         compiler_params=pltpu.CompilerParams(vmem_limit_bytes=SCREEN_VMEM),
         name="add_sources",
@@ -497,68 +550,45 @@
 
 
 def gathered_shards(phases, coherence, pixel_index, send_list, counts, band_width):
-    acq_loc, local = phases.shape
+    acq_loc = phases.shape[0]
     n_tile = lax.axis_size("tile")
     n_acq = lax.axis_size("acq")
     packed = (n_tile // 2 + 1) * LANES
-    smem = pl.BlockSpec(memory_space=pltpu.SMEM)
     vmem = pl.BlockSpec(memory_space=pltpu.VMEM)
     f32 = jnp.float32
-    packet, own = pl.pallas_call(
-        functools.partial(gather_kernel, n_tile),
+    packet, own = gather_call(phases, coherence, pixel_index, send_list, counts)
+    parts = [xor_permute(packet, "acq", k) for k in range(1, n_acq)]
+    packet_shape = jax.ShapeDtypeStruct((acq_loc, packed + LANES), f32)
+    begun, highpass, down = pl.pallas_call(
+        functools.partial(filter_own_kernel, n_acq),
         out_shape=(
-            jax.ShapeDtypeStruct((acq_loc, packed + LANES), f32),
-            jax.ShapeDtypeStruct((acq_loc, packed), f32),
+            packet_shape,
+            jax.ShapeDtypeStruct((n_acq * acq_loc, acq_loc), f32),
+            jax.ShapeDtypeStruct((3, packed, LANES), f32),
         ),
-        in_specs=[smem, vmem, vmem, vmem, vmem],
-        out_specs=(vmem, vmem),
-        compiler_params=pltpu.CompilerParams(vmem_limit_bytes=56 << 20),
-        name="gather_slots",
-    )(
-        counts,
-        send_list,
-        phases,
-        coherence.reshape(-1, LANES),
-        pixel_index.reshape(-1, LANES),
-    )
-    here = lax.axis_index("acq")
-    parts = [packet] + [xor_permute(packet, "acq", k) for k in range(1, n_acq)]
-    source = here ^ jnp.arange(n_acq, dtype=jnp.int32)
-    column = (source[:, None] * acq_loc + jnp.arange(acq_loc, dtype=jnp.int32)[None]).reshape(1, -1)
-    row = here * acq_loc + jnp.arange(acq_loc, dtype=jnp.int32)
-    band = lax.dynamic_slice_in_dim(band_width, here * acq_loc, acq_loc)
-    lower = jnp.maximum(row - band, 0)[:, None]
-    upper = jnp.minimum(row + band, ACQ - 1)[:, None]
-    inside = ((column >= lower) & (column <= upper)).astype(f32)
-    highpass = (column == row[:, None]).astype(f32) - inside / (upper - lower + 1).astype(f32)
-    packet_shape = jax.ShapeDtypeStruct((acq_loc, packed + LANES), f32)
-    small = pltpu.CompilerParams(vmem_limit_bytes=4 << 20)
-    begun = pl.pallas_call(
-        filter_own_kernel,
-        out_shape=packet_shape,
         in_specs=[vmem] * 2,
-        out_specs=vmem,
+        out_specs=(vmem,) * 3,
         cost_estimate=pl.CostEstimate(flops=1 << 20, bytes_accessed=1 << 20, transcendentals=0),
-        compiler_params=small,
+        compiler_params=pltpu.CompilerParams(vmem_limit_bytes=4 << 20),
         name="filter_own_slots",
-    )(highpass, packet)
+    )(band_width.reshape(1, -1), packet)
     filtered = pl.pallas_call(
         filter_kernel,
         out_shape=packet_shape,
         in_specs=[vmem] * (n_acq + 1),
         out_specs=vmem,
-        compiler_params=small,
+        compiler_params=pltpu.CompilerParams(vmem_limit_bytes=4 << 20),
         name="filter_slots",
-    )(highpass, begun, *parts[1:])
+    )(highpass, begun, *parts)
     half = n_tile // 2
     across = xor_permute(filtered, "tile", half)
-    sums = add_sources(n_tile, filtered[None], filtered, None, None)
+    sums = add_sources(n_tile, filtered[None], filtered, down, None, None)
     across, sums = lax.optimization_barrier((across, sums))
     held = jnp.stack([filtered, across])
     arriving = [across[None]] + [xor_permute(held, "tile", k) for k in range(1, half)]
     for sources in arriving[:-1]:
-        sums = add_sources(n_tile, sources, filtered, sums, None)
-    screen, residual = add_sources(n_tile, arriving[-1], filtered, sums, own)
+        sums = add_sources(n_tile, sources, filtered, down, sums, None)
+    screen, residual = add_sources(n_tile, arriving[-1], filtered, down, sums, own)
     return residual, screen
 
 

time: 28.1 us -> 26.5 us (0.943)
  waiting for transfers between devices: 4.77 us -> 6.59 us
  Pallas kernels: 11.4 us -> 9.66 us
  local copies, waits for them, and re-layouts: 1.54 us -> 0.01 us
    ppermute x7, waiting for transfers between devices: 4.77 us -> 6.59 us  [xor_permute(): return lax.ppermute(x, axis, [(i, i ^ mask) for i in range(count)])]
    unnamed x6 -> x2, local copies, waits for them, and re-layouts: 1.46 us -> 0.01 us
    pallas_call x5, Pallas kernels: 7.73 us -> 6.5 us  [add_sources(): pl.pallas_call(functools.partial(screen_kernel, n_tile, begins, ends), ou...]
    pallas_call x2, Pallas kernels: 3.39 us -> 2.93 us  [the longest x1 2.38 us: gather_call(): pl.pallas_call(gather_kernel, out_shape=(jax.ShapeDtypeStruct((acq_loc, p...]
  transfers between devices with their start and end apart: 7 -> 7, of which waited for: 3 -> 5; matrix products, arithmetic and copies ran while one was open for 1% -> 0% of each run, Pallas kernels for 19% -> 17%
where the time goes in v4:
time: 26.5 us; the launch traced here: 26.3 us
  Pallas kernels  9.66 us (36%)
  starting transfers between devices  9.34 us (35%)
  waiting for transfers between devices  6.59 us (25%)
  between operations  0.7 us (3%)
    ppermute x7, starting transfers between devices, xor_permute(): return lax.ppermute(x, axis, [(i, i ^ mask) for i in range(count)])  9.34 us
    ppermute x7, waiting for transfers between devices, xor_permute(): return lax.ppermute(x, axis, [(i, i ^ mask) for i in range(count)])  6.59 us
    pallas_call x5, Pallas kernels, add_sources(): pl.pallas_call(functools.partial(screen_kernel, n_tile, begins, ends), ou...  6.5 us
    pallas_call x1, Pallas kernels, gather_call(): pl.pallas_call(gather_kernel, out_shape=(jax.ShapeDtypeStruct((acq_loc, p...  2.38 us
    pallas_call x1, Pallas kernels, gathered_shards(): pl.pallas_call(functools.partial(filter_own_kernel, n_acq), out_shape=(pa...  0.55 us
  transfers between devices with their start and end apart: 7, of which 5 were waited for; matrix products, arithmetic and copies ran while one was open for 0% of the time, Pallas kernels for 17%

profile of v4, /device:TPU:0, one launch (start us, length us, event | category | flops | bytes accessed | tf_op | source)
XLA Modules:
  0.0 26.3 jit_solution(940246549712966253)
XLA Ops:
  0.6 2.4 %gather_slots.1 = (f32[16,768]{1,0:T(8,128)S(1)}, f32[16,640]{1,0:T(8,128)S(1)}) custom-call(s32[1,8]{1,0:T(1,128)} %counts_hbm.1, s32[8,128]{1,0:T(8,128)} %list_hbm.1, f32[128,128]{1,0:T(8,128)} %bitcast.10, s32[128,128]{1,0:T(8,128)} %bitcast.11, f32[16,16384]{1,0:T(8,128)} %phases_hbm.1), custom_call_target="tpu_custom_call" | custom-call | tf_op jit(solution)/shard_map/gather_slots/pallas_call | solution.py:257
  3.0 0.0 copy-start
  3.0 2.4 %collective-permute-start.2 = (f32[16,768]{1,0:T(8,128)S(1)}, f32[16,768]{1,0:T(8,128)S(1)}, u32[]{:S(2)}, u32[]{:S(2)}) collective-permute-start(f32[16,768]{1,0:T(8,128)S(1)} %get-tuple-element.20.part_ref), channel_id=1, source_target_pairs={{0,3},{1,2},{2,1},{3,0},{4,7},{5,6},{6,5},{7,4},{8,11},{9,10},{10,... | collective-permute-start | bytes 147464 | tf_op jit(solution)/shard_map/ppermute | solution.py:549
  5.5 0.6 %collective-permute-start.1 = (f32[16,768]{1,0:T(8,128)S(1)}, f32[16,768]{1,0:T(8,128)S(1)}, u32[]{:S(2)}, u32[]{:S(2)}) collective-permute-start(f32[16,768]{1,0:T(8,128)S(1)} %get-tuple-element.20.part_ref), channel_id=1, source_target_pairs={{0,2},{1,3},{2,0},{3,1},{4,6},{5,7},{6,4},{7,5},{8,10},{9,11},{10,... | collective-permute-start | bytes 147464 | tf_op jit(solution)/shard_map/ppermute | solution.py:549
  6.1 0.0 collective-permute-start
  6.1 0.0 copy-done
  6.2 0.6 %filter_own_slots.1 = (f32[16,768]{1,0:T(8,128)S(1)}, f32[64,16]{1,0:T(8,128)S(1)}, f32[3,640,128]{2,1,0:T(8,128)S(1)}) custom-call(s32[1,64]{1,0:T(1,128)S(1)} %bitcast.9, f32[16,768]{1,0:T(8,128)S(1)} %get-tuple-element.20.part_ref), custom_call_target="tpu_custom_call" | custom-call | flops 1048576 | bytes 1048576 | tf_op jit(solution)/shard_map/filter_own_slots/pallas_call | solution.py:562
  6.7 0.9 %collective-permute-done.2.refs_2_ = f32[16,768]{1,0:T(8,128)S(1)} collective-permute-done((f32[16,768]{1,0:T(8,128)S(1)}, f32[16,768]{1,0:T(8,128)S(1)}, u32[]{:S(2)}, u32[]{:S(2)}) %collective-permute-start.2) | collective-permute-done | bytes 49184 | tf_op jit(solution)/shard_map/ppermute | solution.py:549
  7.6 2.2 %collective-permute-done.1.refs_1_ = f32[16,768]{1,0:T(8,128)S(1)} collective-permute-done((f32[16,768]{1,0:T(8,128)S(1)}, f32[16,768]{1,0:T(8,128)S(1)}, u32[]{:S(2)}, u32[]{:S(2)}) %collective-permute-start.1) | collective-permute-done | bytes 49184 | tf_op jit(solution)/shard_map/ppermute | solution.py:549
  9.8 0.0 collective-permute-done.refs_0_
  9.8 0.2 filter_slots.1.refs_1_
  10.0 2.7 %collective-permute-start.3 = (f32[16,768]{1,0:T(8,128)S(1)}, f32[16,768]{1,0:T(8,128)S(1)}, u32[]{:S(2)}, u32[]{:S(2)}) collective-permute-start(f32[16,768]{1,0:T(8,128)S(1)} %filter_slots.1.refs_1_), channel_id=1, source_target_pairs={{0,16},{4,20},{8,24},{12,28},{16,0},{20,4},{24,8},{28,12},{1,17},{... | collective-permute-start | bytes 147464 | tf_op jit(solution)/shard_map/ppermute | solution.py:549
  12.7 0.7 %add_sources.5 = (f32[136,1024]{1,0:T(8,128)S(1)}, f32[24,640]{1,0:T(8,128)S(1)}) custom-call(f32[1,16,768]{2,1,0:T(8,128)S(1)} %bitcast.5, f32[16,768]{1,0:T(8,128)S(1)} %filter_slots.1.refs_1_, f32[3,640,128]{2,1,0:T(8,128)S(1)} %get-tuple-element.23.refs_2_), custom_call_target="tpu_custom_call" | custom-call | flops 237502464 | bytes 1048576 | tf_op jit(solution)/shard_map/add_sources/pallas_call | solution.py:523
  13.4 2.0 %collective-permute-done.3 = f32[16,768]{1,0:T(8,128)S(1)} collective-permute-done((f32[16,768]{1,0:T(8,128)S(1)}, f32[16,768]{1,0:T(8,128)S(1)}, u32[]{:S(2)}, u32[]{:S(2)}) %collective-permute-start.3) | collective-permute-done | bytes 49184 | tf_op jit(solution)/shard_map/ppermute | solution.py:549
  15.5 1.6 %collective-permute-start.6 = (f32[2,16,768]{2,1,0:T(8,128)S(1)}, f32[2,16,768]{2,1,0:T(8,128)S(1)}, u32[]{:S(2)}, u32[]{:S(2)}) collective-permute-start(f32[2,16,768]{2,1,0:T(8,128)S(1)} %pad_maximum_fusion), channel_id=1, source_target_pairs={{0,4},{4,0},{8,12},{12,8},{16,20},{20,16},{24,28},{28,24},{1,5},{5... | collective-permute-start | bytes 294920 | tf_op jit(solution)/shard_map/ppermute | solution.py:549
  17.1 1.2 %collective-permute-start.5 = (f32[2,16,768]{2,1,0:T(8,128)S(1)}, f32[2,16,768]{2,1,0:T(8,128)S(1)}, u32[]{:S(2)}, u32[]{:S(2)}) collective-permute-start(f32[2,16,768]{2,1,0:T(8,128)S(1)} %pad_maximum_fusion), channel_id=1, source_target_pairs={{0,8},{4,12},{8,0},{12,4},{16,24},{20,28},{24,16},{28,20},{1,9},{5... | collective-permute-start | bytes 294920 | tf_op jit(solution)/shard_map/ppermute | solution.py:549
  18.3 0.8 %collective-permute-start.4 = (f32[2,16,768]{2,1,0:T(8,128)S(1)}, f32[2,16,768]{2,1,0:T(8,128)S(1)}, u32[]{:S(2)}, u32[]{:S(2)}) collective-permute-start(f32[2,16,768]{2,1,0:T(8,128)S(1)} %pad_maximum_fusion), channel_id=1, source_target_pairs={{0,12},{4,8},{8,4},{12,0},{16,28},{20,24},{24,20},{28,16},{1,13},{... | collective-permute-start | bytes 294920 | tf_op jit(solution)/shard_map/ppermute | solution.py:549
  19.0 0.8 %add_sources.6 = (f32[136,1024]{1,0:T(8,128)S(1)}, f32[24,640]{1,0:T(8,128)S(1)}) custom-call(f32[1,16,768]{2,1,0:T(8,128)S(1)} %bitcast.8, f32[16,768]{1,0:T(8,128)S(1)} %filter_slots.1.refs_1_, f32[3,640,128]{2,1,0:T(8,128)S(1)} %get-tuple-element.23.refs_2_, ...), custom_call_target="tpu_custom_call", output_to_operand_aliasing={{0}: (3, {}), {1}: (4, {})} | custom-call | flops 237502464 | bytes 1048576 | tf_op jit(solution)/shard_map/add_sources/pallas_call | solution.py:523
  19.9 1.2 %collective-permute-done.6.refs_0_ = f32[2,16,768]{2,1,0:T(8,128)S(1)} collective-permute-done((f32[2,16,768]{2,1,0:T(8,128)S(1)}, f32[2,16,768]{2,1,0:T(8,128)S(1)}, u32[]{:S(2)}, u32[]{:S(2)}) %collective-permute-start.6) | collective-permute-done | bytes 98336 | tf_op jit(solution)/shard_map/ppermute | solution.py:549
  21.1 1.2 %add_sources.7 = (f32[136,1024]{1,0:T(8,128)S(1)}, f32[24,640]{1,0:T(8,128)S(1)}) custom-call(f32[2,16,768]{2,1,0:T(8,128)S(1)} %collective-permute-done.6.refs_0_, f32[16,768]{1,0:T(8,128)S(1)} %filter_slots.1.refs_1_, f32[3,640,128]{2,1,0:T(8,128)S(1)} %get-tuple-element.23.refs_2_, ...), custom_call_target="tpu_custom_call", output_to_operand_aliasing={{0}: (3, {}), {1}: (4, {})} | custom-call | flops 475004928 | bytes 1048576 | tf_op jit(solution)/shard_map/add_sources/pallas_call | solution.py:523
  22.3 0.0 collective-permute-done.5.refs_0_
  22.3 1.2 %add_sources.8 = (f32[136,1024]{1,0:T(8,128)S(1)}, f32[24,640]{1,0:T(8,128)S(1)}) custom-call(f32[2,16,768]{2,1,0:T(8,128)S(1)} %collective-permute-done.5.refs_0_, f32[16,768]{1,0:T(8,128)S(1)} %filter_slots.1.refs_1_, f32[3,640,128]{2,1,0:T(8,128)S(1)} %get-tuple-element.23.refs_2_, ...), custom_call_target="tpu_custom_call", output_to_operand_aliasing={{0}: (3, {}), {1}: (4, {})} | custom-call | flops 475004928 | bytes 1048576 | tf_op jit(solution)/shard_map/add_sources/pallas_call | solution.py:523
  23.5 0.3 %collective-permute-done.4.refs_0_ = f32[2,16,768]{2,1,0:T(8,128)S(1)} collective-permute-done((f32[2,16,768]{2,1,0:T(8,128)S(1)}, f32[2,16,768]{2,1,0:T(8,128)S(1)}, u32[]{:S(2)}, u32[]{:S(2)}) %collective-permute-start.4) | collective-permute-done | bytes 98336 | tf_op jit(solution)/shard_map/ppermute | solution.py:549
  23.8 2.5 %add_sources.9 = (f32[16,8,1024]{2,1,0:T(8,128)}, f32[16,1024]{1,0:T(8,128)}) custom-call(f32[2,16,768]{2,1,0:T(8,128)S(1)} %collective-permute-done.4.refs_0_, f32[16,768]{1,0:T(8,128)S(1)} %filter_slots.1.refs_1_, f32[3,640,128]{2,1,0:T(8,128)S(1)} %get-tuple-element.23.refs_2_, f32[136,1024]{1,0:T(8,128)S(1)} %get-tuple-element.33.refs_3_, ...), custom_call_target="tpu_custom_call" | custom-call | flops 475004928 | bytes 1048576 | tf_op jit(solution)/shard_map/add_sources/pallas_call | solution.py:523
  (1 shorter events, 0.0 us)
Async XLA Ops:
  3.0 3.1 %copy-start = (s32[64]{0:T(128)S(1)}, s32[64]{0:T(128)}, u32[]{:S(2)}) copy-start(s32[64]{0:T(128)} %param.11) | copy-start | bytes 772
  3.0 4.6 %collective-permute-start.2 = (f32[16,768]{1,0:T(8,128)S(1)}, f32[16,768]{1,0:T(8,128)S(1)}, u32[]{:S(2)}, u32[]{:S(2)}) collective-permute-start(f32[16,768]{1,0:T(8,128)S(1)} %get-tuple-element.20.part_ref), channel_id=1, source_target_pairs={{0,3},{1,2},{2,1},{3,0},{4,7},{5,6},{6,5},{7,4},{8,11},{9,10},{10,... | collective-permute-start | bytes 147464 | tf_op jit(solution)/shard_map/ppermute | solution.py:549
  5.5 4.3 %collective-permute-start.1 = (f32[16,768]{1,0:T(8,128)S(1)}, f32[16,768]{1,0:T(8,128)S(1)}, u32[]{:S(2)}, u32[]{:S(2)}) collective-permute-start(f32[16,768]{1,0:T(8,128)S(1)} %get-tuple-element.20.part_ref), channel_id=1, source_target_pairs={{0,2},{1,3},{2,0},{3,1},{4,6},{5,7},{6,4},{7,5},{8,10},{9,11},{10,... | collective-permute-start | bytes 147464 | tf_op jit(solution)/shard_map/ppermute | solution.py:549
  6.1 3.7 %collective-permute-start = (f32[16,768]{1,0:T(8,128)S(1)}, f32[16,768]{1,0:T(8,128)S(1)}, u32[]{:S(2)}, u32[]{:S(2)}) collective-permute-start(f32[16,768]{1,0:T(8,128)S(1)} %get-tuple-element.20.part_ref), channel_id=1, source_target_pairs={{0,1},{1,0},{2,3},{3,2},{4,5},{5,4},{6,7},{7,6},{8,9},{9,8},{10,11... | collective-permute-start | bytes 147464 | tf_op jit(solution)/shard_map/ppermute | solution.py:549
  10.0 5.4 %collective-permute-start.3 = (f32[16,768]{1,0:T(8,128)S(1)}, f32[16,768]{1,0:T(8,128)S(1)}, u32[]{:S(2)}, u32[]{:S(2)}) collective-permute-start(f32[16,768]{1,0:T(8,128)S(1)} %filter_slots.1.refs_1_), channel_id=1, source_target_pairs={{0,16},{4,20},{8,24},{12,28},{16,0},{20,4},{24,8},{28,12},{1,17},{... | collective-permute-start | bytes 147464 | tf_op jit(solution)/shard_map/ppermute | solution.py:549
  15.5 5.6 %collective-permute-start.6 = (f32[2,16,768]{2,1,0:T(8,128)S(1)}, f32[2,16,768]{2,1,0:T(8,128)S(1)}, u32[]{:S(2)}, u32[]{:S(2)}) collective-permute-start(f32[2,16,768]{2,1,0:T(8,128)S(1)} %pad_maximum_fusion), channel_id=1, source_target_pairs={{0,4},{4,0},{8,12},{12,8},{16,20},{20,16},{24,28},{28,24},{1,5},{5... | collective-permute-start | bytes 294920 | tf_op jit(solution)/shard_map/ppermute | solution.py:549
  17.1 5.2 %collective-permute-start.5 = (f32[2,16,768]{2,1,0:T(8,128)S(1)}, f32[2,16,768]{2,1,0:T(8,128)S(1)}, u32[]{:S(2)}, u32[]{:S(2)}) collective-permute-start(f32[2,16,768]{2,1,0:T(8,128)S(1)} %pad_maximum_fusion), channel_id=1, source_target_pairs={{0,8},{4,12},{8,0},{12,4},{16,24},{20,28},{24,16},{28,20},{1,9},{5... | collective-permute-start | bytes 294920 | tf_op jit(solution)/shard_map/ppermute | solution.py:549
  18.3 5.5 %collective-permute-start.4 = (f32[2,16,768]{2,1,0:T(8,128)S(1)}, f32[2,16,768]{2,1,0:T(8,128)S(1)}, u32[]{:S(2)}, u32[]{:S(2)}) collective-permute-start(f32[2,16,768]{2,1,0:T(8,128)S(1)} %pad_maximum_fusion), channel_id=1, source_target_pairs={{0,12},{4,8},{8,4},{12,0},{16,28},{20,24},{24,20},{28,16},{1,13},{... | collective-permute-start | bytes 294920 | tf_op jit(solution)/shard_map/ppermute | solution.py:549

commit v5 on v4

--- a/solution.py
+++ b/solution.py
@@ -12,6 +12,7 @@
 COLS = 1024
 RADIUS = 4
 SLAB_PIX = 8192
+SLAB_SHIFT = 13
 HALF = 64
 LANES = 128
 
@@ -354,7 +355,7 @@
     else:
         image_out, samples_out = refs[:2]
         refs = refs[2:]
-    tag_ref, few_ref, value_ref, lhs_ref, res_ref, made_ref, made_sem = refs
+    tag_ref, few_ref, value_ref, lhs_ref, made_ref, rest_ref, made_sem = refs
     n_src, acq_loc, packed = all_ref.shape
     packed -= LANES
     n_pair = n_tile // 2
@@ -479,26 +480,29 @@
         samples_out[...] = samples
         return
     below = samples[acq_loc : acq_loc + 1] + samples[acq_loc + 1 : acq_loc + 2]
-    res_ref[...] = own_ref[...] - samples[0:acq_loc] * (1.0 / jnp.maximum(below, limit))
+    rest = own_ref[...] - samples[0:acq_loc] * (1.0 / jnp.maximum(below, limit))
 
     lower = lax.broadcasted_iota(jnp.int32, (1, LANES), 1) < HALF
     tiles = [
-        mine_ref[MAX_BLOCKS + b : MAX_BLOCKS + b + 1, packed:].astype(jnp.int32) // SLAB_PIX
+        mine_ref[MAX_BLOCKS + b : MAX_BLOCKS + b + 1, packed:].astype(jnp.int32) >> SLAB_SHIFT
         for b in range(n_pair + 1)
     ]
-    heavy = res_ref[:, n_pair * LANES :]
+    heavy = rest[:, n_pair * LANES :]
     turned = pltpu.roll(heavy, HALF, 1)
     tile_turned = pltpu.roll(tiles[n_pair], HALF, 1)
     for t in range(n_tile):
-        near = res_ref[:, (t // 2) * LANES : (t // 2 + 1) * LANES]
+        near = rest[:, (t // 2) * LANES : (t // 2 + 1) * LANES]
         tile_near = tiles[t // 2]
         if t % 2:
             near = pltpu.roll(near, HALF, 1)
             tile_near = pltpu.roll(tile_near, HALF, 1)
         far = jnp.where(tile_turned == t, turned, jnp.where(tiles[n_pair] == t, heavy, 0.0))
-        residual_ref[:, t * LANES : (t + 1) * LANES] = jnp.where(
+        rest_ref[:, t * LANES : (t + 1) * LANES] = jnp.where(
             lower, jnp.where(tile_near == t, near, 0.0), far
         )
+    rest_copy = pltpu.make_async_copy(rest_ref, residual_ref, made_sem.at[COLS // CHUNK])
+    copies.append(rest_copy)
+    rest_copy.start()
     for copy in copies:
         copy.wait()
 
@@ -524,15 +528,15 @@
         functools.partial(screen_kernel, n_tile, begins, ends),
         out_shape=tuple(jax.ShapeDtypeStruct(shape, f32) for shape in shapes),
         in_specs=[vmem] * len(args),
-        out_specs=(pl.BlockSpec(memory_space=pl.ANY) if ends else vmem, vmem),
+        out_specs=(pl.BlockSpec(memory_space=pl.ANY) if ends else vmem,) * 2,
         scratch_shapes=[
             pltpu.VMEM((n_src, 8, packed), f32),
             pltpu.VMEM((n_src, 3, 16, packed), bf16),
             pltpu.VMEM((n_src, 2 * acq_loc + 16, packed), bf16),
             pltpu.VMEM((n_lhs, width), bf16),
-            pltpu.VMEM((acq_loc, packed), f32),
             pltpu.VMEM((acq_loc, ROWS_DEV, COLS), f32),
-            pltpu.SemaphoreType.DMA((COLS // CHUNK,)),
+            pltpu.VMEM((acq_loc, n_tile * LANES), f32),
+            pltpu.SemaphoreType.DMA((COLS // CHUNK + 1,)),
         ],
         input_output_aliases={} if begins or ends else {3: 0, 4: 1},
         cost_estimate=pl.CostEstimate(flops=2 * macs, bytes_accessed=1 << 20, transcendentals=0),

time: 26.5 us -> 25.9 us (0.977)
  Pallas kernels: 9.66 us -> 9.14 us
    pallas_call x5, Pallas kernels: 6.5 us -> 5.98 us  [add_sources(): pl.pallas_call(functools.partial(screen_kernel, n_tile, begins, ends), ou...]
  transfers between devices with their start and end apart: 7 -> 7, of which waited for: 5 -> 5; matrix products, arithmetic and copies ran while one was open for 0% -> 0% of each run, Pallas kernels for 17% -> 18%
where the time goes in v5:
time: 25.9 us; the launch traced here: 25.7 us
  starting transfers between devices  9.34 us (36%)
  Pallas kernels  9.14 us (35%)
  waiting for transfers between devices  6.55 us (25%)
  between operations  0.7 us (3%)
    ppermute x7, starting transfers between devices, xor_permute(): return lax.ppermute(x, axis, [(i, i ^ mask) for i in range(count)])  9.34 us
    ppermute x7, waiting for transfers between devices, xor_permute(): return lax.ppermute(x, axis, [(i, i ^ mask) for i in range(count)])  6.55 us
    pallas_call x5, Pallas kernels, add_sources(): pl.pallas_call(functools.partial(screen_kernel, n_tile, begins, ends), ou...  5.98 us
    pallas_call x1, Pallas kernels, gather_call(): pl.pallas_call(gather_kernel, out_shape=(jax.ShapeDtypeStruct((acq_loc, p...  2.38 us
    pallas_call x1, Pallas kernels, gathered_shards(): pl.pallas_call(functools.partial(filter_own_kernel, n_acq), out_shape=(pa...  0.55 us
  transfers between devices with their start and end apart: 7, of which 5 were waited for; matrix products, arithmetic and copies ran while one was open for 0% of the time, Pallas kernels for 18%

profile of v5, /device:TPU:0, one launch (start us, length us, event | category | flops | bytes accessed | tf_op | source)
XLA Modules:
  0.0 25.7 jit_solution(17782445794035794286)
XLA Ops:
  0.6 2.4 %gather_slots.1 = (f32[16,768]{1,0:T(8,128)S(1)}, f32[16,640]{1,0:T(8,128)S(1)}) custom-call(s32[1,8]{1,0:T(1,128)} %counts_hbm.1, s32[8,128]{1,0:T(8,128)} %list_hbm.1, f32[128,128]{1,0:T(8,128)} %bitcast.10, s32[128,128]{1,0:T(8,128)} %bitcast.11, f32[16,16384]{1,0:T(8,128)} %phases_hbm.1), custom_call_target="tpu_custom_call" | custom-call | tf_op jit(solution)/shard_map/gather_slots/pallas_call | solution.py:258
  3.0 0.0 copy-start
  3.0 2.4 %collective-permute-start.2 = (f32[16,768]{1,0:T(8,128)S(1)}, f32[16,768]{1,0:T(8,128)S(1)}, u32[]{:S(2)}, u32[]{:S(2)}) collective-permute-start(f32[16,768]{1,0:T(8,128)S(1)} %get-tuple-element.20.part_ref), channel_id=1, source_target_pairs={{0,3},{1,2},{2,1},{3,0},{4,7},{5,6},{6,5},{7,4},{8,11},{9,10},{10,... | collective-permute-start | bytes 147464 | tf_op jit(solution)/shard_map/ppermute | solution.py:553
  5.5 0.6 %collective-permute-start.1 = (f32[16,768]{1,0:T(8,128)S(1)}, f32[16,768]{1,0:T(8,128)S(1)}, u32[]{:S(2)}, u32[]{:S(2)}) collective-permute-start(f32[16,768]{1,0:T(8,128)S(1)} %get-tuple-element.20.part_ref), channel_id=1, source_target_pairs={{0,2},{1,3},{2,0},{3,1},{4,6},{5,7},{6,4},{7,5},{8,10},{9,11},{10,... | collective-permute-start | bytes 147464 | tf_op jit(solution)/shard_map/ppermute | solution.py:553
  6.1 0.0 collective-permute-start
  6.1 0.0 copy-done
  6.2 0.6 %filter_own_slots.1 = (f32[16,768]{1,0:T(8,128)S(1)}, f32[64,16]{1,0:T(8,128)S(1)}, f32[3,640,128]{2,1,0:T(8,128)S(1)}) custom-call(s32[1,64]{1,0:T(1,128)S(1)} %bitcast.9, f32[16,768]{1,0:T(8,128)S(1)} %get-tuple-element.20.part_ref), custom_call_target="tpu_custom_call" | custom-call | flops 1048576 | bytes 1048576 | tf_op jit(solution)/shard_map/filter_own_slots/pallas_call | solution.py:566
  6.7 0.9 %collective-permute-done.2.refs_2_ = f32[16,768]{1,0:T(8,128)S(1)} collective-permute-done((f32[16,768]{1,0:T(8,128)S(1)}, f32[16,768]{1,0:T(8,128)S(1)}, u32[]{:S(2)}, u32[]{:S(2)}) %collective-permute-start.2) | collective-permute-done | bytes 49184 | tf_op jit(solution)/shard_map/ppermute | solution.py:553
  7.6 2.2 %collective-permute-done.1.refs_1_ = f32[16,768]{1,0:T(8,128)S(1)} collective-permute-done((f32[16,768]{1,0:T(8,128)S(1)}, f32[16,768]{1,0:T(8,128)S(1)}, u32[]{:S(2)}, u32[]{:S(2)}) %collective-permute-start.1) | collective-permute-done | bytes 49184 | tf_op jit(solution)/shard_map/ppermute | solution.py:553
  9.8 0.0 collective-permute-done.refs_0_
  9.8 0.2 filter_slots.1.refs_1_
  10.0 2.7 %collective-permute-start.3 = (f32[16,768]{1,0:T(8,128)S(1)}, f32[16,768]{1,0:T(8,128)S(1)}, u32[]{:S(2)}, u32[]{:S(2)}) collective-permute-start(f32[16,768]{1,0:T(8,128)S(1)} %filter_slots.1.refs_1_), channel_id=1, source_target_pairs={{0,16},{4,20},{8,24},{12,28},{16,0},{20,4},{24,8},{28,12},{1,17},{... | collective-permute-start | bytes 147464 | tf_op jit(solution)/shard_map/ppermute | solution.py:553
  12.7 0.8 %add_sources.5 = (f32[136,1024]{1,0:T(8,128)S(1)}, f32[24,640]{1,0:T(8,128)S(1)}) custom-call(f32[1,16,768]{2,1,0:T(8,128)S(1)} %bitcast.5, f32[16,768]{1,0:T(8,128)S(1)} %filter_slots.1.refs_1_, f32[3,640,128]{2,1,0:T(8,128)S(1)} %get-tuple-element.23.refs_2_), custom_call_target="tpu_custom_call" | custom-call | flops 237502464 | bytes 1048576 | tf_op jit(solution)/shard_map/add_sources/pallas_call | solution.py:527
  13.5 2.0 %collective-permute-done.3 = f32[16,768]{1,0:T(8,128)S(1)} collective-permute-done((f32[16,768]{1,0:T(8,128)S(1)}, f32[16,768]{1,0:T(8,128)S(1)}, u32[]{:S(2)}, u32[]{:S(2)}) %collective-permute-start.3) | collective-permute-done | bytes 49184 | tf_op jit(solution)/shard_map/ppermute | solution.py:553
  15.5 1.6 %collective-permute-start.6 = (f32[2,16,768]{2,1,0:T(8,128)S(1)}, f32[2,16,768]{2,1,0:T(8,128)S(1)}, u32[]{:S(2)}, u32[]{:S(2)}) collective-permute-start(f32[2,16,768]{2,1,0:T(8,128)S(1)} %pad_maximum_fusion), channel_id=1, source_target_pairs={{0,4},{4,0},{8,12},{12,8},{16,20},{20,16},{24,28},{28,24},{1,5},{5... | collective-permute-start | bytes 294920 | tf_op jit(solution)/shard_map/ppermute | solution.py:553
  17.1 1.2 %collective-permute-start.5 = (f32[2,16,768]{2,1,0:T(8,128)S(1)}, f32[2,16,768]{2,1,0:T(8,128)S(1)}, u32[]{:S(2)}, u32[]{:S(2)}) collective-permute-start(f32[2,16,768]{2,1,0:T(8,128)S(1)} %pad_maximum_fusion), channel_id=1, source_target_pairs={{0,8},{4,12},{8,0},{12,4},{16,24},{20,28},{24,16},{28,20},{1,9},{5... | collective-permute-start | bytes 294920 | tf_op jit(solution)/shard_map/ppermute | solution.py:553
  18.3 0.8 %collective-permute-start.4 = (f32[2,16,768]{2,1,0:T(8,128)S(1)}, f32[2,16,768]{2,1,0:T(8,128)S(1)}, u32[]{:S(2)}, u32[]{:S(2)}) collective-permute-start(f32[2,16,768]{2,1,0:T(8,128)S(1)} %pad_maximum_fusion), channel_id=1, source_target_pairs={{0,12},{4,8},{8,4},{12,0},{16,28},{20,24},{24,20},{28,16},{1,13},{... | collective-permute-start | bytes 294920 | tf_op jit(solution)/shard_map/ppermute | solution.py:553
  19.0 0.8 %add_sources.6 = (f32[136,1024]{1,0:T(8,128)S(1)}, f32[24,640]{1,0:T(8,128)S(1)}) custom-call(f32[1,16,768]{2,1,0:T(8,128)S(1)} %bitcast.8, f32[16,768]{1,0:T(8,128)S(1)} %filter_slots.1.refs_1_, f32[3,640,128]{2,1,0:T(8,128)S(1)} %get-tuple-element.23.refs_2_, ...), custom_call_target="tpu_custom_call", output_to_operand_aliasing={{0}: (3, {}), {1}: (4, {})} | custom-call | flops 237502464 | bytes 1048576 | tf_op jit(solution)/shard_map/add_sources/pallas_call | solution.py:527
  19.9 1.2 %collective-permute-done.6.refs_0_ = f32[2,16,768]{2,1,0:T(8,128)S(1)} collective-permute-done((f32[2,16,768]{2,1,0:T(8,128)S(1)}, f32[2,16,768]{2,1,0:T(8,128)S(1)}, u32[]{:S(2)}, u32[]{:S(2)}) %collective-permute-start.6) | collective-permute-done | bytes 98336 | tf_op jit(solution)/shard_map/ppermute | solution.py:553
  21.1 1.2 %add_sources.7 = (f32[136,1024]{1,0:T(8,128)S(1)}, f32[24,640]{1,0:T(8,128)S(1)}) custom-call(f32[2,16,768]{2,1,0:T(8,128)S(1)} %collective-permute-done.6.refs_0_, f32[16,768]{1,0:T(8,128)S(1)} %filter_slots.1.refs_1_, f32[3,640,128]{2,1,0:T(8,128)S(1)} %get-tuple-element.23.refs_2_, ...), custom_call_target="tpu_custom_call", output_to_operand_aliasing={{0}: (3, {}), {1}: (4, {})} | custom-call | flops 475004928 | bytes 1048576 | tf_op jit(solution)/shard_map/add_sources/pallas_call | solution.py:527
  22.3 0.0 collective-permute-done.5.refs_0_
  22.3 1.2 %add_sources.8 = (f32[136,1024]{1,0:T(8,128)S(1)}, f32[24,640]{1,0:T(8,128)S(1)}) custom-call(f32[2,16,768]{2,1,0:T(8,128)S(1)} %collective-permute-done.5.refs_0_, f32[16,768]{1,0:T(8,128)S(1)} %filter_slots.1.refs_1_, f32[3,640,128]{2,1,0:T(8,128)S(1)} %get-tuple-element.23.refs_2_, ...), custom_call_target="tpu_custom_call", output_to_operand_aliasing={{0}: (3, {}), {1}: (4, {})} | custom-call | flops 475004928 | bytes 1048576 | tf_op jit(solution)/shard_map/add_sources/pallas_call | solution.py:527
  23.5 0.3 %collective-permute-done.4.refs_0_ = f32[2,16,768]{2,1,0:T(8,128)S(1)} collective-permute-done((f32[2,16,768]{2,1,0:T(8,128)S(1)}, f32[2,16,768]{2,1,0:T(8,128)S(1)}, u32[]{:S(2)}, u32[]{:S(2)}) %collective-permute-start.4) | collective-permute-done | bytes 98336 | tf_op jit(solution)/shard_map/ppermute | solution.py:553
  23.8 2.0 %add_sources.9 = (f32[16,8,1024]{2,1,0:T(8,128)}, f32[16,1024]{1,0:T(8,128)}) custom-call(f32[2,16,768]{2,1,0:T(8,128)S(1)} %collective-permute-done.4.refs_0_, f32[16,768]{1,0:T(8,128)S(1)} %filter_slots.1.refs_1_, f32[3,640,128]{2,1,0:T(8,128)S(1)} %get-tuple-element.23.refs_2_, f32[136,1024]{1,0:T(8,128)S(1)} %get-tuple-element.33.refs_3_, ...), custom_call_target="tpu_custom_call" | custom-call | flops 475004928 | bytes 1048576 | tf_op jit(solution)/shard_map/add_sources/pallas_call | solution.py:527
  (1 shorter events, 0.0 us)
Async XLA Ops:
  3.0 3.1 %copy-start = (s32[64]{0:T(128)S(1)}, s32[64]{0:T(128)}, u32[]{:S(2)}) copy-start(s32[64]{0:T(128)} %param.11) | copy-start | bytes 772
  3.0 4.6 %collective-permute-start.2 = (f32[16,768]{1,0:T(8,128)S(1)}, f32[16,768]{1,0:T(8,128)S(1)}, u32[]{:S(2)}, u32[]{:S(2)}) collective-permute-start(f32[16,768]{1,0:T(8,128)S(1)} %get-tuple-element.20.part_ref), channel_id=1, source_target_pairs={{0,3},{1,2},{2,1},{3,0},{4,7},{5,6},{6,5},{7,4},{8,11},{9,10},{10,... | collective-permute-start | bytes 147464 | tf_op jit(solution)/shard_map/ppermute | solution.py:553
  5.5 4.3 %collective-permute-start.1 = (f32[16,768]{1,0:T(8,128)S(1)}, f32[16,768]{1,0:T(8,128)S(1)}, u32[]{:S(2)}, u32[]{:S(2)}) collective-permute-start(f32[16,768]{1,0:T(8,128)S(1)} %get-tuple-element.20.part_ref), channel_id=1, source_target_pairs={{0,2},{1,3},{2,0},{3,1},{4,6},{5,7},{6,4},{7,5},{8,10},{9,11},{10,... | collective-permute-start | bytes 147464 | tf_op jit(solution)/shard_map/ppermute | solution.py:553
  6.1 3.7 %collective-permute-start = (f32[16,768]{1,0:T(8,128)S(1)}, f32[16,768]{1,0:T(8,128)S(1)}, u32[]{:S(2)}, u32[]{:S(2)}) collective-permute-start(f32[16,768]{1,0:T(8,128)S(1)} %get-tuple-element.20.part_ref), channel_id=1, source_target_pairs={{0,1},{1,0},{2,3},{3,2},{4,5},{5,4},{6,7},{7,6},{8,9},{9,8},{10,11... | collective-permute-start | bytes 147464 | tf_op jit(solution)/shard_map/ppermute | solution.py:553
  10.0 5.4 %collective-permute-start.3 = (f32[16,768]{1,0:T(8,128)S(1)}, f32[16,768]{1,0:T(8,128)S(1)}, u32[]{:S(2)}, u32[]{:S(2)}) collective-permute-start(f32[16,768]{1,0:T(8,128)S(1)} %filter_slots.1.refs_1_), channel_id=1, source_target_pairs={{0,16},{4,20},{8,24},{12,28},{16,0},{20,4},{24,8},{28,12},{1,17},{... | collective-permute-start | bytes 147464 | tf_op jit(solution)/shard_map/ppermute | solution.py:553
  15.5 5.6 %collective-permute-start.6 = (f32[2,16,768]{2,1,0:T(8,128)S(1)}, f32[2,16,768]{2,1,0:T(8,128)S(1)}, u32[]{:S(2)}, u32[]{:S(2)}) collective-permute-start(f32[2,16,768]{2,1,0:T(8,128)S(1)} %pad_maximum_fusion), channel_id=1, source_target_pairs={{0,4},{4,0},{8,12},{12,8},{16,20},{20,16},{24,28},{28,24},{1,5},{5... | collective-permute-start | bytes 294920 | tf_op jit(solution)/shard_map/ppermute | solution.py:553
  17.1 5.2 %collective-permute-start.5 = (f32[2,16,768]{2,1,0:T(8,128)S(1)}, f32[2,16,768]{2,1,0:T(8,128)S(1)}, u32[]{:S(2)}, u32[]{:S(2)}) collective-permute-start(f32[2,16,768]{2,1,0:T(8,128)S(1)} %pad_maximum_fusion), channel_id=1, source_target_pairs={{0,8},{4,12},{8,0},{12,4},{16,24},{20,28},{24,16},{28,20},{1,9},{5... | collective-permute-start | bytes 294920 | tf_op jit(solution)/shard_map/ppermute | solution.py:553
  18.3 5.5 %collective-permute-start.4 = (f32[2,16,768]{2,1,0:T(8,128)S(1)}, f32[2,16,768]{2,1,0:T(8,128)S(1)}, u32[]{:S(2)}, u32[]{:S(2)}) collective-permute-start(f32[2,16,768]{2,1,0:T(8,128)S(1)} %pad_maximum_fusion), channel_id=1, source_target_pairs={{0,12},{4,8},{8,4},{12,0},{16,28},{20,24},{24,20},{28,16},{1,13},{... | collective-permute-start | bytes 294920 | tf_op jit(solution)/shard_map/ppermute | solution.py:553

commit v6 on v5

--- a/solution.py
+++ b/solution.py
@@ -410,16 +410,16 @@
         w_hi = w_part.astype(bf16).astype(f32)
         lhs_ref[2 * n_img :, lanes] = jnp.concatenate([w_hi, w_part - w_hi], 0).astype(bf16)
 
-    def pair_hats(start):
+    def pair_hats(start, columns):
         slots = slice(start, start + HALF)
-        near = range(n_pair + 1)
+        near = columns
         if start < n_pair * LANES:
             tile = start // HALF
             near = {(tile - 1) // 2, tile // 2, (tile + 1) // 2, n_pair}
+        row_i, coarse_i, fine_i = (down_ref[k, slots, :].astype(bf16) for k in range(3))
         blocks = []
-        row_i, coarse_i, fine_i = (down_ref[k, slots, :].astype(bf16) for k in range(3))
         for src in range(n_src):
-            for b in range(n_pair + 1):
+            for b in columns:
                 if b not in near:
                     blocks.append(jnp.zeros((HALF, LANES), bf16))
                     continue
@@ -429,16 +429,32 @@
                 )
                 across = (coarse_i - coarse) + (fine_i - fine)
                 blocks.append(hat_bf16(row_i - row) * hat_bf16(across))
-
         return jnp.concatenate(blocks, 1)
 
     def sample():
-        pairs = jnp.concatenate([pair_hats(at) for at in range(0, packed, HALF)], 0)
-        values = jnp.concatenate([value_ref[src] for src in range(n_src)], 1)
-        got = dot_f32(values, pairs, NT)
-        total = got[0:acq_loc] + got[acq_loc : 2 * acq_loc]
-        below = got[2 * acq_loc : 2 * acq_loc + 8]
-        return jnp.concatenate([total, below], 0)
+        every = list(range(n_pair + 1))
+        parts = []
+        for i in range(0, n_pair + 1, 2):
+            if i < n_pair:
+                columns = list(range(max(i - 1, 0), min(i + 3, n_pair))) + [n_pair]
+                stop = min(i + 2, n_pair)
+            else:
+                columns, stop = every, i + 1
+            starts = range(i * LANES, stop * LANES, HALF)
+            pairs = jnp.concatenate([pair_hats(start, columns) for start in starts], 0)
+            values = jnp.concatenate(
+                [
+                    value_ref[src, :, b * LANES : (b + 1) * LANES]
+                    for src in range(n_src)
+                    for b in columns
+                ],
+                1,
+            )
+            got = dot_f32(values, pairs, NT)
+            total = got[0:acq_loc] + got[acq_loc : 2 * acq_loc]
+            below = got[2 * acq_loc : 2 * acq_loc + 8]
+            parts.append(jnp.concatenate([total, below], 0))
+        return jnp.concatenate(parts, 1)
 
     def slab(c):
         cols = []
@@ -589,7 +605,7 @@
     sums = add_sources(n_tile, filtered[None], filtered, down, None, None)
     across, sums = lax.optimization_barrier((across, sums))
     held = jnp.stack([filtered, across])
-    arriving = [across[None]] + [xor_permute(held, "tile", k) for k in range(1, half)]
+    arriving = [across[None]] + [xor_permute(held, "tile", k) for k in (2,3,1)]
     for sources in arriving[:-1]:
         sums = add_sources(n_tile, sources, filtered, down, sums, None)
     screen, residual = add_sources(n_tile, arriving[-1], filtered, down, sums, own)

time: 25.9 us -> 25.6 us (0.988)
  no operation moved by 1% of the time
where the time goes in v6:
time: 25.6 us; the launch traced here: 25.4 us
  starting transfers between devices  9.34 us (36%)
  Pallas kernels  9.03 us (35%)
  waiting for transfers between devices  6.34 us (25%)
  between operations  0.7 us (3%)
    ppermute x7, starting transfers between devices, xor_permute(): return lax.ppermute(x, axis, [(i, i ^ mask) for i in range(count)])  9.34 us
    ppermute x7, waiting for transfers between devices, xor_permute(): return lax.ppermute(x, axis, [(i, i ^ mask) for i in range(count)])  6.34 us
    pallas_call x5, Pallas kernels, add_sources(): pl.pallas_call(functools.partial(screen_kernel, n_tile, begins, ends), ou...  5.87 us
    pallas_call x1, Pallas kernels, gather_call(): pl.pallas_call(gather_kernel, out_shape=(jax.ShapeDtypeStruct((acq_loc, p...  2.38 us
    pallas_call x1, Pallas kernels, gathered_shards(): pl.pallas_call(functools.partial(filter_own_kernel, n_acq), out_shape=(pa...  0.55 us
  transfers between devices with their start and end apart: 7, of which 5 were waited for; matrix products, arithmetic and copies ran while one was open for 0% of the time, Pallas kernels for 18%

profile of v6, /device:TPU:0, one launch (start us, length us, event | category | flops | bytes accessed | tf_op | source)
XLA Modules:
  0.0 25.4 jit_solution(13328548076825480885)
XLA Ops:
  0.6 2.4 %gather_slots.1 = (f32[16,768]{1,0:T(8,128)S(1)}, f32[16,640]{1,0:T(8,128)S(1)}) custom-call(s32[1,8]{1,0:T(1,128)} %counts_hbm.1, s32[8,128]{1,0:T(8,128)} %list_hbm.1, f32[128,128]{1,0:T(8,128)} %bitcast.10, s32[128,128]{1,0:T(8,128)} %bitcast.11, f32[16,16384]{1,0:T(8,128)} %phases_hbm.1), custom_call_target="tpu_custom_call" | custom-call | tf_op jit(solution)/shard_map/gather_slots/pallas_call | solution.py:258
  3.0 0.0 copy-start
  3.0 2.4 %collective-permute-start.2 = (f32[16,768]{1,0:T(8,128)S(1)}, f32[16,768]{1,0:T(8,128)S(1)}, u32[]{:S(2)}, u32[]{:S(2)}) collective-permute-start(f32[16,768]{1,0:T(8,128)S(1)} %get-tuple-element.20.part_ref), channel_id=1, source_target_pairs={{0,3},{1,2},{2,1},{3,0},{4,7},{5,6},{6,5},{7,4},{8,11},{9,10},{10,... | collective-permute-start | bytes 147464 | tf_op jit(solution)/shard_map/ppermute | solution.py:569
  5.5 0.6 %collective-permute-start.1 = (f32[16,768]{1,0:T(8,128)S(1)}, f32[16,768]{1,0:T(8,128)S(1)}, u32[]{:S(2)}, u32[]{:S(2)}) collective-permute-start(f32[16,768]{1,0:T(8,128)S(1)} %get-tuple-element.20.part_ref), channel_id=1, source_target_pairs={{0,2},{1,3},{2,0},{3,1},{4,6},{5,7},{6,4},{7,5},{8,10},{9,11},{10,... | collective-permute-start | bytes 147464 | tf_op jit(solution)/shard_map/ppermute | solution.py:569
  6.1 0.0 collective-permute-start
  6.1 0.0 copy-done
  6.2 0.6 %filter_own_slots.1 = (f32[16,768]{1,0:T(8,128)S(1)}, f32[64,16]{1,0:T(8,128)S(1)}, f32[3,640,128]{2,1,0:T(8,128)S(1)}) custom-call(s32[1,64]{1,0:T(1,128)S(1)} %bitcast.9, f32[16,768]{1,0:T(8,128)S(1)} %get-tuple-element.20.part_ref), custom_call_target="tpu_custom_call" | custom-call | flops 1048576 | bytes 1048576 | tf_op jit(solution)/shard_map/filter_own_slots/pallas_call | solution.py:582
  6.7 0.9 %collective-permute-done.2.refs_2_ = f32[16,768]{1,0:T(8,128)S(1)} collective-permute-done((f32[16,768]{1,0:T(8,128)S(1)}, f32[16,768]{1,0:T(8,128)S(1)}, u32[]{:S(2)}, u32[]{:S(2)}) %collective-permute-start.2) | collective-permute-done | bytes 49184 | tf_op jit(solution)/shard_map/ppermute | solution.py:569
  7.6 2.2 %collective-permute-done.1.refs_1_ = f32[16,768]{1,0:T(8,128)S(1)} collective-permute-done((f32[16,768]{1,0:T(8,128)S(1)}, f32[16,768]{1,0:T(8,128)S(1)}, u32[]{:S(2)}, u32[]{:S(2)}) %collective-permute-start.1) | collective-permute-done | bytes 49184 | tf_op jit(solution)/shard_map/ppermute | solution.py:569
  9.8 0.0 collective-permute-done.refs_0_
  9.8 0.2 filter_slots.1.refs_1_
  10.0 2.7 %collective-permute-start.3 = (f32[16,768]{1,0:T(8,128)S(1)}, f32[16,768]{1,0:T(8,128)S(1)}, u32[]{:S(2)}, u32[]{:S(2)}) collective-permute-start(f32[16,768]{1,0:T(8,128)S(1)} %filter_slots.1.refs_1_), channel_id=1, source_target_pairs={{0,16},{4,20},{8,24},{12,28},{16,0},{20,4},{24,8},{28,12},{1,17},{... | collective-permute-start | bytes 147464 | tf_op jit(solution)/shard_map/ppermute | solution.py:569
  12.7 0.7 %add_sources.5 = (f32[136,1024]{1,0:T(8,128)S(1)}, f32[24,640]{1,0:T(8,128)S(1)}) custom-call(f32[1,16,768]{2,1,0:T(8,128)S(1)} %bitcast.5, f32[16,768]{1,0:T(8,128)S(1)} %filter_slots.1.refs_1_, f32[3,640,128]{2,1,0:T(8,128)S(1)} %get-tuple-element.23.refs_2_), custom_call_target="tpu_custom_call" | custom-call | flops 237502464 | bytes 1048576 | tf_op jit(solution)/shard_map/add_sources/pallas_call | solution.py:543
  13.4 2.1 %collective-permute-done.3 = f32[16,768]{1,0:T(8,128)S(1)} collective-permute-done((f32[16,768]{1,0:T(8,128)S(1)}, f32[16,768]{1,0:T(8,128)S(1)}, u32[]{:S(2)}, u32[]{:S(2)}) %collective-permute-start.3) | collective-permute-done | bytes 49184 | tf_op jit(solution)/shard_map/ppermute | solution.py:569
  15.5 1.3 %collective-permute-start.6 = (f32[2,16,768]{2,1,0:T(8,128)S(1)}, f32[2,16,768]{2,1,0:T(8,128)S(1)}, u32[]{:S(2)}, u32[]{:S(2)}) collective-permute-start(f32[2,16,768]{2,1,0:T(8,128)S(1)} %pad_maximum_fusion), channel_id=1, source_target_pairs={{0,8},{4,12},{8,0},{12,4},{16,24},{20,28},{24,16},{28,20},{1,9},{5... | collective-permute-start | bytes 294920 | tf_op jit(solution)/shard_map/ppermute | solution.py:569
  16.7 1.8 %collective-permute-start.5 = (f32[2,16,768]{2,1,0:T(8,128)S(1)}, f32[2,16,768]{2,1,0:T(8,128)S(1)}, u32[]{:S(2)}, u32[]{:S(2)}) collective-permute-start(f32[2,16,768]{2,1,0:T(8,128)S(1)} %pad_maximum_fusion), channel_id=1, source_target_pairs={{0,12},{4,8},{8,4},{12,0},{16,28},{20,24},{24,20},{28,16},{1,13},{... | collective-permute-start | bytes 294920 | tf_op jit(solution)/shard_map/ppermute | solution.py:569
  18.5 0.5 %collective-permute-start.4 = (f32[2,16,768]{2,1,0:T(8,128)S(1)}, f32[2,16,768]{2,1,0:T(8,128)S(1)}, u32[]{:S(2)}, u32[]{:S(2)}) collective-permute-start(f32[2,16,768]{2,1,0:T(8,128)S(1)} %pad_maximum_fusion), channel_id=1, source_target_pairs={{0,4},{4,0},{8,12},{12,8},{16,20},{20,16},{24,28},{28,24},{1,5},{5... | collective-permute-start | bytes 294920 | tf_op jit(solution)/shard_map/ppermute | solution.py:569
  19.0 0.8 %add_sources.6 = (f32[136,1024]{1,0:T(8,128)S(1)}, f32[24,640]{1,0:T(8,128)S(1)}) custom-call(f32[1,16,768]{2,1,0:T(8,128)S(1)} %bitcast.8, f32[16,768]{1,0:T(8,128)S(1)} %filter_slots.1.refs_1_, f32[3,640,128]{2,1,0:T(8,128)S(1)} %get-tuple-element.23.refs_2_, ...), custom_call_target="tpu_custom_call", output_to_operand_aliasing={{0}: (3, {}), {1}: (4, {})} | custom-call | flops 237502464 | bytes 1048576 | tf_op jit(solution)/shard_map/add_sources/pallas_call | solution.py:543
  19.9 0.9 %collective-permute-done.6.refs_0_ = f32[2,16,768]{2,1,0:T(8,128)S(1)} collective-permute-done((f32[2,16,768]{2,1,0:T(8,128)S(1)}, f32[2,16,768]{2,1,0:T(8,128)S(1)}, u32[]{:S(2)}, u32[]{:S(2)}) %collective-permute-start.6) | collective-permute-done | bytes 98336 | tf_op jit(solution)/shard_map/ppermute | solution.py:569
  20.8 1.2 %add_sources.7 = (f32[136,1024]{1,0:T(8,128)S(1)}, f32[24,640]{1,0:T(8,128)S(1)}) custom-call(f32[2,16,768]{2,1,0:T(8,128)S(1)} %collective-permute-done.6.refs_0_, f32[16,768]{1,0:T(8,128)S(1)} %filter_slots.1.refs_1_, f32[3,640,128]{2,1,0:T(8,128)S(1)} %get-tuple-element.23.refs_2_, ...), custom_call_target="tpu_custom_call", output_to_operand_aliasing={{0}: (3, {}), {1}: (4, {})} | custom-call | flops 475004928 | bytes 1048576 | tf_op jit(solution)/shard_map/add_sources/pallas_call | solution.py:543
  22.0 0.2 collective-permute-done.5.refs_0_
  22.3 1.2 %add_sources.8 = (f32[136,1024]{1,0:T(8,128)S(1)}, f32[24,640]{1,0:T(8,128)S(1)}) custom-call(f32[2,16,768]{2,1,0:T(8,128)S(1)} %collective-permute-done.5.refs_0_, f32[16,768]{1,0:T(8,128)S(1)} %filter_slots.1.refs_1_, f32[3,640,128]{2,1,0:T(8,128)S(1)} %get-tuple-element.23.refs_2_, ...), custom_call_target="tpu_custom_call", output_to_operand_aliasing={{0}: (3, {}), {1}: (4, {})} | custom-call | flops 475004928 | bytes 1048576 | tf_op jit(solution)/shard_map/add_sources/pallas_call | solution.py:543
  23.5 0.0 collective-permute-done.4.refs_0_
  23.5 1.9 %add_sources.9 = (f32[16,8,1024]{2,1,0:T(8,128)}, f32[16,1024]{1,0:T(8,128)}) custom-call(f32[2,16,768]{2,1,0:T(8,128)S(1)} %collective-permute-done.4.refs_0_, f32[16,768]{1,0:T(8,128)S(1)} %filter_slots.1.refs_1_, f32[3,640,128]{2,1,0:T(8,128)S(1)} %get-tuple-element.23.refs_2_, f32[136,1024]{1,0:T(8,128)S(1)} %get-tuple-element.33.refs_3_, ...), custom_call_target="tpu_custom_call" | custom-call | flops 475004928 | bytes 1048576 | tf_op jit(solution)/shard_map/add_sources/pallas_call | solution.py:543
  (1 shorter events, 0.0 us)
Async XLA Ops:
  3.0 3.1 %copy-start = (s32[64]{0:T(128)S(1)}, s32[64]{0:T(128)}, u32[]{:S(2)}) copy-start(s32[64]{0:T(128)} %param.11) | copy-start | bytes 772
  3.0 4.6 %collective-permute-start.2 = (f32[16,768]{1,0:T(8,128)S(1)}, f32[16,768]{1,0:T(8,128)S(1)}, u32[]{:S(2)}, u32[]{:S(2)}) collective-permute-start(f32[16,768]{1,0:T(8,128)S(1)} %get-tuple-element.20.part_ref), channel_id=1, source_target_pairs={{0,3},{1,2},{2,1},{3,0},{4,7},{5,6},{6,5},{7,4},{8,11},{9,10},{10,... | collective-permute-start | bytes 147464 | tf_op jit(solution)/shard_map/ppermute | solution.py:569
  5.5 4.3 %collective-permute-start.1 = (f32[16,768]{1,0:T(8,128)S(1)}, f32[16,768]{1,0:T(8,128)S(1)}, u32[]{:S(2)}, u32[]{:S(2)}) collective-permute-start(f32[16,768]{1,0:T(8,128)S(1)} %get-tuple-element.20.part_ref), channel_id=1, source_target_pairs={{0,2},{1,3},{2,0},{3,1},{4,6},{5,7},{6,4},{7,5},{8,10},{9,11},{10,... | collective-permute-start | bytes 147464 | tf_op jit(solution)/shard_map/ppermute | solution.py:569
  6.1 3.7 %collective-permute-start = (f32[16,768]{1,0:T(8,128)S(1)}, f32[16,768]{1,0:T(8,128)S(1)}, u32[]{:S(2)}, u32[]{:S(2)}) collective-permute-start(f32[16,768]{1,0:T(8,128)S(1)} %get-tuple-element.20.part_ref), channel_id=1, source_target_pairs={{0,1},{1,0},{2,3},{3,2},{4,5},{5,4},{6,7},{7,6},{8,9},{9,8},{10,11... | collective-permute-start | bytes 147464 | tf_op jit(solution)/shard_map/ppermute | solution.py:569
  10.0 5.4 %collective-permute-start.3 = (f32[16,768]{1,0:T(8,128)S(1)}, f32[16,768]{1,0:T(8,128)S(1)}, u32[]{:S(2)}, u32[]{:S(2)}) collective-permute-start(f32[16,768]{1,0:T(8,128)S(1)} %filter_slots.1.refs_1_), channel_id=1, source_target_pairs={{0,16},{4,20},{8,24},{12,28},{16,0},{20,4},{24,8},{28,12},{1,17},{... | collective-permute-start | bytes 147464 | tf_op jit(solution)/shard_map/ppermute | solution.py:569
  15.5 5.3 %collective-permute-start.6 = (f32[2,16,768]{2,1,0:T(8,128)S(1)}, f32[2,16,768]{2,1,0:T(8,128)S(1)}, u32[]{:S(2)}, u32[]{:S(2)}) collective-permute-start(f32[2,16,768]{2,1,0:T(8,128)S(1)} %pad_maximum_fusion), channel_id=1, source_target_pairs={{0,8},{4,12},{8,0},{12,4},{16,24},{20,28},{24,16},{28,20},{1,9},{5... | collective-permute-start | bytes 294920 | tf_op jit(solution)/shard_map/ppermute | solution.py:569
  16.7 5.5 %collective-permute-start.5 = (f32[2,16,768]{2,1,0:T(8,128)S(1)}, f32[2,16,768]{2,1,0:T(8,128)S(1)}, u32[]{:S(2)}, u32[]{:S(2)}) collective-permute-start(f32[2,16,768]{2,1,0:T(8,128)S(1)} %pad_maximum_fusion), channel_id=1, source_target_pairs={{0,12},{4,8},{8,4},{12,0},{16,28},{20,24},{24,20},{28,16},{1,13},{... | collective-permute-start | bytes 294920 | tf_op jit(solution)/shard_map/ppermute | solution.py:569
  18.5 5.0 %collective-permute-start.4 = (f32[2,16,768]{2,1,0:T(8,128)S(1)}, f32[2,16,768]{2,1,0:T(8,128)S(1)}, u32[]{:S(2)}, u32[]{:S(2)}) collective-permute-start(f32[2,16,768]{2,1,0:T(8,128)S(1)} %pad_maximum_fusion), channel_id=1, source_target_pairs={{0,4},{4,0},{8,12},{12,8},{16,20},{20,16},{24,28},{28,24},{1,5},{5... | collective-permute-start | bytes 294920 | tf_op jit(solution)/shard_map/ppermute | solution.py:569

commit v7 on v6

--- a/solution.py
+++ b/solution.py
@@ -175,7 +175,7 @@
 
 
 def gather_kernel(
-    counts_hbm, list_hbm, coh_hbm, pix_hbm, phases_hbm, out_ref, own_ref,
+    counts_hbm, list_hbm, coh_hbm, pix_hbm, phases_hbm, out_ref, tags_ref, own_ref,
     counts_ref, list_ref, coh_ref, pix_ref, phases_ref, sems,
 ):
     acq_loc, local = phases_ref.shape
@@ -231,11 +231,11 @@
     weight = pick(0) * live
     pixel = pick(1) + tile.astype(jnp.float32) * float(SLAB_PIX)
     pixel = jnp.where(live > 0.0, pixel, float(NOWHERE))
-    out_ref[:, packed:] = jnp.zeros((acq_loc, LANES), jnp.float32)
+    tags_ref[...] = jnp.zeros(tags_ref.shape, jnp.float32)
     for b in range(packed // LANES):
         cut = slice(b * LANES, (b + 1) * LANES)
-        out_ref[b : b + 1, packed:] = weight[:, cut]
-        out_ref[MAX_BLOCKS + b : MAX_BLOCKS + b + 1, packed:] = pixel[:, cut]
+        tags_ref[b : b + 1, :] = weight[:, cut]
+        tags_ref[MAX_BLOCKS + b : MAX_BLOCKS + b + 1, :] = pixel[:, cut]
     own = jnp.zeros((acq_loc, packed), jnp.float32)
     for start in range(0, pieces, step):
         copies[4 + start // step].wait()
@@ -246,7 +246,7 @@
         for h in range(step):
             own = jnp.where(high == start + h, both[h * acq_loc : (h + 1) * acq_loc], own)
     own_ref[...] = own
-    out_ref[:, 0:packed] = own * weight
+    out_ref[...] = own * weight
 
 
 def gather_call(phases, coherence, pixel_index, send_list, counts):
@@ -258,11 +258,12 @@
     return pl.pallas_call(
         gather_kernel,
         out_shape=(
-            jax.ShapeDtypeStruct((acq_loc, packed + LANES), f32),
+            jax.ShapeDtypeStruct((acq_loc, packed), f32),
+            jax.ShapeDtypeStruct((2 * MAX_BLOCKS, LANES), f32),
             jax.ShapeDtypeStruct((acq_loc, packed), f32),
         ),
         in_specs=[pl.BlockSpec(memory_space=pl.ANY)] * len(inputs),
-        out_specs=(vmem, vmem),
+        out_specs=(vmem,) * 3,
         scratch_shapes=[pltpu.VMEM(x.shape, x.dtype) for x in inputs]
         + [pltpu.SemaphoreType.DMA((4 + max(local // (LO * STEP), 1),))],
         compiler_params=pltpu.CompilerParams(vmem_limit_bytes=12 << 20),
@@ -284,9 +285,8 @@
     return jnp.transpose(jnp.broadcast_to(row, (LANES, LANES)))
 
 
-def filter_own_kernel(n_acq, band_ref, part_ref, out_ref, h_ref, down_ref):
-    acq_loc, lanes = part_ref.shape
-    packed = lanes - LANES
+def filter_own_kernel(n_acq, band_ref, part_ref, tags_ref, out_ref, h_ref, down_ref):
+    acq_loc, packed = part_ref.shape
     me = lax.axis_index("acq")
     band = band_ref[:, 0:acq_loc]
     for a in range(1, n_acq):
@@ -300,10 +300,10 @@
         inside = (source >= lower) & (source <= upper)
         unit = jnp.where(source == mine, 1.0, 0.0)
         h_ref[k * acq_loc : (k + 1) * acq_loc, :] = unit - jnp.where(inside, share, 0.0)
-    out_ref[:, 0:packed] = filter_dot(h_ref[0:acq_loc, :], part_ref[:, 0:packed])
-    out_ref[:, packed:] = part_ref[:, packed:]
+    out_ref[:, 0:packed] = filter_dot(h_ref[0:acq_loc, :], part_ref[...])
+    out_ref[:, packed:] = tags_ref[...]
     for b in range(packed // LANES):
-        pixel = part_ref[MAX_BLOCKS + b : MAX_BLOCKS + b + 1, packed:]
+        pixel = tags_ref[MAX_BLOCKS + b : MAX_BLOCKS + b + 1, :]
         row, col = split_pixel(pixel)
         for k, value in enumerate((row, *split_column(col))):
             down_ref[k, b * LANES : (b + 1) * LANES, :] = down_lanes(value)
@@ -313,7 +313,7 @@
     *parts, out_ref = refs
     acq_loc, lanes = begun_ref.shape
     packed = lanes - LANES
-    series = jnp.concatenate([part[:, 0:packed] for part in parts], 0)
+    series = jnp.concatenate([part[...] for part in parts], 0)
     out_ref[:, 0:packed] = begun_ref[:, 0:packed] + filter_dot(h_ref[acq_loc:, :], series)
     out_ref[:, packed:] = begun_ref[:, packed:]
 
@@ -576,8 +576,8 @@
     packed = (n_tile // 2 + 1) * LANES
     vmem = pl.BlockSpec(memory_space=pltpu.VMEM)
     f32 = jnp.float32
-    packet, own = gather_call(phases, coherence, pixel_index, send_list, counts)
-    parts = [xor_permute(packet, "acq", k) for k in range(1, n_acq)]
+    outgoing, tags, own = gather_call(phases, coherence, pixel_index, send_list, counts)
+    parts = [xor_permute(outgoing, "acq", k) for k in range(1, n_acq)]
     packet_shape = jax.ShapeDtypeStruct((acq_loc, packed + LANES), f32)
     begun, highpass, down = pl.pallas_call(
         functools.partial(filter_own_kernel, n_acq),
@@ -586,12 +586,12 @@
             jax.ShapeDtypeStruct((n_acq * acq_loc, acq_loc), f32),
             jax.ShapeDtypeStruct((3, packed, LANES), f32),
         ),
-        in_specs=[vmem] * 2,
+        in_specs=[vmem] * 3,
         out_specs=(vmem,) * 3,
         cost_estimate=pl.CostEstimate(flops=1 << 20, bytes_accessed=1 << 20, transcendentals=0),
         compiler_params=pltpu.CompilerParams(vmem_limit_bytes=4 << 20),
         name="filter_own_slots",
-    )(band_width.reshape(1, -1), packet)
+    )(band_width.reshape(1, -1), outgoing, tags)
     filtered = pl.pallas_call(
         filter_kernel,
         out_shape=packet_shape,
@@ -605,7 +605,8 @@
     sums = add_sources(n_tile, filtered[None], filtered, down, None, None)
     across, sums = lax.optimization_barrier((across, sums))
     held = jnp.stack([filtered, across])
-    arriving = [across[None]] + [xor_permute(held, "tile", k) for k in (2,3,1)]
+    order = sorted(range(1, half), key=lambda k: (k < half // 2, k))
+    arriving = [across[None]] + [xor_permute(held, "tile", k) for k in order]
     for sources in arriving[:-1]:
         sums = add_sources(n_tile, sources, filtered, down, sums, None)
     screen, residual = add_sources(n_tile, arriving[-1], filtered, down, sums, own)

time: 25.6 us -> 25.4 us (level)
  waiting for transfers between devices: 6.34 us -> 5.51 us
  local copies, waits for them, and re-layouts: 0.01 us -> 0.65 us
    ppermute x7, waiting for transfers between devices: 6.34 us -> 5.51 us  [xor_permute(): return lax.ppermute(x, axis, [(i, i ^ mask) for i in range(count)])]
    unnamed x2, local copies, waits for them, and re-layouts: 0.01 us -> 0.65 us
where the time goes in v7:
time: 25.4 us; the launch traced here: 25.2 us
  starting transfers between devices  9.34 us (37%)
  Pallas kernels  9.03 us (36%)
  waiting for transfers between devices  5.51 us (22%)
  between operations  0.69 us (3%)
  local copies, waits for them, and re-layouts  0.65 us (3%)
    ppermute x7, starting transfers between devices, xor_permute(): return lax.ppermute(x, axis, [(i, i ^ mask) for i in range(count)])  9.34 us
    pallas_call x5, Pallas kernels, add_sources(): pl.pallas_call(functools.partial(screen_kernel, n_tile, begins, ends), ou...  5.88 us
    ppermute x7, waiting for transfers between devices, xor_permute(): return lax.ppermute(x, axis, [(i, i ^ mask) for i in range(count)])  5.51 us
    pallas_call x1, Pallas kernels, gather_call(): pl.pallas_call(gather_kernel, out_shape=(jax.ShapeDtypeStruct((acq_loc, p...  2.37 us
    unnamed x2, local copies, waits for them, and re-layouts  0.65 us
    pallas_call x1, Pallas kernels, gathered_shards(): pl.pallas_call(functools.partial(filter_own_kernel, n_acq), out_shape=(pa...  0.55 us
  transfers between devices with their start and end apart: 7, of which 5 were waited for; matrix products, arithmetic and copies ran while one was open for 0% of the time, Pallas kernels for 18%

profile of v7, /device:TPU:0, one launch (start us, length us, event | category | flops | bytes accessed | tf_op | source)
XLA Modules:
  0.0 25.2 jit_solution(11361362331780355920)
XLA Ops:
  0.6 2.4 %gather_slots.1 = (f32[16,640]{1,0:T(8,128)S(1)}, f32[16,128]{1,0:T(8,128)S(1)}, f32[16,640]{1,0:T(8,128)S(1)}) custom-call(s32[1,8]{1,0:T(1,128)} %counts_hbm.1, s32[8,128]{1,0:T(8,128)} %list_hbm.1, f32[128,128]{1,0:T(8,128)} %bitcast.10, s32[128,128]{1,0:T(8,128)} %bitcast.11, f32[16,16384]{1,0:T(8,128)} %phases_hbm.1), custom_call_target="tpu_custom_call" | custom-call | tf_op jit(solution)/shard_map/gather_slots/pallas_call | solution.py:258
  3.0 2.4 %collective-permute-start.2 = (f32[16,640]{1,0:T(8,128)S(1)}, f32[16,640]{1,0:T(8,128)S(1)}, u32[]{:S(2)}, u32[]{:S(2)}) collective-permute-start(f32[16,640]{1,0:T(8,128)S(1)} %get-tuple-element.21.part_ref), channel_id=1, source_target_pairs={{0,3},{1,2},{2,1},{3,0},{4,7},{5,6},{6,5},{7,4},{8,11},{9,10},{10,... | collective-permute-start | bytes 122888 | tf_op jit(solution)/shard_map/ppermute | solution.py:569
  5.5 0.6 %collective-permute-start.1 = (f32[16,640]{1,0:T(8,128)S(1)}, f32[16,640]{1,0:T(8,128)S(1)}, u32[]{:S(2)}, u32[]{:S(2)}) collective-permute-start(f32[16,640]{1,0:T(8,128)S(1)} %get-tuple-element.21.part_ref), channel_id=1, source_target_pairs={{0,2},{1,3},{2,0},{3,1},{4,6},{5,7},{6,4},{7,5},{8,10},{9,11},{10,... | collective-permute-start | bytes 122888 | tf_op jit(solution)/shard_map/ppermute | solution.py:569
  6.1 0.0 collective-permute-start
  6.1 0.0 copy-start
  6.1 0.7 %copy-done = s32[64]{0:T(128)S(1)} copy-done((s32[64]{0:T(128)S(1)}, s32[64]{0:T(128)}, u32[]{:S(2)}) %copy-start) | copy-done | bytes 280
  6.8 0.6 %filter_own_slots.1 = (f32[16,768]{1,0:T(8,128)S(1)}, f32[64,16]{1,0:T(8,128)S(1)}, f32[3,640,128]{2,1,0:T(8,128)S(1)}) custom-call(s32[1,64]{1,0:T(1,128)S(1)} %bitcast.9, f32[16,640]{1,0:T(8,128)S(1)} %get-tuple-element.21.part_ref, f32[16,128]{1,0:T(8,128)S(1)} %get-tuple-element.22.tags_ref), custom_call_target="tpu_custom_call" | custom-call | flops 1048576 | bytes 1048576 | tf_op jit(solution)/shard_map/filter_own_slots/pallas_call | solution.py:582
  7.3 0.1 collective-permute-done.2.refs_2_
  7.4 2.2 %collective-permute-done.1.refs_1_ = f32[16,640]{1,0:T(8,128)S(1)} collective-permute-done((f32[16,640]{1,0:T(8,128)S(1)}, f32[16,640]{1,0:T(8,128)S(1)}, u32[]{:S(2)}, u32[]{:S(2)}) %collective-permute-start.1) | collective-permute-done | bytes 40992 | tf_op jit(solution)/shard_map/ppermute | solution.py:569
  9.6 0.0 collective-permute-done.refs_0_
  9.6 0.2 filter_slots.1.refs_1_
  9.8 2.7 %collective-permute-start.3 = (f32[16,768]{1,0:T(8,128)S(1)}, f32[16,768]{1,0:T(8,128)S(1)}, u32[]{:S(2)}, u32[]{:S(2)}) collective-permute-start(f32[16,768]{1,0:T(8,128)S(1)} %filter_slots.1.refs_1_), channel_id=1, source_target_pairs={{0,16},{4,20},{8,24},{12,28},{16,0},{20,4},{24,8},{28,12},{1,17},{... | collective-permute-start | bytes 147464 | tf_op jit(solution)/shard_map/ppermute | solution.py:569
  12.5 0.7 %add_sources.5 = (f32[136,1024]{1,0:T(8,128)S(1)}, f32[24,640]{1,0:T(8,128)S(1)}) custom-call(f32[1,16,768]{2,1,0:T(8,128)S(1)} %bitcast.5, f32[16,768]{1,0:T(8,128)S(1)} %filter_slots.1.refs_1_, f32[3,640,128]{2,1,0:T(8,128)S(1)} %get-tuple-element.25.refs_2_), custom_call_target="tpu_custom_call" | custom-call | flops 237502464 | bytes 1048576 | tf_op jit(solution)/shard_map/add_sources/pallas_call | solution.py:543
  13.2 2.1 %collective-permute-done.3 = f32[16,768]{1,0:T(8,128)S(1)} collective-permute-done((f32[16,768]{1,0:T(8,128)S(1)}, f32[16,768]{1,0:T(8,128)S(1)}, u32[]{:S(2)}, u32[]{:S(2)}) %collective-permute-start.3) | collective-permute-done | bytes 49184 | tf_op jit(solution)/shard_map/ppermute | solution.py:569
  15.3 1.3 %collective-permute-start.6 = (f32[2,16,768]{2,1,0:T(8,128)S(1)}, f32[2,16,768]{2,1,0:T(8,128)S(1)}, u32[]{:S(2)}, u32[]{:S(2)}) collective-permute-start(f32[2,16,768]{2,1,0:T(8,128)S(1)} %pad_maximum_fusion), channel_id=1, source_target_pairs={{0,8},{4,12},{8,0},{12,4},{16,24},{20,28},{24,16},{28,20},{1,9},{5... | collective-permute-start | bytes 294920 | tf_op jit(solution)/shard_map/ppermute | solution.py:569
  16.6 1.8 %collective-permute-start.5 = (f32[2,16,768]{2,1,0:T(8,128)S(1)}, f32[2,16,768]{2,1,0:T(8,128)S(1)}, u32[]{:S(2)}, u32[]{:S(2)}) collective-permute-start(f32[2,16,768]{2,1,0:T(8,128)S(1)} %pad_maximum_fusion), channel_id=1, source_target_pairs={{0,12},{4,8},{8,4},{12,0},{16,28},{20,24},{24,20},{28,16},{1,13},{... | collective-permute-start | bytes 294920 | tf_op jit(solution)/shard_map/ppermute | solution.py:569
  18.3 0.5 %collective-permute-start.4 = (f32[2,16,768]{2,1,0:T(8,128)S(1)}, f32[2,16,768]{2,1,0:T(8,128)S(1)}, u32[]{:S(2)}, u32[]{:S(2)}) collective-permute-start(f32[2,16,768]{2,1,0:T(8,128)S(1)} %pad_maximum_fusion), channel_id=1, source_target_pairs={{0,4},{4,0},{8,12},{12,8},{16,20},{20,16},{24,28},{28,24},{1,5},{5... | collective-permute-start | bytes 294920 | tf_op jit(solution)/shard_map/ppermute | solution.py:569
  18.9 0.8 %add_sources.6 = (f32[136,1024]{1,0:T(8,128)S(1)}, f32[24,640]{1,0:T(8,128)S(1)}) custom-call(f32[1,16,768]{2,1,0:T(8,128)S(1)} %bitcast.8, f32[16,768]{1,0:T(8,128)S(1)} %filter_slots.1.refs_1_, f32[3,640,128]{2,1,0:T(8,128)S(1)} %get-tuple-element.25.refs_2_, ...), custom_call_target="tpu_custom_call", output_to_operand_aliasing={{0}: (3, {}), {1}: (4, {})} | custom-call | flops 237502464 | bytes 1048576 | tf_op jit(solution)/shard_map/add_sources/pallas_call | solution.py:543
  19.7 0.9 %collective-permute-done.6.refs_0_ = f32[2,16,768]{2,1,0:T(8,128)S(1)} collective-permute-done((f32[2,16,768]{2,1,0:T(8,128)S(1)}, f32[2,16,768]{2,1,0:T(8,128)S(1)}, u32[]{:S(2)}, u32[]{:S(2)}) %collective-permute-start.6) | collective-permute-done | bytes 98336 | tf_op jit(solution)/shard_map/ppermute | solution.py:569
  20.6 1.2 %add_sources.7 = (f32[136,1024]{1,0:T(8,128)S(1)}, f32[24,640]{1,0:T(8,128)S(1)}) custom-call(f32[2,16,768]{2,1,0:T(8,128)S(1)} %collective-permute-done.6.refs_0_, f32[16,768]{1,0:T(8,128)S(1)} %filter_slots.1.refs_1_, f32[3,640,128]{2,1,0:T(8,128)S(1)} %get-tuple-element.25.refs_2_, ...), custom_call_target="tpu_custom_call", output_to_operand_aliasing={{0}: (3, {}), {1}: (4, {})} | custom-call | flops 475004928 | bytes 1048576 | tf_op jit(solution)/shard_map/add_sources/pallas_call | solution.py:543
  21.8 0.2 collective-permute-done.5.refs_0_
  22.1 1.2 %add_sources.8 = (f32[136,1024]{1,0:T(8,128)S(1)}, f32[24,640]{1,0:T(8,128)S(1)}) custom-call(f32[2,16,768]{2,1,0:T(8,128)S(1)} %collective-permute-done.5.refs_0_, f32[16,768]{1,0:T(8,128)S(1)} %filter_slots.1.refs_1_, f32[3,640,128]{2,1,0:T(8,128)S(1)} %get-tuple-element.25.refs_2_, ...), custom_call_target="tpu_custom_call", output_to_operand_aliasing={{0}: (3, {}), {1}: (4, {})} | custom-call | flops 475004928 | bytes 1048576 | tf_op jit(solution)/shard_map/add_sources/pallas_call | solution.py:543
  23.3 0.0 collective-permute-done.4.refs_0_
  23.3 1.9 %add_sources.9 = (f32[16,8,1024]{2,1,0:T(8,128)}, f32[16,1024]{1,0:T(8,128)}) custom-call(f32[2,16,768]{2,1,0:T(8,128)S(1)} %collective-permute-done.4.refs_0_, f32[16,768]{1,0:T(8,128)S(1)} %filter_slots.1.refs_1_, f32[3,640,128]{2,1,0:T(8,128)S(1)} %get-tuple-element.25.refs_2_, f32[136,1024]{1,0:T(8,128)S(1)} %get-tuple-element.35.refs_3_, ...), custom_call_target="tpu_custom_call" | custom-call | flops 475004928 | bytes 1048576 | tf_op jit(solution)/shard_map/add_sources/pallas_call | solution.py:543
  (1 shorter events, 0.0 us)
Async XLA Ops:
  3.0 4.4 %collective-permute-start.2 = (f32[16,640]{1,0:T(8,128)S(1)}, f32[16,640]{1,0:T(8,128)S(1)}, u32[]{:S(2)}, u32[]{:S(2)}) collective-permute-start(f32[16,640]{1,0:T(8,128)S(1)} %get-tuple-element.21.part_ref), channel_id=1, source_target_pairs={{0,3},{1,2},{2,1},{3,0},{4,7},{5,6},{6,5},{7,4},{8,11},{9,10},{10,... | collective-permute-start | bytes 122888 | tf_op jit(solution)/shard_map/ppermute | solution.py:569
  5.5 4.1 %collective-permute-start.1 = (f32[16,640]{1,0:T(8,128)S(1)}, f32[16,640]{1,0:T(8,128)S(1)}, u32[]{:S(2)}, u32[]{:S(2)}) collective-permute-start(f32[16,640]{1,0:T(8,128)S(1)} %get-tuple-element.21.part_ref), channel_id=1, source_target_pairs={{0,2},{1,3},{2,0},{3,1},{4,6},{5,7},{6,4},{7,5},{8,10},{9,11},{10,... | collective-permute-start | bytes 122888 | tf_op jit(solution)/shard_map/ppermute | solution.py:569
  6.1 3.5 %collective-permute-start = (f32[16,640]{1,0:T(8,128)S(1)}, f32[16,640]{1,0:T(8,128)S(1)}, u32[]{:S(2)}, u32[]{:S(2)}) collective-permute-start(f32[16,640]{1,0:T(8,128)S(1)} %get-tuple-element.21.part_ref), channel_id=1, source_target_pairs={{0,1},{1,0},{2,3},{3,2},{4,5},{5,4},{6,7},{7,6},{8,9},{9,8},{10,11... | collective-permute-start | bytes 122888 | tf_op jit(solution)/shard_map/ppermute | solution.py:569
  6.1 0.7 %copy-start = (s32[64]{0:T(128)S(1)}, s32[64]{0:T(128)}, u32[]{:S(2)}) copy-start(s32[64]{0:T(128)} %param.11) | copy-start | bytes 772
  9.8 5.4 %collective-permute-start.3 = (f32[16,768]{1,0:T(8,128)S(1)}, f32[16,768]{1,0:T(8,128)S(1)}, u32[]{:S(2)}, u32[]{:S(2)}) collective-permute-start(f32[16,768]{1,0:T(8,128)S(1)} %filter_slots.1.refs_1_), channel_id=1, source_target_pairs={{0,16},{4,20},{8,24},{12,28},{16,0},{20,4},{24,8},{28,12},{1,17},{... | collective-permute-start | bytes 147464 | tf_op jit(solution)/shard_map/ppermute | solution.py:569
  15.3 5.3 %collective-permute-start.6 = (f32[2,16,768]{2,1,0:T(8,128)S(1)}, f32[2,16,768]{2,1,0:T(8,128)S(1)}, u32[]{:S(2)}, u32[]{:S(2)}) collective-permute-start(f32[2,16,768]{2,1,0:T(8,128)S(1)} %pad_maximum_fusion), channel_id=1, source_target_pairs={{0,8},{4,12},{8,0},{12,4},{16,24},{20,28},{24,16},{28,20},{1,9},{5... | collective-permute-start | bytes 294920 | tf_op jit(solution)/shard_map/ppermute | solution.py:569
  16.6 5.5 %collective-permute-start.5 = (f32[2,16,768]{2,1,0:T(8,128)S(1)}, f32[2,16,768]{2,1,0:T(8,128)S(1)}, u32[]{:S(2)}, u32[]{:S(2)}) collective-permute-start(f32[2,16,768]{2,1,0:T(8,128)S(1)} %pad_maximum_fusion), channel_id=1, source_target_pairs={{0,12},{4,8},{8,4},{12,0},{16,28},{20,24},{24,20},{28,16},{1,13},{... | collective-permute-start | bytes 294920 | tf_op jit(solution)/shard_map/ppermute | solution.py:569
  18.3 5.0 %collective-permute-start.4 = (f32[2,16,768]{2,1,0:T(8,128)S(1)}, f32[2,16,768]{2,1,0:T(8,128)S(1)}, u32[]{:S(2)}, u32[]{:S(2)}) collective-permute-start(f32[2,16,768]{2,1,0:T(8,128)S(1)} %pad_maximum_fusion), channel_id=1, source_target_pairs={{0,4},{4,0},{8,12},{12,8},{16,20},{20,16},{24,28},{28,24},{1,5},{5... | collective-permute-start | bytes 294920 | tf_op jit(solution)/shard_map/ppermute | solution.py:569

commit v8 on v7

--- a/solution.py
+++ b/solution.py
@@ -295,8 +295,8 @@
     lower = jnp.maximum(mine - band, 0)
     upper = jnp.minimum(mine + band, ACQ - 1)
     share = 1.0 / (upper - lower + 1).astype(jnp.float32)
-    for k in range(n_acq):
-        source = (me ^ k) * acq_loc + lax.broadcasted_iota(jnp.int32, (acq_loc, acq_loc), 0)
+    for k, part in enumerate((0, 1, 3, 2)):
+        source = (me ^ part) * acq_loc + lax.broadcasted_iota(jnp.int32, (acq_loc, acq_loc), 0)
         inside = (source >= lower) & (source <= upper)
         unit = jnp.where(source == mine, 1.0, 0.0)
         h_ref[k * acq_loc : (k + 1) * acq_loc, :] = unit - jnp.where(inside, share, 0.0)
@@ -577,7 +577,7 @@
     vmem = pl.BlockSpec(memory_space=pltpu.VMEM)
     f32 = jnp.float32
     outgoing, tags, own = gather_call(phases, coherence, pixel_index, send_list, counts)
-    parts = [xor_permute(outgoing, "acq", k) for k in range(1, n_acq)]
+    parts = [xor_permute(outgoing, "acq", k) for k in (1, 3, 2)]
     packet_shape = jax.ShapeDtypeStruct((acq_loc, packed + LANES), f32)
     begun, highpass, down = pl.pallas_call(
         functools.partial(filter_own_kernel, n_acq),

time: 25.4 us -> 25.4 us (level)
  no operation moved by 1% of the time
where the time goes in v8:
time: 25.4 us; the launch traced here: 25.2 us
  starting transfers between devices  9.41 us (37%)
  Pallas kernels  9.03 us (36%)
  waiting for transfers between devices  5.44 us (21%)
  between operations  0.69 us (3%)
  local copies, waits for them, and re-layouts  0.65 us (3%)
    ppermute x7, starting transfers between devices, xor_permute(): return lax.ppermute(x, axis, [(i, i ^ mask) for i in range(count)])  9.41 us
    pallas_call x5, Pallas kernels, add_sources(): pl.pallas_call(functools.partial(screen_kernel, n_tile, begins, ends), ou...  5.87 us
    ppermute x7, waiting for transfers between devices, xor_permute(): return lax.ppermute(x, axis, [(i, i ^ mask) for i in range(count)])  5.44 us
    pallas_call x1, Pallas kernels, gather_call(): pl.pallas_call(gather_kernel, out_shape=(jax.ShapeDtypeStruct((acq_loc, p...  2.37 us
    unnamed x2, local copies, waits for them, and re-layouts  0.65 us
    pallas_call x1, Pallas kernels, gathered_shards(): pl.pallas_call(functools.partial(filter_own_kernel, n_acq), out_shape=(pa...  0.55 us
  transfers between devices with their start and end apart: 7, of which 5 were waited for; matrix products, arithmetic and copies ran while one was open for 0% of the time, Pallas kernels for 18%

profile of v8, /device:TPU:0, one launch (start us, length us, event | category | flops | bytes accessed | tf_op | source)
XLA Modules:
  0.0 25.2 jit_solution(2739250492081412296)
XLA Ops:
  0.6 2.4 %gather_slots.1 = (f32[16,640]{1,0:T(8,128)S(1)}, f32[16,128]{1,0:T(8,128)S(1)}, f32[16,640]{1,0:T(8,128)S(1)}) custom-call(s32[1,8]{1,0:T(1,128)} %counts_hbm.1, s32[8,128]{1,0:T(8,128)} %list_hbm.1, f32[128,128]{1,0:T(8,128)} %bitcast.10, s32[128,128]{1,0:T(8,128)} %bitcast.11, f32[16,16384]{1,0:T(8,128)} %phases_hbm.1), custom_call_target="tpu_custom_call" | custom-call | tf_op jit(solution)/shard_map/gather_slots/pallas_call | solution.py:258
  3.0 3.0 %collective-permute-start.2 = (f32[16,640]{1,0:T(8,128)S(1)}, f32[16,640]{1,0:T(8,128)S(1)}, u32[]{:S(2)}, u32[]{:S(2)}) collective-permute-start(f32[16,640]{1,0:T(8,128)S(1)} %get-tuple-element.21.part_ref), channel_id=1, source_target_pairs={{0,2},{1,3},{2,0},{3,1},{4,6},{5,7},{6,4},{7,5},{8,10},{9,11},{10,... | collective-permute-start | bytes 122888 | tf_op jit(solution)/shard_map/ppermute | solution.py:569
  6.0 0.0 collective-permute-start.1
  6.0 0.2 collective-permute-start
  6.2 0.0 copy-start
  6.2 0.7 %copy-done = s32[64]{0:T(128)S(1)} copy-done((s32[64]{0:T(128)S(1)}, s32[64]{0:T(128)}, u32[]{:S(2)}) %copy-start) | copy-done | bytes 280
  6.9 0.6 %filter_own_slots.1 = (f32[16,768]{1,0:T(8,128)S(1)}, f32[64,16]{1,0:T(8,128)S(1)}, f32[3,640,128]{2,1,0:T(8,128)S(1)}) custom-call(s32[1,64]{1,0:T(1,128)S(1)} %bitcast.9, f32[16,640]{1,0:T(8,128)S(1)} %get-tuple-element.21.part_ref, f32[16,128]{1,0:T(8,128)S(1)} %get-tuple-element.22.tags_ref), custom_call_target="tpu_custom_call" | custom-call | flops 1048576 | bytes 1048576 | tf_op jit(solution)/shard_map/filter_own_slots/pallas_call | solution.py:582
  7.4 0.6 %collective-permute-done.2.refs_2_ = f32[16,640]{1,0:T(8,128)S(1)} collective-permute-done((f32[16,640]{1,0:T(8,128)S(1)}, f32[16,640]{1,0:T(8,128)S(1)}, u32[]{:S(2)}, u32[]{:S(2)}) %collective-permute-start.2) | collective-permute-done | bytes 40992 | tf_op jit(solution)/shard_map/ppermute | solution.py:569
  8.0 1.6 %collective-permute-done.1.refs_1_ = f32[16,640]{1,0:T(8,128)S(1)} collective-permute-done((f32[16,640]{1,0:T(8,128)S(1)}, f32[16,640]{1,0:T(8,128)S(1)}, u32[]{:S(2)}, u32[]{:S(2)}) %collective-permute-start.1) | collective-permute-done | bytes 40992 | tf_op jit(solution)/shard_map/ppermute | solution.py:569
  9.6 0.0 collective-permute-done.refs_0_
  9.6 0.2 filter_slots.1.refs_1_
  9.9 2.7 %collective-permute-start.3 = (f32[16,768]{1,0:T(8,128)S(1)}, f32[16,768]{1,0:T(8,128)S(1)}, u32[]{:S(2)}, u32[]{:S(2)}) collective-permute-start(f32[16,768]{1,0:T(8,128)S(1)} %filter_slots.1.refs_1_), channel_id=1, source_target_pairs={{0,16},{4,20},{8,24},{12,28},{16,0},{20,4},{24,8},{28,12},{1,17},{... | collective-permute-start | bytes 147464 | tf_op jit(solution)/shard_map/ppermute | solution.py:569
  12.5 0.7 %add_sources.5 = (f32[136,1024]{1,0:T(8,128)S(1)}, f32[24,640]{1,0:T(8,128)S(1)}) custom-call(f32[1,16,768]{2,1,0:T(8,128)S(1)} %bitcast.5, f32[16,768]{1,0:T(8,128)S(1)} %filter_slots.1.refs_1_, f32[3,640,128]{2,1,0:T(8,128)S(1)} %get-tuple-element.25.refs_2_), custom_call_target="tpu_custom_call" | custom-call | flops 237502464 | bytes 1048576 | tf_op jit(solution)/shard_map/add_sources/pallas_call | solution.py:543
  13.2 2.1 %collective-permute-done.3 = f32[16,768]{1,0:T(8,128)S(1)} collective-permute-done((f32[16,768]{1,0:T(8,128)S(1)}, f32[16,768]{1,0:T(8,128)S(1)}, u32[]{:S(2)}, u32[]{:S(2)}) %collective-permute-start.3) | collective-permute-done | bytes 49184 | tf_op jit(solution)/shard_map/ppermute | solution.py:569
  15.3 1.2 %collective-permute-start.6 = (f32[2,16,768]{2,1,0:T(8,128)S(1)}, f32[2,16,768]{2,1,0:T(8,128)S(1)}, u32[]{:S(2)}, u32[]{:S(2)}) collective-permute-start(f32[2,16,768]{2,1,0:T(8,128)S(1)} %pad_maximum_fusion), channel_id=1, source_target_pairs={{0,8},{4,12},{8,0},{12,4},{16,24},{20,28},{24,16},{28,20},{1,9},{5... | collective-permute-start | bytes 294920 | tf_op jit(solution)/shard_map/ppermute | solution.py:569
  16.6 1.8 %collective-permute-start.5 = (f32[2,16,768]{2,1,0:T(8,128)S(1)}, f32[2,16,768]{2,1,0:T(8,128)S(1)}, u32[]{:S(2)}, u32[]{:S(2)}) collective-permute-start(f32[2,16,768]{2,1,0:T(8,128)S(1)} %pad_maximum_fusion), channel_id=1, source_target_pairs={{0,12},{4,8},{8,4},{12,0},{16,28},{20,24},{24,20},{28,16},{1,13},{... | collective-permute-start | bytes 294920 | tf_op jit(solution)/shard_map/ppermute | solution.py:569
  18.4 0.5 %collective-permute-start.4 = (f32[2,16,768]{2,1,0:T(8,128)S(1)}, f32[2,16,768]{2,1,0:T(8,128)S(1)}, u32[]{:S(2)}, u32[]{:S(2)}) collective-permute-start(f32[2,16,768]{2,1,0:T(8,128)S(1)} %pad_maximum_fusion), channel_id=1, source_target_pairs={{0,4},{4,0},{8,12},{12,8},{16,20},{20,16},{24,28},{28,24},{1,5},{5... | collective-permute-start | bytes 294920 | tf_op jit(solution)/shard_map/ppermute | solution.py:569
  18.9 0.8 %add_sources.6 = (f32[136,1024]{1,0:T(8,128)S(1)}, f32[24,640]{1,0:T(8,128)S(1)}) custom-call(f32[1,16,768]{2,1,0:T(8,128)S(1)} %bitcast.8, f32[16,768]{1,0:T(8,128)S(1)} %filter_slots.1.refs_1_, f32[3,640,128]{2,1,0:T(8,128)S(1)} %get-tuple-element.25.refs_2_, ...), custom_call_target="tpu_custom_call", output_to_operand_aliasing={{0}: (3, {}), {1}: (4, {})} | custom-call | flops 237502464 | bytes 1048576 | tf_op jit(solution)/shard_map/add_sources/pallas_call | solution.py:543
  19.8 0.9 %collective-permute-done.6.refs_0_ = f32[2,16,768]{2,1,0:T(8,128)S(1)} collective-permute-done((f32[2,16,768]{2,1,0:T(8,128)S(1)}, f32[2,16,768]{2,1,0:T(8,128)S(1)}, u32[]{:S(2)}, u32[]{:S(2)}) %collective-permute-start.6) | collective-permute-done | bytes 98336 | tf_op jit(solution)/shard_map/ppermute | solution.py:569
  20.7 1.2 %add_sources.7 = (f32[136,1024]{1,0:T(8,128)S(1)}, f32[24,640]{1,0:T(8,128)S(1)}) custom-call(f32[2,16,768]{2,1,0:T(8,128)S(1)} %collective-permute-done.6.refs_0_, f32[16,768]{1,0:T(8,128)S(1)} %filter_slots.1.refs_1_, f32[3,640,128]{2,1,0:T(8,128)S(1)} %get-tuple-element.25.refs_2_, ...), custom_call_target="tpu_custom_call", output_to_operand_aliasing={{0}: (3, {}), {1}: (4, {})} | custom-call | flops 475004928 | bytes 1048576 | tf_op jit(solution)/shard_map/add_sources/pallas_call | solution.py:543
  21.9 0.2 collective-permute-done.5.refs_0_
  22.1 1.2 %add_sources.8 = (f32[136,1024]{1,0:T(8,128)S(1)}, f32[24,640]{1,0:T(8,128)S(1)}) custom-call(f32[2,16,768]{2,1,0:T(8,128)S(1)} %collective-permute-done.5.refs_0_, f32[16,768]{1,0:T(8,128)S(1)} %filter_slots.1.refs_1_, f32[3,640,128]{2,1,0:T(8,128)S(1)} %get-tuple-element.25.refs_2_, ...), custom_call_target="tpu_custom_call", output_to_operand_aliasing={{0}: (3, {}), {1}: (4, {})} | custom-call | flops 475004928 | bytes 1048576 | tf_op jit(solution)/shard_map/add_sources/pallas_call | solution.py:543
  23.3 0.0 collective-permute-done.4.refs_0_
  23.3 1.9 %add_sources.9 = (f32[16,8,1024]{2,1,0:T(8,128)}, f32[16,1024]{1,0:T(8,128)}) custom-call(f32[2,16,768]{2,1,0:T(8,128)S(1)} %collective-permute-done.4.refs_0_, f32[16,768]{1,0:T(8,128)S(1)} %filter_slots.1.refs_1_, f32[3,640,128]{2,1,0:T(8,128)S(1)} %get-tuple-element.25.refs_2_, f32[136,1024]{1,0:T(8,128)S(1)} %get-tuple-element.35.refs_3_, ...), custom_call_target="tpu_custom_call" | custom-call | flops 475004928 | bytes 1048576 | tf_op jit(solution)/shard_map/add_sources/pallas_call | solution.py:543
  (1 shorter events, 0.0 us)
Async XLA Ops:
  3.0 5.0 %collective-permute-start.2 = (f32[16,640]{1,0:T(8,128)S(1)}, f32[16,640]{1,0:T(8,128)S(1)}, u32[]{:S(2)}, u32[]{:S(2)}) collective-permute-start(f32[16,640]{1,0:T(8,128)S(1)} %get-tuple-element.21.part_ref), channel_id=1, source_target_pairs={{0,2},{1,3},{2,0},{3,1},{4,6},{5,7},{6,4},{7,5},{8,10},{9,11},{10,... | collective-permute-start | bytes 122888 | tf_op jit(solution)/shard_map/ppermute | solution.py:569
  6.0 3.6 %collective-permute-start.1 = (f32[16,640]{1,0:T(8,128)S(1)}, f32[16,640]{1,0:T(8,128)S(1)}, u32[]{:S(2)}, u32[]{:S(2)}) collective-permute-start(f32[16,640]{1,0:T(8,128)S(1)} %get-tuple-element.21.part_ref), channel_id=1, source_target_pairs={{0,3},{1,2},{2,1},{3,0},{4,7},{5,6},{6,5},{7,4},{8,11},{9,10},{10,... | collective-permute-start | bytes 122888 | tf_op jit(solution)/shard_map/ppermute | solution.py:569
  6.0 3.6 %collective-permute-start = (f32[16,640]{1,0:T(8,128)S(1)}, f32[16,640]{1,0:T(8,128)S(1)}, u32[]{:S(2)}, u32[]{:S(2)}) collective-permute-start(f32[16,640]{1,0:T(8,128)S(1)} %get-tuple-element.21.part_ref), channel_id=1, source_target_pairs={{0,1},{1,0},{2,3},{3,2},{4,5},{5,4},{6,7},{7,6},{8,9},{9,8},{10,11... | collective-permute-start | bytes 122888 | tf_op jit(solution)/shard_map/ppermute | solution.py:569
  6.2 0.7 %copy-start = (s32[64]{0:T(128)S(1)}, s32[64]{0:T(128)}, u32[]{:S(2)}) copy-start(s32[64]{0:T(128)} %param.11) | copy-start | bytes 772
  9.9 5.5 %collective-permute-start.3 = (f32[16,768]{1,0:T(8,128)S(1)}, f32[16,768]{1,0:T(8,128)S(1)}, u32[]{:S(2)}, u32[]{:S(2)}) collective-permute-start(f32[16,768]{1,0:T(8,128)S(1)} %filter_slots.1.refs_1_), channel_id=1, source_target_pairs={{0,16},{4,20},{8,24},{12,28},{16,0},{20,4},{24,8},{28,12},{1,17},{... | collective-permute-start | bytes 147464 | tf_op jit(solution)/shard_map/ppermute | solution.py:569
  15.3 5.3 %collective-permute-start.6 = (f32[2,16,768]{2,1,0:T(8,128)S(1)}, f32[2,16,768]{2,1,0:T(8,128)S(1)}, u32[]{:S(2)}, u32[]{:S(2)}) collective-permute-start(f32[2,16,768]{2,1,0:T(8,128)S(1)} %pad_maximum_fusion), channel_id=1, source_target_pairs={{0,8},{4,12},{8,0},{12,4},{16,24},{20,28},{24,16},{28,20},{1,9},{5... | collective-permute-start | bytes 294920 | tf_op jit(solution)/shard_map/ppermute | solution.py:569
  16.6 5.5 %collective-permute-start.5 = (f32[2,16,768]{2,1,0:T(8,128)S(1)}, f32[2,16,768]{2,1,0:T(8,128)S(1)}, u32[]{:S(2)}, u32[]{:S(2)}) collective-permute-start(f32[2,16,768]{2,1,0:T(8,128)S(1)} %pad_maximum_fusion), channel_id=1, source_target_pairs={{0,12},{4,8},{8,4},{12,0},{16,28},{20,24},{24,20},{28,16},{1,13},{... | collective-permute-start | bytes 294920 | tf_op jit(solution)/shard_map/ppermute | solution.py:569
  18.4 4.9 %collective-permute-start.4 = (f32[2,16,768]{2,1,0:T(8,128)S(1)}, f32[2,16,768]{2,1,0:T(8,128)S(1)}, u32[]{:S(2)}, u32[]{:S(2)}) collective-permute-start(f32[2,16,768]{2,1,0:T(8,128)S(1)} %pad_maximum_fusion), channel_id=1, source_target_pairs={{0,4},{4,0},{8,12},{12,8},{16,20},{20,16},{24,28},{28,24},{1,5},{5... | collective-permute-start | bytes 294920 | tf_op jit(solution)/shard_map/ppermute | solution.py:569
